TPU v7x, 256 devices: a whole 4x4x8 slice. The times are simulated.
256 devices in a mesh: gx: 4 (over y), gy: 8 (over x, core), gz: 8 (over z).
Axes of the slice: x: 4, y: 4, z: 8, core: 2. Of those that a mesh axis runs over, the one named last changes fastest.
Arguments:
- data: float32 [128, 256, 1024], P('gx', 'gy', 'gz'), may hold values from -120 to 120
- weights: float32 [8, 1024], P(None, 'gz'), may hold values from -3 to 3
Outputs:
- solution: float32 [128, 256, 1024], P('gx', 'gy', 'gz')
- residual: float32 [128, 256, 1024], P('gx', 'gy', 'gz')
- norms: float32 [4], replicated
All inputs are finite; a program needn't handle non-finite values.
Results may differ from a plain program's by a relative error of at most 0.0001.
Values sent between devices are 32-bit elements; how exact they have to be, the bound alone decides.
No kernel may reach another device: no remote copies, remote signals or barrier semaphores. Data moves between devices by JAX's collectives and lax.ppermute only.
A program may use at most 128 MiB of HBM per device.

v0:
```python
import jax
import jax.numpy as jnp
from jax import lax
from jax.sharding import Mesh
from jax.sharding import PartitionSpec as P

HALF = 4
GY = ("gy_0", "gy_1")
GX_GY_GZ = ("gx", "gy_0", "gy_1", "gz")


relaxation = 0.45


def padded_2(block, sides, width):
    for axis, dim in sides:
        count = lax.axis_size(axis)
        forward = [(i, i + 1) for i in range(count - 1)]
        backward = [(target, source) for source, target in forward]
        low = lax.ppermute(
            lax.slice_in_dim(block, block.shape[dim] - width, None, axis=dim), axis, forward
        )
        high = lax.ppermute(lax.slice_in_dim(block, 0, width, axis=dim), axis, backward)
        block = jnp.concatenate([low, block, high], axis=dim)
    return block


def padded_3(array, sides, width):
    edges = {}
    for axis, dim in sides:
        size, length = (lax.axis_size(axis), array.shape[dim])
        up = [(i, (i + 1) % size) for i in range(size - 1)]
        last = lax.slice_in_dim(array, length - width, length, axis=dim)
        first = lax.slice_in_dim(array, 0, width, axis=dim)
        edges[dim] = (
            lax.ppermute(last, axis, up),
            lax.ppermute(first, axis, [(b, a) for a, b in up]),
        )
    done = []
    for _, dim in sides:
        low, high = edges[dim]
        around = [(width, width) if d in done else (0, 0) for d in range(array.ndim)]
        array = jnp.concatenate([jnp.pad(low, around), array, jnp.pad(high, around)], axis=dim)
        done.append(dim)
    return array


def by_axis(array, axes):
    for axis in axes:
        array = lax.psum(array, axis)
    return array


def band_offsets():
    return [j - HALF for j in range(HALF)] + [j - HALF + 1 for j in range(HALF, 2 * HALF)]


def forward_band(padded, weights):
    count = weights.shape[1]
    result = padded[:, :, HALF : HALF + count]
    for j, offset in enumerate(band_offsets()):
        result = (
            result + weights[j][None, None, :] * padded[:, :, HALF + offset : HALF + offset + count]
        )
    return result


def backward_band(padded, transposed):
    count = transposed.shape[1]
    result = padded[:, :, HALF : HALF + count]
    for j, offset in enumerate(band_offsets()):
        result = (
            result
            + transposed[j][None, None, :] * padded[:, :, HALF - offset : HALF - offset + count]
        )
    return result


def transposed_weights(padded, count):
    return jnp.stack(
        [
            padded[j, HALF - offset : HALF - offset + count]
            for j, offset in enumerate(band_offsets())
        ]
    )


def combine(field, back, near, stiffness):
    return back + stiffness * (6.0 * field - near)


def diagonal_of(transposed, stiffness):
    return 1.0 + jnp.sum(transposed * transposed, axis=0) + 6.0 * stiffness


def coarsen(weights):
    return 0.5 * (weights[:, 0::2] + weights[:, 1::2])


def restrict_dim(padded, dim):
    half_count = (padded.shape[dim] - 2) // 2
    s0 = lax.slice_in_dim(padded, 0, 2 * half_count - 1, 2, dim)
    s1 = lax.slice_in_dim(padded, 1, 2 * half_count, 2, dim)
    s2 = lax.slice_in_dim(padded, 2, 2 * half_count + 1, 2, dim)
    s3 = lax.slice_in_dim(padded, 3, 2 * half_count + 2, 2, dim)
    return (s0 + 3.0 * s1 + 3.0 * s2 + s3) * 0.125


def prolong_dim(padded, dim):
    count = padded.shape[dim] - 2
    below = lax.slice_in_dim(padded, 0, count, 1, dim)
    centre = lax.slice_in_dim(padded, 1, count + 1, 1, dim)
    above = lax.slice_in_dim(padded, 2, count + 2, 1, dim)
    even = 0.75 * centre + 0.25 * below
    odd = 0.75 * centre + 0.25 * above
    joined = jnp.stack([even, odd], dim + 1)
    shape = list(centre.shape)
    shape[dim] = 2 * count
    return joined.reshape(shape)


def restrict_all(padded):
    for dim in range(3):
        padded = restrict_dim(padded, dim)
    return padded


def prolong_all(padded):
    for dim in range(3):
        padded = prolong_dim(padded, dim)
    return padded


def prepare(weights):
    padded = padded_2(weights, (("gz", 1),), HALF)
    return (transposed_weights(padded, weights.shape[1]), padded)


def transpose_apply(values, transposed):
    padded = padded_2(values, (("gz", 2),), HALF)
    return backward_band(padded, transposed)


def operate(field, wide_weights, transposed, stiffness):
    shape = field.shape
    column = padded_2(field, (("gz", 2),), 2 * HALF)
    side = padded_3(field, (("gx", 0), (GY, 1)), 1)
    near = side[2:, 1:-1, :] + side[:-2, 1:-1, :] + side[1:-1, 2:, :] + side[1:-1, :-2, :]
    near = (
        near
        + column[:, :, 2 * HALF + 1 : 2 * HALF + 1 + shape[2]]
        + column[:, :, 2 * HALF - 1 : 2 * HALF - 1 + shape[2]]
    )
    back = backward_band(forward_band(column, wide_weights), transposed)
    return combine(field, back, near, stiffness)


def narrow(defect):
    return restrict_all(padded_2(defect, (("gx", 0), (GY, 1), ("gz", 2)), 1))


def spread(coarse):
    return prolong_all(padded_2(coarse, (("gx", 0), (GY, 1), ("gz", 2)), 1))


def sweep(error, right, apply_fn, diag):
    return error + relaxation * (right - apply_fn(error)) / diag


def local_apply(wide_weights, transposed, stiffness):

    def apply_fn(field):
        return operate(field, wide_weights, transposed, stiffness)

    return apply_fn


def square_total(defect):
    partial_total = jnp.sum(defect * defect)
    return partial_total


def body(data, weights):
    devices = lax.axis_size("gx") * lax.axis_size(GY) * lax.axis_size("gz")
    level_weights = [weights]
    for level in range(3):
        level_weights.append(coarsen(level_weights[-1]))
    level_trans = []
    level_wide = []
    for level in range(3):
        transposed, wide = prepare(level_weights[level])
        level_trans.append(transposed)
        level_wide.append(wide)
    rhs = transpose_apply(data, level_trans[0])
    right = rhs
    rights, errors, diags, totals, counts = ([], [], [], [], [])
    for level in range(3):
        stiffness = 0.25**level
        diag = diagonal_of(level_trans[level], stiffness)
        apply_fn = local_apply(level_wide[level], level_trans[level], stiffness)
        error = relaxation * right / diag
        error = sweep(error, right, apply_fn, diag)
        defect = right - apply_fn(error)
        totals.append(square_total(defect))
        counts.append(defect.size * devices)
        rights.append(right)
        errors.append(error)
        diags.append(diag)
        right = narrow(defect)
    stiffness = 0.25**3
    coarse_trans, coarse_wide = prepare(level_weights[3])
    diag = diagonal_of(coarse_trans, stiffness)
    apply_fn = local_apply(coarse_wide, coarse_trans, stiffness)
    coarse = relaxation * right / diag
    coarse = sweep(coarse, right, apply_fn, diag)
    correction = spread(coarse)
    for level in (2, 1, 0):
        apply_fn = local_apply(level_wide[level], level_trans[level], 0.25**level)
        update = errors[level] + correction
        update = sweep(update, rights[level], apply_fn, diags[level])
        update = sweep(update, rights[level], apply_fn, diags[level])
        if level > 0:
            correction = spread(update)
        coarse = update
    residual = rhs - operate(coarse, level_wide[0], level_trans[0], 1.0)
    totals.append(square_total(residual))
    counts.append(residual.size * devices)
    totals = list(jax.tree.map(lambda part: by_axis(part, GX_GY_GZ), tuple(totals)))
    norms = jnp.sqrt(jnp.stack([totals[k] / counts[k] for k in range(4)]))
    return (coarse, residual, norms)


def solution(mesh):
    split = Mesh(
        mesh.devices.reshape(mesh.shape["gx"], 4, 2, mesh.shape["gz"]), ("gx", "gy_0", "gy_1", "gz")
    )
    placed = (P("gx", GY, "gz"), P(None, "gz"))
    return jax.shard_map(
        body,
        mesh=split,
        in_specs=placed,
        out_specs=(P("gx", GY, "gz"), P("gx", GY, "gz"), P()),
        check_vma=False,
    )
```

profile of v0, /device:TPU:32, one launch (start us, length us, event | category | flops | bytes accessed | tf_op | source)
XLA Modules:
  0.0 798.6 jit_solution(13713375748327662424)
XLA Ops:
  21.1 4.9 collective-permute-start.23
  37.0 5.1 collective-permute-start.63
  72.2 8.7 %multiply_divide_fusion = (f32[32,32,128]{1,0,2:T(8,128)S(1)}, f32[32,32,128]{1,0,2:T(8,128)}) fusion(f32[128]{0:T(128)S(1)} %broadcast_add_fusion.3, f32[32,32,128]{1,0,2:T(8,128)} %copy.613, f32[128]{0:T(128)S(1)} %bitcast.214, f32[32,32,128]{1,0,2:T(8,128)} %copy.612, f32[128]{0:T(128)S(1)} %bitcast.220, f32[32,32,128]{1,0,2:T(8,128)} %copy.611, ...), kind=kLoop, calls=%fused_computation.310 | loop fusion | flops 2359296 | bytes 5771776 | tf_op jit(solution)/shard_map/div | solution.py:201
  114.3 12.2 %fusion.92 = f32[32,32,128]{1,0,2:T(8,128)S(1)} fusion(f32[32,32,128]{1,0,2:T(8,128)} %copy-done.4, f32[32,32,128]{1,0,2:T(8,128)S(1)} %copy-done.5, f32[32,32,8]{1,0,2:T(8,128)S(1)} %collective-permute-done.5, f32[32,32,8]{1,0,2:T(8,128)S(1)} %collective-permute-done.4, f32[32,1,128]{1,0,2:T(8,128)S(1)} %copy-done.17, ...), kind=kLoop, calls=%fused_computation.158 | loop fusion | flops 5767168 | bytes 6427136 | tf_op jit(solution)/shard_map/add | solution.py:167
  129.3 4.9 collective-permute-start.10
  161.0 5.9 multiply_reduce_fusion.1
  188.2 5.3 collective-permute-start.20
  195.5 4.9 collective-permute-done.21
  203.8 6.3 slice.2087
  210.1 6.3 slice.2088
  216.4 6.4 slice.2089
  222.8 6.4 slice.2090
  231.7 6.4 slice.2091
  238.1 6.6 slice.2092
  244.7 6.6 slice.2093
  251.2 6.6 slice.2094
  260.7 4.9 collective-permute-start.24
  282.0 4.9 collective-permute-start.30
  294.9 4.9 collective-permute-start.33
  368.6 5.1 collective-permute-start.50
  390.5 4.8 collective-permute-start.56
  453.8 4.7 collective-permute-done.73
  458.6 5.3 collective-permute-start.74
  560.7 4.9 collective-permute-start.100
  654.3 5.4 fusion.75
  662.5 5.1 collective-permute-start.118
  682.1 5.0 collective-permute-start.121
  696.0 12.2 %fusion.65 = f32[32,32,128]{1,0,2:T(8,128)S(1)} fusion(f32[32,32,128]{1,0,2:T(8,128)} %copy-done, f32[32,32,128]{1,0,2:T(8,128)S(1)} %copy-done.8, f32[32,32,8]{1,0,2:T(8,128)S(1)} %collective-permute-done.119, f32[32,32,8]{1,0,2:T(8,128)S(1)} %collective-permute-done.118, f32[32,1,128]{1,0,2:T(8,128)S(1)} %copy-done.19, ...), kind=kLoop, calls=%fused_computation.131 | loop fusion | flops 5767168 | bytes 6427136 | tf_op jit(solution)/shard_map/add | solution.py:167
  744.0 6.7 multiply_reduce_fusion
  750.8 10.1 %all-reduce.30 = (f32[]{:T(128)}, f32[]{:T(128)}, f32[]{:T(128)}, f32[]{:T(128)}) all-reduce(f32[]{:T(128)} %get-tuple-element.37, f32[]{:T(128)} %get-tuple-element.35, f32[]{:T(128)} %get-tuple-element.33, f32[]{:T(128)} %get-tuple-element.31), channel_id=1, replica_groups=mesh['gx'=4,'gy_0'=4,'gy_1'=2,'gz'=8] {'gx'}, use_global_device_ids=true, to_apply=%region_20.21 | all-reduce | flops 4 | bytes 32 | tf_op jit(solution)/shard_map/psum | solution.py:50
  760.8 10.0 %all-reduce.29 = (f32[]{:T(128)}, f32[]{:T(128)}, f32[]{:T(128)}, f32[]{:T(128)}) all-reduce(f32[]{:T(128)} %get-tuple-element.23, f32[]{:T(128)} %get-tuple-element.24, f32[]{:T(128)} %get-tuple-element.25, f32[]{:T(128)} %get-tuple-element.26), channel_id=1, replica_groups=mesh['gx'=4,'gy_0'=4,'gy_1'=2,'gz'=8] {'gy_0'}, use_global_device_ids=true, to_apply=%region_21.22 | all-reduce | flops 4 | bytes 32 | tf_op jit(solution)/shard_map/psum | solution.py:50
  774.0 17.8 %all-reduce.28 = (f32[]{:T(128)}, f32[]{:T(128)}, f32[]{:T(128)}, f32[]{:T(128)}) all-reduce(f32[]{:T(128)} %get-tuple-element.27, f32[]{:T(128)} %get-tuple-element.28, f32[]{:T(128)} %get-tuple-element.29, f32[]{:T(128)} %get-tuple-element.30), channel_id=1, replica_groups=mesh['gx'=4,'gy_0'=4,'gy_1'=2,'gz'=8] {'gz'}, use_global_device_ids=true, to_apply=%region_23.24 | all-reduce | flops 4 | bytes 32 | tf_op jit(solution)/shard_map/psum | solution.py:50
  (754 shorter events, 575.9 us)
Async XLA Ops:
  1.5 19.6 %collective-permute-start = (f32[8,4]{1,0:T(8,128)S(1)}, f32[8,4]{1,0:T(8,128)S(1)}, u32[]{:S(2)}, u32[]{:S(2)}) collective-permute-start(f32[8,4]{1,0:T(8,128)S(1)} %get-tuple-element.305), channel_id=1, source_target_pairs={{1,0},{2,1},{3,2},{4,3},{5,4},{6,5},{7,6},{9,8},{10,9},{11,10},{12... | collective-permute-start | bytes 392 | tf_op jit(solution)/shard_map/ppermute | solution.py:23
  5.3 20.8 %collective-permute-start.2 = (f32[8,4]{1,0:T(8,128)S(1)}, f32[8,4]{1,0:T(8,128)S(1)}, u32[]{:S(2)}, u32[]{:S(2)}) collective-permute-start(f32[8,4]{1,0:T(8,128)S(1)} %get-tuple-element.304), channel_id=1, source_target_pairs={{0,1},{1,2},{2,3},{3,4},{4,5},{5,6},{6,7},{8,9},{9,10},{10,11},{11... | collective-permute-start | bytes 392 | tf_op jit(solution)/shard_map/ppermute | solution.py:20
  9.5 34.2 %collective-permute-start.3 = (f32[32,32,4]{2,1,0:T(8,128)S(1)}, f32[32,32,4]{2,1,0:T(8,128)S(1)}, u32[]{:S(2)}, u32[]{:S(2)}) collective-permute-start(f32[32,32,4]{2,1,0:T(8,128)S(1)} %get-tuple-element.122), channel_id=1, source_target_pairs={{0,1},{1,2},{2,3},{3,4},{4,5},{5,6},{6,7},{8,9},{9,10},{10,11},{11... | collective-permute-start | bytes 49160 | tf_op jit(solution)/shard_map/ppermute | solution.py:20
  13.4 31.4 %collective-permute-start.1 = (f32[32,32,4]{2,1,0:T(8,128)}, f32[32,32,4]{2,1,0:T(8,128)}, u32[]{:S(2)}, u32[]{:S(2)}) collective-permute-start(f32[32,32,4]{2,1,0:T(8,128)} %get-tuple-element.121), channel_id=1, source_target_pairs={{1,0},{2,1},{3,2},{4,3},{5,4},{6,5},{7,6},{9,8},{10,9},{11,10},{12... | collective-permute-start | bytes 49160 | tf_op jit(solution)/shard_map/ppermute | solution.py:23
  15.8 14.3 %collective-permute-start.22 = (f32[8,4]{1,0:T(8,128)S(1)}, f32[8,4]{1,0:T(8,128)S(1)}, u32[]{:S(2)}, u32[]{:S(2)}) collective-permute-start(f32[8,4]{1,0:T(8,128)S(1)} %get-tuple-element.303), channel_id=1, source_target_pairs={{1,0},{2,1},{3,2},{4,3},{5,4},{6,5},{7,6},{9,8},{10,9},{11,10},{12... | collective-permute-start | bytes 392 | tf_op jit(solution)/shard_map/ppermute | solution.py:23
  83.8 27.4 %collective-permute-start.4 = (f32[32,32,8]{1,0,2:T(8,128)S(1)}, f32[32,32,8]{1,0,2:T(8,128)S(1)}, u32[]{:S(2)}, u32[]{:S(2)}) collective-permute-start(f32[32,32,8]{1,0,2:T(8,128)S(1)} %get-tuple-element.79), channel_id=1, source_target_pairs={{0,1},{1,2},{2,3},{3,4},{4,5},{5,6},{6,7},{8,9},{9,10},{10,11},{11... | collective-permute-start | bytes 98312 | tf_op jit(solution)/shard_map/ppermute | solution.py:20
  87.9 23.3 %collective-permute-start.5 = (f32[32,32,8]{1,0,2:T(8,128)S(1)}, f32[32,32,8]{1,0,2:T(8,128)S(1)}, u32[]{:S(2)}, u32[]{:S(2)}) collective-permute-start(f32[32,32,8]{1,0,2:T(8,128)S(1)} %get-tuple-element.80), channel_id=1, source_target_pairs={{1,0},{2,1},{3,2},{4,3},{5,4},{6,5},{7,6},{9,8},{10,9},{11,10},{12... | collective-permute-start | bytes 98312 | tf_op jit(solution)/shard_map/ppermute | solution.py:23
  99.6 14.3 %collective-permute-start.6 = (f32[1,32,128]{1,0,2:T(1,128)S(1)}, f32[1,32,128]{1,0,2:T(1,128)S(1)}, u32[]{:S(2)}, u32[]{:S(2)}) collective-permute-start(f32[1,32,128]{1,0,2:T(1,128)S(1)} %get-tuple-element.78), channel_id=1, source_target_pairs={{64,0},{128,64},{192,128},{65,1},{129,65},{193,129},{66,2},{130,66... | collective-permute-start | bytes 49160 | tf_op jit(solution)/shard_map/ppermute | solution.py:37
  129.3 28.5 %collective-permute-start.10 = (f32[32,32,8]{1,0,2:T(8,128)S(1)}, f32[32,32,8]{1,0,2:T(8,128)S(1)}, u32[]{:S(2)}, u32[]{:S(2)}) collective-permute-start(f32[32,32,8]{1,0,2:T(8,128)S(1)} %get-tuple-element.74), channel_id=1, source_target_pairs={{0,1},{1,2},{2,3},{3,4},{4,5},{5,6},{6,7},{8,9},{9,10},{10,11},{11... | collective-permute-start | bytes 98312 | tf_op jit(solution)/shard_map/ppermute | solution.py:20
  134.2 23.6 %collective-permute-start.11 = (f32[32,32,8]{1,0,2:T(8,128)S(1)}, f32[32,32,8]{1,0,2:T(8,128)S(1)}, u32[]{:S(2)}, u32[]{:S(2)}) collective-permute-start(f32[32,32,8]{1,0,2:T(8,128)S(1)} %get-tuple-element.73), channel_id=1, source_target_pairs={{1,0},{2,1},{3,2},{4,3},{5,4},{6,5},{7,6},{9,8},{10,9},{11,10},{12... | collective-permute-start | bytes 98312 | tf_op jit(solution)/shard_map/ppermute | solution.py:23
  145.9 14.6 %collective-permute-start.12 = (f32[1,32,128]{1,0,2:T(1,128)S(1)}, f32[1,32,128]{1,0,2:T(1,128)S(1)}, u32[]{:S(2)}, u32[]{:S(2)}) collective-permute-start(f32[1,32,128]{1,0,2:T(1,128)S(1)} %get-tuple-element.72), channel_id=1, source_target_pairs={{64,0},{128,64},{192,128},{65,1},{129,65},{193,129},{66,2},{130,66... | collective-permute-start | bytes 49160 | tf_op jit(solution)/shard_map/ppermute | solution.py:37
  147.4 13.1 %collective-permute-start.13 = (f32[1,32,128]{1,0,2:T(1,128)S(1)}, f32[1,32,128]{1,0,2:T(1,128)S(1)}, u32[]{:S(2)}, u32[]{:S(2)}) collective-permute-start(f32[1,32,128]{1,0,2:T(1,128)S(1)} %get-tuple-element.71), channel_id=1, source_target_pairs={{0,64},{64,128},{128,192},{1,65},{65,129},{129,193},{2,66},{66,130... | collective-permute-start | bytes 49160 | tf_op jit(solution)/shard_map/ppermute | solution.py:36
  260.7 13.1 %collective-permute-start.24 = (f32[16,16,8]{1,0,2:T(8,128)S(1)}, f32[16,16,8]{1,0,2:T(8,128)S(1)}, u32[]{:S(2)}, u32[]{:S(2)}) collective-permute-start(f32[16,16,8]{1,0,2:T(8,128)S(1)} %get-tuple-element.119), channel_id=1, source_target_pairs={{0,1},{1,2},{2,3},{3,4},{4,5},{5,6},{6,7},{8,9},{9,10},{10,11},{11... | collective-permute-start | bytes 24584 | tf_op jit(solution)/shard_map/ppermute | solution.py:20
  368.6 14.1 %collective-permute-start.50 = (f32[8,8,8]{1,0,2:T(8,128)S(1)}, f32[8,8,8]{1,0,2:T(8,128)S(1)}, u32[]{:S(2)}, u32[]{:S(2)}) collective-permute-start(f32[8,8,8]{1,0,2:T(8,128)S(1)} %get-tuple-element.163), channel_id=1, source_target_pairs={{0,1},{1,2},{2,3},{3,4},{4,5},{5,6},{6,7},{8,9},{9,10},{10,11},{11... | collective-permute-start | bytes 6152 | tf_op jit(solution)/shard_map/ppermute | solution.py:20
  373.7 13.5 %collective-permute-start.51 = (f32[8,8,8]{1,0,2:T(8,128)S(1)}, f32[8,8,8]{1,0,2:T(8,128)S(1)}, u32[]{:S(2)}, u32[]{:S(2)}) collective-permute-start(f32[8,8,8]{1,0,2:T(8,128)S(1)} %get-tuple-element.162), channel_id=1, source_target_pairs={{1,0},{2,1},{3,2},{4,3},{5,4},{6,5},{7,6},{9,8},{10,9},{11,10},{12... | collective-permute-start | bytes 6152 | tf_op jit(solution)/shard_map/ppermute | solution.py:23
  422.4 13.4 %collective-permute-start.64 = (f32[4,4,8]{2,1,0:T(4,128)S(1)}, f32[4,4,8]{2,1,0:T(4,128)S(1)}, u32[]{:S(2)}, u32[]{:S(2)}) collective-permute-start(f32[4,4,8]{2,1,0:T(4,128)S(1)} %get-tuple-element.194), channel_id=1, source_target_pairs={{0,1},{1,2},{2,3},{3,4},{4,5},{5,6},{6,7},{8,9},{9,10},{10,11},{11... | collective-permute-start | bytes 1544 | tf_op jit(solution)/shard_map/ppermute | solution.py:20
  560.7 13.6 %collective-permute-start.100 = (f32[16,16,8]{1,0,2:T(8,128)S(1)}, f32[16,16,8]{1,0,2:T(8,128)S(1)}, u32[]{:S(2)}, u32[]{:S(2)}) collective-permute-start(f32[16,16,8]{1,0,2:T(8,128)S(1)} %get-tuple-element.99), channel_id=1, source_target_pairs={{0,1},{1,2},{2,3},{3,4},{4,5},{5,6},{6,7},{8,9},{9,10},{10,11},{11... | collective-permute-start | bytes 24584 | tf_op jit(solution)/shard_map/ppermute | solution.py:20
  565.5 13.3 %collective-permute-start.101 = (f32[16,16,8]{1,0,2:T(8,128)S(1)}, f32[16,16,8]{1,0,2:T(8,128)S(1)}, u32[]{:S(2)}, u32[]{:S(2)}) collective-permute-start(f32[16,16,8]{1,0,2:T(8,128)S(1)} %get-tuple-element.100), channel_id=1, source_target_pairs={{1,0},{2,1},{3,2},{4,3},{5,4},{6,5},{7,6},{9,8},{10,9},{11,10},{12... | collective-permute-start | bytes 24584 | tf_op jit(solution)/shard_map/ppermute | solution.py:23
  621.5 28.6 %collective-permute-start.112 = (f32[32,32,8]{1,0,2:T(8,128)S(1)}, f32[32,32,8]{1,0,2:T(8,128)S(1)}, u32[]{:S(2)}, u32[]{:S(2)}) collective-permute-start(f32[32,32,8]{1,0,2:T(8,128)S(1)} %get-tuple-element.65), channel_id=1, source_target_pairs={{0,1},{1,2},{2,3},{3,4},{4,5},{5,6},{6,7},{8,9},{9,10},{10,11},{11... | collective-permute-start | bytes 98312 | tf_op jit(solution)/shard_map/ppermute | solution.py:20
  625.8 24.3 %collective-permute-start.113 = (f32[32,32,8]{1,0,2:T(8,128)S(1)}, f32[32,32,8]{1,0,2:T(8,128)S(1)}, u32[]{:S(2)}, u32[]{:S(2)}) collective-permute-start(f32[32,32,8]{1,0,2:T(8,128)S(1)} %get-tuple-element.66), channel_id=1, source_target_pairs={{1,0},{2,1},{3,2},{4,3},{5,4},{6,5},{7,6},{9,8},{10,9},{11,10},{12... | collective-permute-start | bytes 98312 | tf_op jit(solution)/shard_map/ppermute | solution.py:23
  638.4 14.8 %collective-permute-start.114 = (f32[1,32,128]{1,0,2:T(1,128)S(1)}, f32[1,32,128]{1,0,2:T(1,128)S(1)}, u32[]{:S(2)}, u32[]{:S(2)}) collective-permute-start(f32[1,32,128]{1,0,2:T(1,128)S(1)} %get-tuple-element.64), channel_id=1, source_target_pairs={{64,0},{128,64},{192,128},{65,1},{129,65},{193,129},{66,2},{130,66... | collective-permute-start | bytes 49160 | tf_op jit(solution)/shard_map/ppermute | solution.py:37
  639.7 13.5 %collective-permute-start.115 = (f32[1,32,128]{1,0,2:T(1,128)S(1)}, f32[1,32,128]{1,0,2:T(1,128)S(1)}, u32[]{:S(2)}, u32[]{:S(2)}) collective-permute-start(f32[1,32,128]{1,0,2:T(1,128)S(1)} %get-tuple-element.63), channel_id=1, source_target_pairs={{0,64},{64,128},{128,192},{1,65},{65,129},{129,193},{2,66},{66,130... | collective-permute-start | bytes 49160 | tf_op jit(solution)/shard_map/ppermute | solution.py:36
  662.5 30.3 %collective-permute-start.118 = (f32[32,32,8]{1,0,2:T(8,128)S(1)}, f32[32,32,8]{1,0,2:T(8,128)S(1)}, u32[]{:S(2)}, u32[]{:S(2)}) collective-permute-start(f32[32,32,8]{1,0,2:T(8,128)S(1)} %get-tuple-element.59), channel_id=1, source_target_pairs={{0,1},{1,2},{2,3},{3,4},{4,5},{5,6},{6,7},{8,9},{9,10},{10,11},{11... | collective-permute-start | bytes 98312 | tf_op jit(solution)/shard_map/ppermute | solution.py:20
  667.7 25.2 %collective-permute-start.119 = (f32[32,32,8]{1,0,2:T(8,128)S(1)}, f32[32,32,8]{1,0,2:T(8,128)S(1)}, u32[]{:S(2)}, u32[]{:S(2)}) collective-permute-start(f32[32,32,8]{1,0,2:T(8,128)S(1)} %get-tuple-element.60), channel_id=1, source_target_pairs={{1,0},{2,1},{3,2},{4,3},{5,4},{6,5},{7,6},{9,8},{10,9},{11,10},{12... | collective-permute-start | bytes 98312 | tf_op jit(solution)/shard_map/ppermute | solution.py:23
  676.2 13.7 %collective-permute-start.123 = (f32[32,1,128]{2,0,1:T(8,128)S(1)}, f32[32,1,128]{2,0,1:T(8,128)S(1)}, u32[]{:S(2)}, u32[]{:S(2)}) collective-permute-start(f32[32,1,128]{2,0,1:T(8,128)S(1)} %copy.595), channel_id=1, source_target_pairs={{0,8},{8,16},{16,24},{24,32},{32,40},{40,48},{48,56},{1,9},{9,17},... | collective-permute-start | bytes 49160 | tf_op jit(solution)/shard_map/ppermute | solution.py:36
  680.8 14.7 %collective-permute-start.120 = (f32[1,32,128]{1,0,2:T(1,128)S(1)}, f32[1,32,128]{1,0,2:T(1,128)S(1)}, u32[]{:S(2)}, u32[]{:S(2)}) collective-permute-start(f32[1,32,128]{1,0,2:T(1,128)S(1)} %get-tuple-element.58), channel_id=1, source_target_pairs={{64,0},{128,64},{192,128},{65,1},{129,65},{193,129},{66,2},{130,66... | collective-permute-start | bytes 49160 | tf_op jit(solution)/shard_map/ppermute | solution.py:37
  682.1 13.4 %collective-permute-start.121 = (f32[1,32,128]{1,0,2:T(1,128)S(1)}, f32[1,32,128]{1,0,2:T(1,128)S(1)}, u32[]{:S(2)}, u32[]{:S(2)}) collective-permute-start(f32[1,32,128]{1,0,2:T(1,128)S(1)} %get-tuple-element.57), channel_id=1, source_target_pairs={{0,64},{64,128},{128,192},{1,65},{65,129},{129,193},{2,66},{66,130... | collective-permute-start | bytes 49160 | tf_op jit(solution)/shard_map/ppermute | solution.py:36
  711.0 29.9 %collective-permute-start.124 = (f32[32,32,8]{1,0,2:T(8,128)S(1)}, f32[32,32,8]{1,0,2:T(8,128)S(1)}, u32[]{:S(2)}, u32[]{:S(2)}) collective-permute-start(f32[32,32,8]{1,0,2:T(8,128)S(1)} %get-tuple-element.54), channel_id=1, source_target_pairs={{0,1},{1,2},{2,3},{3,4},{4,5},{5,6},{6,7},{8,9},{9,10},{10,11},{11... | collective-permute-start | bytes 98312 | tf_op jit(solution)/shard_map/ppermute | solution.py:20
  714.9 26.0 %collective-permute-start.125 = (f32[32,32,8]{1,0,2:T(8,128)S(1)}, f32[32,32,8]{1,0,2:T(8,128)S(1)}, u32[]{:S(2)}, u32[]{:S(2)}) collective-permute-start(f32[32,32,8]{1,0,2:T(8,128)S(1)} %get-tuple-element.53), channel_id=1, source_target_pairs={{1,0},{2,1},{3,2},{4,3},{5,4},{6,5},{7,6},{9,8},{10,9},{11,10},{12... | collective-permute-start | bytes 98312 | tf_op jit(solution)/shard_map/ppermute | solution.py:23
  723.4 14.5 %collective-permute-start.129 = (f32[32,1,128]{2,0,1:T(8,128)S(1)}, f32[32,1,128]{2,0,1:T(8,128)S(1)}, u32[]{:S(2)}, u32[]{:S(2)}) collective-permute-start(f32[32,1,128]{2,0,1:T(8,128)S(1)} %copy.599), channel_id=1, source_target_pairs={{0,8},{8,16},{16,24},{24,32},{32,40},{40,48},{48,56},{1,9},{9,17},... | collective-permute-start | bytes 49160 | tf_op jit(solution)/shard_map/ppermute | solution.py:36
  729.0 14.5 %collective-permute-start.126 = (f32[1,32,128]{1,0,2:T(1,128)S(1)}, f32[1,32,128]{1,0,2:T(1,128)S(1)}, u32[]{:S(2)}, u32[]{:S(2)}) collective-permute-start(f32[1,32,128]{1,0,2:T(1,128)S(1)} %get-tuple-element.52), channel_id=1, source_target_pairs={{64,0},{128,64},{192,128},{65,1},{129,65},{193,129},{66,2},{130,66... | collective-permute-start | bytes 49160 | tf_op jit(solution)/shard_map/ppermute | solution.py:37
  730.3 13.2 %collective-permute-start.127 = (f32[1,32,128]{1,0,2:T(1,128)S(1)}, f32[1,32,128]{1,0,2:T(1,128)S(1)}, u32[]{:S(2)}, u32[]{:S(2)}) collective-permute-start(f32[1,32,128]{1,0,2:T(1,128)S(1)} %get-tuple-element.51), channel_id=1, source_target_pairs={{0,64},{64,128},{128,192},{1,65},{65,129},{129,193},{2,66},{66,130... | collective-permute-start | bytes 49160 | tf_op jit(solution)/shard_map/ppermute | solution.py:36
  (222 other events, 6159.9 us)
where the time goes:
time: 807 us; the launch traced here: 799 us
  starting transfers between devices  360 us (45%)
  local copies, waits for them, and re-layouts  202 us (25%)
  other arithmetic  108 us (13%)
  waiting for transfers between devices  78.9 us (10%)
  blocking collectives  41 us (5%)
    ppermute x37, starting transfers between devices, padded_2(): lax.ppermute(lax.slice_in_dim(block, block.shape[dim] - width, None, axis...  143 us
    ppermute x28, starting transfers between devices, padded_3(): lax.ppermute(last, axis, up)  114 us
    ppermute x37, waiting for transfers between devices, padded_2(): lax.ppermute(lax.slice_in_dim(block, 0, width, axis=dim), axis, backward)  69.1 us
    ppermute x37, starting transfers between devices, padded_2(): lax.ppermute(lax.slice_in_dim(block, 0, width, axis=dim), axis, backward)  66.5 us
    unnamed x264, local copies, waits for them, and re-layouts  42.3 us
    psum x4, blocking collectives, by_axis(): array = lax.psum(array, axis)  41 us
    add x10, other arithmetic, sweep(): return error + relaxation * (right - apply_fn(error)) / diag  38.5 us
    ppermute x28, starting transfers between devices, padded_3(): lax.ppermute(first, axis, [(b, a) for a, b in up])  36.3 us
  transfers between devices with their start and end apart: 130, of which 32 were waited for; matrix products, arithmetic and copies ran while one was open for 13% of the time, Pallas kernels for 0%

commit v1 on v0

v1 whole, which is shorter than its diff:
```python
import jax
import jax.numpy as jnp
from jax import lax
from jax.sharding import PartitionSpec as P
from jax.experimental import pallas as pl
from jax.experimental.pallas import tpu as pltpu

OFFSETS = (-4, -3, -2, -1, 1, 2, 3, 4)
RELAX = 0.45
NX, NY, NZ = 128, 256, 1024
F32, BF16 = jnp.float32, jnp.bfloat16
H0, H1, H2, H3 = 4, 5, 11, 4
S0, S1, S2, S3 = 1.0, 0.25, 0.0625, 0.015625
SLOT = 40
VMEM_LIMIT = 56 * 2**20


def place_0(p):
    return jnp.where(p < 192, p, p - 256)


def place_1(p):
    lane = p & 127
    return jnp.where((lane < 96) == (p < 128), lane, lane - 128)


def place_2(p):
    lane = p & 127
    return jnp.where((lane < 80) == (p < 128), lane, lane - 128)


def place_3(p):
    return jnp.where(p < 64, p, p - 128)


def inside(z, iz, level, reach):
    count = 128 >> level
    glob = iz * count + z
    return (z >= -reach) & (z < count + reach) & (glob >= 0) & (glob < (NZ >> level))


def rows(shape, dim):
    return lax.broadcasted_iota(jnp.int32, shape, dim)


def halves(a):
    hi = a.astype(BF16)
    return hi, (a - hi.astype(F32)).astype(BF16)


def thrice(matrix):
    hi, lo = halves(matrix)
    return jnp.concatenate([hi, hi, lo], axis=0)


def times(field, matrix):
    shape = field.shape
    hi, lo = halves(field.reshape(shape[0] * shape[1], shape[2]))
    out = jnp.dot(jnp.concatenate([hi, lo, hi], axis=1), matrix, preferred_element_type=F32)
    return out.reshape(shape[0], shape[1], matrix.shape[1])


def times_exact(field, matrix):
    shape = field.shape
    hi, lo = halves(field.reshape(shape[0] * shape[1], shape[2]))
    out = jnp.dot(jnp.concatenate([hi, lo], axis=1), matrix, preferred_element_type=F32)
    return out.reshape(shape[0], shape[1], matrix.shape[1])


def operators(w, place, iz, level, reach, stiffness):
    n = w.shape[1]
    zk = place(rows((n, n), 0))
    zn = place(rows((n, n), 1))
    both = inside(zk, iz, level, reach) & inside(zn, iz, level, reach)
    gap = jnp.where(both, zk - zn, 99)
    band = jnp.where(gap == 0, 1.0, 0.0)
    eye = jnp.where(rows((n, n), 0) == rows((n, n), 1), 1.0, 0.0)
    for j, offset in enumerate(OFFSETS):
        band = jnp.where(gap == offset, w[j : j + 1, :], band)
    gram = lax.dot_general(
        band, band, (((1,), (1,)), ((), ())), precision=lax.Precision.HIGHEST, preferred_element_type=F32
    )
    diag = jnp.sum(gram * eye, axis=0, keepdims=True) + 6.0 * stiffness
    line = inside(place(rows((1, n), 1)), iz, level, reach)
    factor = jnp.where(line, RELAX / diag, 0.0)
    op = gram + stiffness * (6.0 * eye - jnp.where((gap == 1) | (gap == -1), 1.0, 0.0))
    return band, op, eye - op * factor, factor


def restrict_matrix(place_f, n_f, place_c, n_c, iz, level, reach):
    zf = place_f(rows((n_f, n_c), 0))
    zc = place_c(rows((n_f, n_c), 1))
    gap = zf - 2 * zc
    near = jnp.where((gap == 0) | (gap == 1), 0.375, 0.0) + jnp.where((gap == -1) | (gap == 2), 0.125, 0.0)
    m = jnp.where(inside(zf, iz, level, reach), near, 0.0).astype(BF16)
    return jnp.concatenate([m, m], axis=0)


def prolong_matrix(place_c, n_c, place_f, n_f, iz, level, reach):
    zc = place_c(rows((n_c, n_f), 0))
    zf = place_f(rows((n_c, n_f), 1))
    gap = zf - 2 * zc
    near = jnp.where((gap == 0) | (gap == 1), 0.75, 0.0) + jnp.where((gap == -1) | (gap == 2), 0.25, 0.0)
    m = jnp.where(inside(zf, iz, level, reach), near, 0.0).astype(BF16)
    return jnp.concatenate([m, m], axis=0)


def plane_mask(shape, level, ix, iy, reach):
    x = ix * (32 >> level) + rows(shape, 0) - reach
    y = iy * (32 >> level) + rows(shape, 1) - reach
    ok = (x >= 0) & (x < (NX >> level)) & (y >= 0) & (y < (NY >> level))
    return jnp.where(ok, 1.0, 0.0)


def around(ref, a, b):
    mid = ref[a:b]
    count = mid.shape[1]
    return mid, (ref[a + 1 : b + 1] + ref[a - 1 : b - 1]) + (pltpu.roll(mid, 1, 1) + pltpu.roll(mid, count - 1, 1))


def chunks(a, b, step):
    return [(c, min(c + step, b)) for c in range(a, b, step)]


def relax(src, dst, a, b, step, matrix, right, side):
    for p, q in chunks(a, b, step):
        mid, near = around(src, p, q)
        dst[p:q] = times(mid, matrix) + right(p, q) + side[p:q] * near


def weights_kernel(pos, w0, w1, b0, k0, m0, f0, k1, m1, f1):
    iz = pos[2]
    band, op, step, factor = operators(w0[...], place_0, iz, 0, 36, S0)
    b0[...] = thrice(jnp.transpose(band))
    k0[...] = thrice(step)
    m0[...] = thrice(op)
    f0[...] = jnp.broadcast_to(factor, (8, 256))
    lane = rows((8, 128), 1)
    first, second = w1[:, :128], w1[:, 128:]
    laid = jnp.concatenate([jnp.where(lane < 96, first, second), jnp.where(lane < 96, second, first)], axis=1)
    band, op, step, factor = operators(laid, place_1, iz, 1, 41, S1)
    k1[...] = thrice(step[:, :128])
    m1[...] = thrice(op[:128, :128])
    f1[...] = jnp.broadcast_to(factor, (8, 256))


def pack_kernel(width, reach, count, n, data, xlo, xhi, ylo, yhi, full, to_left, to_right):
    def plane(p):
        if p >= n + 2 * reach:
            return jnp.zeros(full.shape[1:], F32)
        if p < reach:
            mid = xlo[p]
        elif p < reach + n:
            mid = data[p - reach]
        else:
            mid = xhi[p - reach - n]
        parts = [ylo[p], mid, yhi[p]]
        rest = full.shape[1] - n - 2 * reach
        if rest:
            parts.append(jnp.zeros((rest, count), F32))
        out = jnp.concatenate(parts, axis=0)
        if count < 128:
            out = jnp.concatenate([out, jnp.zeros((full.shape[1], 128 - count), F32)], axis=1)
        return out

    lane = rows(full.shape[1:], 1)
    for g in range(to_left.shape[0]):
        left, right = None, None
        for i in range(3):
            p = 3 * g + i
            value = plane(p)
            if p < full.shape[0]:
                full[p] = value
            a = pltpu.roll(value, SLOT * i, 1) if i else value
            b = pltpu.roll(value, (SLOT * i + width - count) % 128, 1)
            left = a if i == 0 else jnp.where(lane < SLOT * i, left, a)
            right = b if i == 0 else jnp.where(lane < SLOT * i, right, b)
        to_left[g] = left
        to_right[g] = right


def down_0_kernel(pos, dxy, from_right, from_left, b0, k0, m0, f0, r1, e_out, r_out, stat, d, e0, side, g, gx):
    ix, iy, iz = pos[0], pos[1], pos[2]
    lane = rows((40, 128), 1)
    for p in range(40):
        group, i = divmod(p, 3)
        mask = plane_mask((1, 40, 128), 0, ix, iy, H0) if False else None
        xr = ix * 32 + p - H0
        y = iy * 32 + rows((40, 128), 0) - H0
        ok = jnp.where((y >= 0) & (y < NY), jnp.where((xr >= 0) & (xr < NX), 1.0, 0.0), 0.0)
        right = pltpu.roll(from_right[group], (128 - SLOT * i) % 128, 1) if i else from_right[group]
        left = pltpu.roll(from_left[group], (92 - SLOT * i) % 128, 1)
        d[p, :, :128] = dxy[p] * ok
        d[p, :, 128:] = jnp.where(lane < 36, right, jnp.where(lane >= 92, left, 0.0)) * ok
        fs = f0[0:1, :] * S0
        side[p, :, :128] = ok * fs[:, :128]
        side[p, :, 128:] = ok * fs[:, 128:]
    factor = f0[0:1, :].reshape(1, 1, 256)
    for p, q in chunks(0, 40, 8):
        r = times(d[p:q], b0[...])
        r_out[p:q] = r
        e0[p:q] = r * factor
    relax(e0, e_out, 1, 39, 10, k0[...], lambda p, q: e0[p:q], side)
    e_out[0] = jnp.zeros((40, 256), F32)
    e_out[39] = jnp.zeros((40, 256), F32)
    total = jnp.zeros((40, 128), F32)
    for p, q in chunks(3, 37, 9):
        mid, near = around(e_out, p, q)
        value = r_out[p:q] - times(mid, m0[...]) + S0 * near
        x = ix * 32 + rows(value.shape, 0) + (p - H0)
        y = iy * 32 + rows(value.shape, 1) - H0
        value = jnp.where((x >= 0) & (x < NX) & (y >= 0) & (y < NY), value, 0.0)
        g[p:q] = value
        own = value[max(p, 4) - p : min(q, 36) - p, :, :128]
        total = total + jnp.sum(own * own, axis=0)
    row = rows((40, 128), 0)
    stat[...] = jnp.full((8, 128), jnp.sum(jnp.where((row >= 4) & (row < 36), total, 0.0)), F32)
    for i in range(16):
        value = ((g[2 * i + 3] + g[2 * i + 6]) + 3.0 * (g[2 * i + 4] + g[2 * i + 5])) * 0.125
        gx[i, 0] = value[:, :128]
        gx[i, 1] = value[:, 128:]
    gy = [
        jnp.concatenate([gx[:, t, pl.ds(3 + a, 16, stride=2), :] for t in range(2)], axis=2) for a in range(4)
    ]
    gy = ((gy[0] + gy[3]) + 3.0 * (gy[1] + gy[2])) * 0.125
    fold = restrict_matrix(place_0, 256, lambda q: q, 128, iz, 0, 36)
    r1[...] = times_exact(gy, fold)[:, :, :64]


def down_1_kernel(pos, rxy, from_right, from_left, k1, m1, f1, w2, msg, e_out, r_out, stat, e0, e0b, side, g, gx):
    ix, iy, iz = pos[0], pos[1], pos[2]
    lane = rows((32, 128), 1)
    for p in range(26):
        group, i = divmod(p, 3)
        xr = ix * 16 + p - H1
        yrow = rows((32, 128), 0)
        y = iy * 16 + yrow - H1
        ok = jnp.where(
            (y >= 0) & (y < NY // 2) & (yrow < 26), jnp.where((xr >= 0) & (xr < NX // 2), 1.0, 0.0), 0.0
        )
        right = pltpu.roll(from_right[group], (64 - SLOT * i) % 128, 1)
        left = pltpu.roll(from_left[group], (91 - SLOT * i) % 128, 1)
        first = jnp.where(lane < 64, rxy[p], jnp.where(lane < 101, right, 0.0))
        second = jnp.where(lane >= 91, left, 0.0)
        main = jnp.where(lane < 96, first, second) * ok
        rest = jnp.where(lane < 96, second, first) * ok
        r_out[p] = main
        e0[p] = main * f1[0:1, :128]
        e0b[p] = rest * f1[0:1, 128:]
        side[p] = ok * (f1[0:1, :128] * S1)
    for p, q in chunks(1, 25, 8):
        mid, near = around(e0, p, q)
        both = jnp.concatenate([mid, e0b[p:q]], axis=2)
        e_out[p:q] = times(both, k1[...]) + mid + side[p:q] * near
    e_out[0] = jnp.zeros((32, 128), F32)
    e_out[25] = jnp.zeros((32, 128), F32)
    total = jnp.zeros((32, 128), F32)
    for p, q in chunks(4, 22, 9):
        mid, near = around(e_out, p, q)
        value = r_out[p:q] - times(mid, m1[...]) + S1 * near
        x = ix * 16 + rows(value.shape, 0) + (p - H1)
        y = iy * 16 + rows(value.shape, 1) - H1
        value = jnp.where((x >= 0) & (x < NX // 2) & (y >= 0) & (y < NY // 2), value, 0.0)
        g[p:q] = value
        own = value[max(p, 5) - p : min(q, 21) - p]
        total = total + jnp.sum(own * own, axis=0)
    row = rows((32, 128), 0)
    keep = (row >= 5) & (row < 21) & (lane < 64)
    stat[...] = jnp.full((8, 128), jnp.sum(jnp.where(keep, total, 0.0)), F32)
    for i in range(8):
        gx[i] = ((g[2 * i + 4] + g[2 * i + 7]) + 3.0 * (g[2 * i + 5] + g[2 * i + 6])) * 0.125
    gy = [gx[:, pl.ds(4 + a, 8, stride=2), :] for a in range(4)]
    gy = ((gy[0] + gy[3]) + 3.0 * (gy[1] + gy[2])) * 0.125
    fold = restrict_matrix(place_1, 128, lambda q: q, 128, iz, 1, 32)
    msg[:8] = times_exact(gy, fold)[:, :, :32]
    msg[8] = w2[...]


def weights_2_kernel(pos, w2, w3, k2, k2u, m2, f2, k3, f3):
    iz = pos[2]
    lane = rows((8, 128), 1)
    first, second = w2[:, :128], w2[:, 128:]
    laid = jnp.concatenate([jnp.where(lane < 80, first, second), jnp.where(lane < 80, second, first)], axis=1)
    band, op, step, factor = operators(laid, place_2, iz, 2, 69, S2)
    k2[...] = thrice(step)
    k2u[...] = thrice(step[:128, :128])
    m2[...] = thrice(op)
    f2[...] = jnp.broadcast_to(factor, (8, 256))
    band, op, step, factor = operators(w3[...], place_3, iz, 3, 28, S3)
    k3[...] = thrice(step)
    f3[...] = jnp.broadcast_to(factor, (8, 128))


def up_kernel(
    pos, r2x, ya, yb, yc, yd, k2, k2u, m2, f2, k3, f3,
    k1, f1, e1s, r1s, k0, m0, f0, e0s, r0s, stat0, stat1,
    sol, res, stat,
    ra, ea, eb, side2, gx2, r3, e3, side3, c3, cy2, ua, ub, side1, cy1, va, vb, side0, cy0,
):
    ix, iy, iz = pos[0], pos[1], pos[2]
    lane = rows((32, 128), 1)
    yrow = rows((32, 128), 0)
    for p in range(30):
        xr = ix * 8 + p - H2
        y = iy * 8 + yrow - H2
        ok = jnp.where(
            (y >= 0) & (y < NY // 4) & (yrow < 30), jnp.where((xr >= 0) & (xr < NX // 4), 1.0, 0.0), 0.0
        )
        full = jnp.concatenate([yc[p], ya[p], r2x[p], yb[p], yd[p], jnp.zeros((2, 256), F32)], axis=0)
        first, second = full[:, :128], full[:, 128:]
        main = jnp.where(lane < 80, first, second) * ok
        rest = jnp.where(lane < 80, second, first) * ok
        ra[p, :, :128] = main
        ra[p, :, 128:] = rest
        ea[p, :, :128] = main * f2[0:1, :128]
        ea[p, :, 128:] = rest * f2[0:1, 128:]
        side2[p, :, :128] = ok * (f2[0:1, :128] * S2)
        side2[p, :, 128:] = ok * (f2[0:1, 128:] * S2)
    relax(ea, eb, 1, 29, 10, k2[...], lambda p, q: ea[p:q], side2)
    total = jnp.zeros((32, 128), F32)
    for p, q in chunks(2, 28, 13):
        mid, near = around(eb, p, q)
        value = ra[p:q] - times(mid, m2[...]) + S2 * near
        x = ix * 8 + rows(value.shape, 0) + (p - H2)
        y = iy * 8 + rows(value.shape, 1) - H2
        value = jnp.where((x >= 0) & (x < NX // 4) & (y >= 0) & (y < NY // 4), value, 0.0)
        ea[p:q] = value
        own = value[max(p, 11) - p : min(q, 19) - p, :, :128]
        total = total + jnp.sum(own * own, axis=0)
    keep = (yrow >= 11) & (yrow < 19) & (lane < 32)
    sum2 = jnp.sum(jnp.where(keep, total, 0.0))
    for i in range(12):
        value = ((ea[2 * i + 2] + ea[2 * i + 5]) + 3.0 * (ea[2 * i + 3] + ea[2 * i + 4])) * 0.125
        gx2[i, 0, :32] = value[:, :128]
        gx2[i, 1, :32] = value[:, 128:]
        gx2[i, 0, 32:] = jnp.zeros((8, 128), F32)
        gx2[i, 1, 32:] = jnp.zeros((8, 128), F32)
    gy = [
        jnp.concatenate([gx2[:, t, pl.ds(2 + a, 16, stride=2), :] for t in range(2)], axis=2) for a in range(4)
    ]
    gy = ((gy[0] + gy[3]) + 3.0 * (gy[1] + gy[2])) * 0.125
    fold = restrict_matrix(place_2, 256, place_3, 128, iz, 2, 65)
    mask = plane_mask((12, 16, 128), 3, ix, iy, H3)
    right3 = times_exact(gy, fold) * mask
    factor3 = f3[0:1, :].reshape(1, 1, 128)
    e3[...] = right3 * factor3
    side3[...] = mask * (factor3 * S3)
    c3[...] = jnp.zeros((12, 16, 128), F32)
    relax(e3, c3, 1, 11, 10, k3[...], lambda p, q: e3[p:q], side3)
    grow = prolong_matrix(place_3, 128, place_2, 128, iz, 2, 69)
    cz = times_exact(c3[...], grow)
    below, above = pltpu.roll(cz, 1, 1), pltpu.roll(cz, 15, 1)
    cy2[...] = jnp.zeros((12, 32, 128), F32)
    cy2[:, pl.ds(3, 12, stride=2), :] = (0.75 * cz + 0.25 * below)[:, :12]
    cy2[:, pl.ds(4, 12, stride=2), :] = (0.75 * cz + 0.25 * above)[:, :12]
    ua2, ub2 = r3, gx2
    fr2 = f2[0:1, :128].reshape(1, 1, 128)
    for xf in range(6, 24):
        f = xf - H2
        j = f // 2 + 4
        other = j - 1 if f % 2 == 0 else j + 1
        xr = ix * 8 + f
        y = iy * 8 + yrow - H2
        ok = jnp.where((y >= 0) & (y < NY // 4), jnp.where((xr >= 0) & (xr < NX // 4), 1.0, 0.0), 0.0)
        ea[xf, :, :128] = eb[xf, :, :128] + ok * (0.75 * cy2[j] + 0.25 * cy2[other])

    def relax_2(src, dst, a, b):
        for p, q in chunks(a, b, 8):
            mid = src[p:q, :, :128]
            near = (src[p + 1 : q + 1, :, :128] + src[p - 1 : q - 1, :, :128]) + (
                pltpu.roll(mid, 1, 1) + pltpu.roll(mid, 31, 1)
            )
            dst[p:q, :, :128] = times(mid, k2u[...]) + fr2 * ra[p:q, :, :128] + side2[p:q, :, :128] * near

    relax_2(ea, eb, 7, 23)
    relax_2(eb, ea, 8, 22)
    grow = prolong_matrix(place_2, 128, place_1, 128, iz, 1, 41)
    for p in range(14):
        r3[p] = ea[8 + p, :, :128]
    r3[...] = times_exact(r3[...], grow)
    cy1[...] = jnp.zeros((14, 32, 128), F32)
    cy1[:, pl.ds(1, 12, stride=2), :] = 0.75 * r3[:, 9:21, :] + 0.25 * r3[:, 8:20, :]
    cy1[:, pl.ds(2, 12, stride=2), :] = 0.75 * r3[:, 9:21, :] + 0.25 * r3[:, 10:22, :]
    fr1 = f1[0:1, :128].reshape(1, 1, 128)
    for xf in range(26):
        f = xf - H1
        xr = ix * 16 + f
        y = iy * 16 + yrow - H1
        ok = jnp.where((y >= 0) & (y < NY // 2), jnp.where((xr >= 0) & (xr < NX // 2), 1.0, 0.0), 0.0)
        side1[xf] = ok * (f1[0:1, :128] * S1)
        if 1 <= xf <= 24:
            j = f // 2 + 3
            other = j - 1 if f % 2 == 0 else j + 1
            ua[xf] = e1s[xf] + ok * (0.75 * cy1[j] + 0.25 * cy1[other])
    relax(ua, ub, 2, 24, 11, k1[...], lambda p, q: fr1 * r1s[p:q], side1)
    relax(ub, ua, 3, 23, 10, k1[...], lambda p, q: fr1 * r1s[p:q], side1)
    grow = prolong_matrix(place_1, 128, place_0, 256, iz, 0, 36)
    for p, q in chunks(0, 20, 10):
        cz = times_exact(ua[3 + p : 3 + q], grow)
        for t in range(2):
            part = cz[:, :, 128 * t : 128 * t + 128]
            cy0[p:q, t, pl.ds(0, 20, stride=2), :] = 0.75 * part[:, 3:23] + 0.25 * part[:, 2:22]
            cy0[p:q, t, pl.ds(1, 20, stride=2), :] = 0.75 * part[:, 3:23] + 0.25 * part[:, 4:24]
    fr0 = f0[0:1, :].reshape(1, 1, 256)
    for xf in range(40):
        f = xf - H0
        xr = ix * 32 + f
        y = iy * 32 + rows((40, 128), 0) - H0
        ok = jnp.where((y >= 0) & (y < NY), jnp.where((xr >= 0) & (xr < NX), 1.0, 0.0), 0.0)
        for t in range(2):
            part = slice(128 * t, 128 * t + 128)
            side0[xf, :, part] = ok * (f0[0:1, part] * S0)
            if 1 <= xf <= 38:
                j = f // 2 + 2
                other = j - 1 if f % 2 == 0 else j + 1
                va[xf, :, part] = e0s[xf, :, part] + ok * (0.75 * cy0[j, t] + 0.25 * cy0[other, t])
    relax(va, vb, 2, 38, 9, k0[...], lambda p, q: fr0 * r0s[p:q], side0)
    relax(vb, va, 3, 37, 9, k0[...], lambda p, q: fr0 * r0s[p:q], side0)
    total = jnp.zeros((32, 128), F32)
    last = m0[:, :128]
    for p, q in chunks(4, 36, 8):
        mid = va[p:q]
        flat = va[p:q, :, :128]
        near = (va[p + 1 : q + 1, :, :128] + va[p - 1 : q - 1, :, :128]) + (
            pltpu.roll(flat, 1, 1) + pltpu.roll(flat, 39, 1)
        )
        value = (r0s[p:q, :, :128] - times(mid, last) + S0 * near)[:, 4:36]
        res[p - 4 : q - 4] = value
        sol[p - 4 : q - 4] = va[p:q, 4:36, :128]
        total = total + jnp.sum(value * value, axis=0)
    sum3 = jnp.sum(total)
    tile = rows((8, 128), 1)
    stat[...] = jnp.where(
        tile == 0, stat0[...], jnp.where(tile == 1, stat1[...], jnp.where(tile == 2, sum2, jnp.where(tile == 3, sum3, 0.0)))
    )


def shift(x, axis, k):
    n = lax.axis_size(axis)
    return lax.ppermute(x, axis, [((i + k) % n, i) for i in range(n)])


def swap(x, axes, sizes, flip):
    n = 1
    for s in sizes:
        n *= s
    return lax.ppermute(x, axes, [(i ^ flip, i) for i in range(n)])


def f32(*shape):
    return jax.ShapeDtypeStruct(shape, F32)


def bf16(*shape):
    return jax.ShapeDtypeStruct(shape, BF16)


def scratch(*shape):
    return pltpu.VMEM(shape, F32)


def call(kernel, outs, scratches, n_in, name, scalars=True):
    specs = [pl.BlockSpec(memory_space=pltpu.SMEM)] if scalars else []
    specs += [pl.BlockSpec(memory_space=pltpu.VMEM)] * n_in
    return pl.pallas_call(
        kernel,
        out_shape=outs,
        in_specs=specs,
        out_specs=[pl.BlockSpec(memory_space=pltpu.VMEM)] * len(outs),
        scratch_shapes=scratches,
        compiler_params=pltpu.CompilerParams(vmem_limit_bytes=VMEM_LIMIT),
        name=name,
    )


def coarsen(w):
    return 0.5 * (w[:, 0::2] + w[:, 1::2])


def pack(width, reach, count, n, height, groups, parts, name):
    def kernel(*refs):
        pack_kernel(width, reach, count, n, *refs)

    outs = [f32(n + 2 * reach, height, 128), f32(groups, height, 128), f32(groups, height, 128)]
    return call(kernel, outs, [], 5, name, scalars=False)(*parts)


def sides(block, reach):
    n = block.shape[0]
    xlo = shift(block[n - reach :], "gx", -1)
    xhi = shift(block[:reach], "gx", 1)
    top = jnp.concatenate([xlo[:, n - reach :], block[:, n - reach :], xhi[:, n - reach :]], axis=0)
    bottom = jnp.concatenate([xlo[:, :reach], block[:, :reach], xhi[:, :reach]], axis=0)
    return block, xlo, xhi, shift(top, "gy", -1), shift(bottom, "gy", 1)


def body(data, weights):
    pos = jnp.stack([lax.axis_index("gx"), lax.axis_index("gy"), lax.axis_index("gz")]).astype(jnp.int32)
    w1 = coarsen(weights)
    w2 = coarsen(w1)
    both = jnp.concatenate([weights, w1], axis=1)
    wl, wr = shift(both, "gz", -1), shift(both, "gz", 1)
    wide0 = jnp.concatenate([weights, wr[:, :64], wl[:, 64:128]], axis=1)
    wide1 = jnp.concatenate([w1, wr[:, 128:], wl[:, 128:], wl[:, 128:]], axis=1)
    b0, k0, m0, f0, k1, m1, f1 = call(
        weights_kernel,
        [bf16(768, 256), bf16(768, 256), bf16(768, 256), f32(8, 256), bf16(768, 128), bf16(384, 128), f32(8, 256)],
        [], 2, "weights_fine",
    )(pos, wide0, wide1)
    dxy, to_left, to_right = pack(36, H0, 128, 32, 40, 14, sides(data, H0), "pack_data")
    from_right, from_left = shift(to_left, "gz", 1), shift(to_right, "gz", -1)
    big = (40, 40, 256)
    r1, e0s, r0s, stat0 = call(
        down_0_kernel,
        [f32(16, 16, 64), f32(*big), f32(*big), f32(8, 128)],
        [scratch(*big), scratch(*big), scratch(*big), scratch(*big), scratch(16, 2, 40, 128)],
        7, "down_0",
    )(pos, dxy, from_right, from_left, b0, k0, m0, f0)
    rxy, to_left, to_right = pack(37, H1, 64, 16, 32, 9, sides(r1, H1), "pack_r1")
    from_right, from_left = shift(to_left, "gz", 1), shift(to_right, "gz", -1)
    mid = (26, 32, 128)
    msg, e1s, r1s, stat1 = call(
        down_1_kernel,
        [f32(9, 8, 32), f32(*mid), f32(*mid), f32(8, 128)],
        [scratch(*mid), scratch(*mid), scratch(*mid), scratch(*mid), scratch(8, 32, 128)],
        7, "down_1",
    )(pos, rxy, from_right, from_left, k1, m1, f1, w2)
    near = {k: shift(msg, "gz", k) for k in (1, -1, 2, -2, 3, -3)}
    wide = jnp.concatenate([msg, near[1], near[2], near[3], jnp.zeros_like(msg), near[-3], near[-2], near[-1]], axis=2)
    wide2 = wide[8]
    k2, k2u, m2, f2, k3, f3 = call(
        weights_2_kernel,
        [bf16(768, 256), bf16(384, 128), bf16(768, 256), f32(8, 256), bf16(384, 128), f32(8, 128)],
        [], 2, "weights_coarse",
    )(pos, wide2, coarsen(wide2))
    r2z = wide[:8]
    x1, x2, x3 = (shift(r2z, "gx", k) for k in (1, 2, 3))
    r2x = jnp.concatenate([x2[5:], x3, r2z, x1, x2[:3]], axis=0)
    ya, yb = shift(r2x, "gy", -1), shift(r2x, "gy", 1)
    yc, yd = shift(r2x[:, 5:], "gy", -2), shift(r2x[:, :3], "gy", 2)
    k1u = jnp.concatenate([k1[:128], k1[256:384], k1[512:640]], axis=0)
    lev2 = (30, 32, 256)
    sol, res, stat = call(
        up_kernel,
        [f32(32, 32, 128), f32(32, 32, 128), f32(8, 128)],
        [
            scratch(*lev2), scratch(*lev2), scratch(*lev2), scratch(*lev2), scratch(12, 2, 40, 128),
            scratch(14, 32, 128), scratch(12, 16, 128), scratch(12, 16, 128), scratch(12, 16, 128),
            scratch(12, 32, 128), scratch(*mid), scratch(*mid), scratch(*mid), scratch(14, 32, 128),
            scratch(*big), scratch(*big), scratch(*big), scratch(20, 2, 40, 128),
        ],
        22, "up",
    )(pos, r2x, ya, yb, yc, yd, k2, k2u, m2, f2, k3, f3, k1u, f1, e1s, r1s, k0, m0, f0, e0s, r0s, stat0, stat1)
    t = stat[:1]
    for axes, sizes, flips in (
        ("gx", (4,), (1, 2, 3)),
        ("gy", (8,), (2, 4, 6)),
        (("gy", "gz"), (8, 8), (1, 8, 9)),
        ("gz", (8,), (2, 4, 6)),
    ):
        a, b, c = (swap(t, axes, sizes, f) for f in flips)
        t = (t + a) + (b + c)
    cells = jnp.array([NX * NY * NZ >> (3 * k) for k in (0, 1, 2, 0)], F32)
    return sol, res, jnp.sqrt(t[0, :4] / cells)


def solution(mesh):
    placed = (P("gx", "gy", "gz"), P(None, "gz"))
    return jax.shard_map(
        body,
        mesh=mesh,
        in_specs=placed,
        out_specs=(P("gx", "gy", "gz"), P("gx", "gy", "gz"), P()),
        check_vma=False,
    )
```

time: 807 us -> 146 us (0.18)
  the two profiles are of different devices: /device:TPU:32 before, /device:TPU:10 now
where the time goes in v1:
time: 146 us; the launch traced here: 145 us
  starting transfers between devices  53.3 us (37%)
  waiting for transfers between devices  45.5 us (31%)
  Pallas kernels  28.2 us (19%)
  local copies, waits for them, and re-layouts  12.4 us (8%)
  other arithmetic  5.1 us (3%)
    ppermute x27, starting transfers between devices, shift(): return lax.ppermute(x, axis, [((i + k) % n, i) for i in range(n)])  35.7 us
    ppermute x27, waiting for transfers between devices, shift(): return lax.ppermute(x, axis, [((i + k) % n, i) for i in range(n)])  32 us
    ppermute x12, starting transfers between devices, swap(): return lax.ppermute(x, axes, [(i ^ flip, i) for i in range(n)])  17.6 us
    ppermute x12, waiting for transfers between devices, swap(): return lax.ppermute(x, axes, [(i ^ flip, i) for i in range(n)])  13.5 us
    pallas_call x1, Pallas kernels, body(): call(up_kernel, [f32(32, 32, 128), f32(32, 32, 128), f32(8, 128)], [scrat...  10.1 us
    pallas_call x1, Pallas kernels, body(): call(down_0_kernel, [f32(16, 16, 64), f32(*big), f32(*big), f32(8, 128)],...  5.5 us
    unnamed x46, local copies, waits for them, and re-layouts  4.77 us
    pallas_call x2, Pallas kernels, pack(): return call(kernel, outs, [], 5, name, scalars=False)(*parts)  4.51 us
  transfers between devices with their start and end apart: 39, of which 23 were waited for; matrix products, arithmetic and copies ran while one was open for 5% of the time, Pallas kernels for 5%

profile of v1, /device:TPU:10, one launch (start us, length us, event | category | flops | bytes accessed | tf_op | source)
XLA Modules:
  0.0 145.5 jit_solution(920274702039821934)
XLA Ops:
  3.1 1.9 %collective-permute-start.7 = (f32[8,192]{1,0:T(8,128)S(1)}, f32[8,192]{1,0:T(8,128)S(1)}, u32[]{:S(2)}, u32[]{:S(2)}) collective-permute-start(f32[8,192]{1,0:T(8,128)S(1)} %pad_maximum_fusion.5), channel_id=1, source_target_pairs={{7,0},{0,1},{1,2},{2,3},{3,4},{4,5},{5,6},{6,7},{15,8},{8,9},{9,10... | collective-permute-start | bytes 18440 | tf_op jit(solution)/shard_map/ppermute | solution.py:440
  5.0 3.9 %collective-permute-start.6 = (f32[8,192]{1,0:T(8,128)S(1)}, f32[8,192]{1,0:T(8,128)S(1)}, u32[]{:S(2)}, u32[]{:S(2)}) collective-permute-start(f32[8,192]{1,0:T(8,128)S(1)} %pad_maximum_fusion.5), channel_id=1, source_target_pairs={{1,0},{2,1},{3,2},{4,3},{5,4},{6,5},{7,6},{0,7},{9,8},{10,9},{11,1... | collective-permute-start | bytes 18440 | tf_op jit(solution)/shard_map/ppermute | solution.py:440
  17.5 2.0 %collective-permute-done.2.refs_3_ = f32[40,4,128]{2,1,0:T(4,128)S(1)} collective-permute-done((f32[40,4,128]{2,1,0:T(4,128)S(1)}, f32[40,4,128]{2,1,0:T(4,128)S(1)}, u32[]{:S(2)}, u32[]{:S(2)}) %collective-permute-start.2) | collective-permute-done | bytes 81952 | tf_op jit(solution)/shard_map/ppermute | solution.py:440
  20.8 2.5 %pack_data.1 = (f32[40,40,128]{2,1,0:T(8,128)}, f32[14,40,128]{2,1,0:T(8,128)}, f32[14,40,128]{2,1,0:T(8,128)}) custom-call(f32[32,32,128]{2,1,0:T(8,128)} %refs_0_.1, f32[4,32,128]{2,1,0:T(8,128)} %copy-done.15, f32[4,32,128]{2,1,0:T(8,128)} %copy-done.14, f32[40,4,128]{2,1,0:T(4,128)} %copy-done.16, f32[40,4,128]{2,1,0:T(4,128)} %copy-done.17), custom_call_target="tpu_custom_call" | custom-call | tf_op jit(solution)/shard_map/pack_data/pallas_call | solution.py:485
  23.3 2.0 %collective-permute-start.4 = (f32[14,40,128]{2,1,0:T(8,128)}, f32[14,40,128]{2,1,0:T(8,128)S(1)}, u32[]{:S(2)}, u32[]{:S(2)}) collective-permute-start(f32[14,40,128]{2,1,0:T(8,128)} %get-tuple-element.34), channel_id=1, source_target_pairs={{1,0},{2,1},{3,2},{4,3},{5,4},{6,5},{7,6},{0,7},{9,8},{10,9},{11,1... | collective-permute-start | bytes 860168 | tf_op jit(solution)/shard_map/ppermute | solution.py:440
  26.0 2.6 %weights_fine.1 = (bf16[768,256]{1,0:T(8,128)(2,1)}, bf16[768,256]{1,0:T(8,128)(2,1)}, bf16[768,256]{1,0:T(8,128)(2,1)}, f32[8,256]{1,0:T(8,128)}, bf16[768,128]...) custom-call(s32[3]{0:T(128)} %pad_add_fusion.pos, f32[8,256]{1,0:T(8,128)} %get-tuple-element.88.w0, ...), custom_call_target="tpu_custom_call" | custom-call | tf_op jit(solution)/shard_map/weights_fine/pallas_call | solution.py:505
  28.7 4.5 %collective-permute-done.4.from_right = f32[14,40,128]{2,1,0:T(8,128)S(1)} collective-permute-done((f32[14,40,128]{2,1,0:T(8,128)}, f32[14,40,128]{2,1,0:T(8,128)S(1)}, u32[]{:S(2)}, u32[]{:S(2)}) %collective-permute-start.4) | collective-permute-done | bytes 286752 | tf_op jit(solution)/shard_map/ppermute | solution.py:440
  33.2 3.0 %collective-permute-done.5.from_left = f32[14,40,128]{2,1,0:T(8,128)S(1)} collective-permute-done((f32[14,40,128]{2,1,0:T(8,128)}, f32[14,40,128]{2,1,0:T(8,128)S(1)}, u32[]{:S(2)}, u32[]{:S(2)}) %collective-permute-start.5) | collective-permute-done | bytes 286752 | tf_op jit(solution)/shard_map/ppermute | solution.py:440
  36.9 5.5 %down_0.1 = (f32[16,16,64]{2,1,0:T(8,128)}, f32[40,40,256]{2,1,0:T(8,128)}, f32[40,40,256]{2,1,0:T(8,128)}, f32[8,128]{1,0:T(8,128)}) custom-call(s32[3]{0:T(128)} %pad_add_fusion.pos, f32[40,40,128]{2,1,0:T(8,128)} %get-tuple-element.33.dxy, f32[14,40,128]{2,1,0:T(8,128)} %copy-done.2, f32[14,40,128]{2,1,0:T(8,128)} %copy-done.3, ...), custom_call_target="tpu_custom_call" | custom-call | tf_op jit(solution)/shard_map/down_0/pallas_call | solution.py:513
  43.3 3.2 %collective-permute-start.9 = (f32[5,16,64]{2,1,0:T(8,128)S(1)}, f32[5,16,64]{2,1,0:T(8,128)S(1)}, u32[]{:S(2)}, u32[]{:S(2)}) collective-permute-start(f32[5,16,64]{2,1,0:T(8,128)S(1)} %get-tuple-element.74), channel_id=1, source_target_pairs={{64,0},{128,64},{192,128},{0,192},{65,1},{129,65},{193,129},{1,193... | collective-permute-start | bytes 61448 | tf_op jit(solution)/shard_map/ppermute | solution.py:440
  48.2 3.3 %collective-permute-done.8.refs_1_ = f32[5,16,64]{2,1,0:T(8,128)S(1)} collective-permute-done((f32[5,16,64]{2,1,0:T(8,128)S(1)}, f32[5,16,64]{2,1,0:T(8,128)S(1)}, u32[]{:S(2)}, u32[]{:S(2)}) %collective-permute-start.8) | collective-permute-done | bytes 20512 | tf_op jit(solution)/shard_map/ppermute | solution.py:440
  53.5 2.1 %collective-permute-done.10.refs_3_ = f32[26,5,64]{2,1,0:T(8,128)S(1)} collective-permute-done((f32[26,5,64]{2,1,0:T(8,128)S(1)}, f32[26,5,64]{2,1,0:T(8,128)S(1)}, u32[]{:S(2)}, u32[]{:S(2)}) %collective-permute-start.10) | collective-permute-done | bytes 33312 | tf_op jit(solution)/shard_map/ppermute | solution.py:440
  56.9 2.0 %pack_r1.1 = (f32[26,32,128]{2,1,0:T(8,128)}, f32[9,32,128]{2,1,0:T(8,128)}, f32[9,32,128]{2,1,0:T(8,128)}) custom-call(f32[16,16,64]{2,1,0:T(8,128)} %get-tuple-element.40.refs_0_, f32[5,16,64]{2,1,0:T(8,128)} %copy-done.7, f32[5,16,64]{2,1,0:T(8,128)} %copy-done.6, f32[26,5,64]{2,1,0:T(8,128)} %copy-done.12, f32[26,5,64]{2,1,0:T(8,128)} %copy-done.13), custom_call_target="tpu_custom_call" | custom-call | tf_op jit(solution)/shard_map/pack_r1/pallas_call | solution.py:485
  61.5 4.1 %collective-permute-done.12.from_right = f32[9,32,128]{2,1,0:T(8,128)S(1)} collective-permute-done((f32[9,32,128]{2,1,0:T(8,128)}, f32[9,32,128]{2,1,0:T(8,128)S(1)}, u32[]{:S(2)}, u32[]{:S(2)}) %collective-permute-start.12) | collective-permute-done | bytes 147488 | tf_op jit(solution)/shard_map/ppermute | solution.py:440
  67.5 3.1 %down_1.1 = (f32[9,8,32]{2,1,0:T(8,128)}, f32[26,32,128]{2,1,0:T(8,128)}, f32[26,32,128]{2,1,0:T(8,128)}, f32[8,128]{1,0:T(8,128)}) custom-call(s32[3]{0:T(128)} %pad_add_fusion.pos, f32[26,32,128]{2,1,0:T(8,128)} %get-tuple-element.41.rxy, f32[9,32,128]{2,1,0:T(8,128)} %copy-done.8, f32[9,32,128]{2,1,0:T(8,128)} %copy-done.9, ...), custom_call_target="tpu_custom_call" | custom-call | tf_op jit(solution)/shard_map/down_1/pallas_call | solution.py:522
  71.4 3.1 %collective-permute-start.17 = (f32[9,8,32]{2,1,0:T(8,128)}, f32[9,8,32]{2,1,0:T(8,128)S(1)}, u32[]{:S(2)}, u32[]{:S(2)}) collective-permute-start(f32[9,8,32]{2,1,0:T(8,128)} %get-tuple-element.47), channel_id=1, source_target_pairs={{5,0},{6,1},{7,2},{0,3},{1,4},{2,5},{3,6},{4,7},{13,8},{14,9},{15,... | collective-permute-start | bytes 27656 | tf_op jit(solution)/shard_map/ppermute | solution.py:440
  74.5 1.9 %collective-permute-start.16 = (f32[9,8,32]{2,1,0:T(8,128)}, f32[9,8,32]{2,1,0:T(8,128)S(1)}, u32[]{:S(2)}, u32[]{:S(2)}) collective-permute-start(f32[9,8,32]{2,1,0:T(8,128)} %get-tuple-element.47), channel_id=1, source_target_pairs={{3,0},{4,1},{5,2},{6,3},{7,4},{0,5},{1,6},{2,7},{11,8},{12,9},{13,... | collective-permute-start | bytes 27656 | tf_op jit(solution)/shard_map/ppermute | solution.py:440
  76.5 3.9 %collective-permute-start.15 = (f32[9,8,32]{2,1,0:T(8,128)}, f32[9,8,32]{2,1,0:T(8,128)S(1)}, u32[]{:S(2)}, u32[]{:S(2)}) collective-permute-start(f32[9,8,32]{2,1,0:T(8,128)} %get-tuple-element.47), channel_id=1, source_target_pairs={{2,0},{3,1},{4,2},{5,3},{6,4},{7,5},{0,6},{1,7},{10,8},{11,9},{12,... | collective-permute-start | bytes 27656 | tf_op jit(solution)/shard_map/ppermute | solution.py:440
  86.0 2.1 %collective-permute-start.22 = (f32[8,8,256]{2,1,0:T(8,128)S(1)}, f32[8,8,256]{2,1,0:T(8,128)S(1)}, u32[]{:S(2)}, u32[]{:S(2)}) collective-permute-start(f32[8,8,256]{2,1,0:T(8,128)S(1)} %slice.161), channel_id=1, source_target_pairs={{64,0},{128,64},{192,128},{0,192},{65,1},{129,65},{193,129},{1,193... | collective-permute-start | bytes 196616 | tf_op jit(solution)/shard_map/ppermute | solution.py:440
  88.8 2.6 %collective-permute-done.20 = f32[8,8,256]{2,1,0:T(8,128)S(1)} collective-permute-done((f32[8,8,256]{2,1,0:T(8,128)S(1)}, f32[8,8,256]{2,1,0:T(8,128)S(1)}, u32[]{:S(2)}, u32[]{:S(2)}) %collective-permute-start.20) | collective-permute-done | bytes 65568 | tf_op jit(solution)/shard_map/ppermute | solution.py:440
  96.3 2.4 %weights_coarse.1 = (bf16[768,256]{1,0:T(8,128)(2,1)}, bf16[384,128]{1,0:T(8,128)(2,1)}, bf16[768,256]{1,0:T(8,128)(2,1)}, f32[8,256]{1,0:T(8,128)}, bf16[384,128]{1,0:T(8,128)(2,1)}, /*index=5*/f32[8,128]{1,0:T(8,128)}) custom-call(s32[3]{0:T(128)} %pad_add_fusion.pos, f32[8,256]{1,0:T(8,128)} %copy-done.18, f32[8,128]{1,0:T(8,128)} %add_multiply_fusion.w3), custom_call_target="tpu_custom_call" | custom-call | tf_op jit(solution)/shard_map/weights_coarse/pallas_call | solution.py:531
  98.7 2.8 %collective-permute-done.26.yd = f32[30,3,256]{2,1,0:T(4,128)S(1)} collective-permute-done((f32[30,3,256]{2,1,0:T(4,128)S(1)}, f32[30,3,256]{2,1,0:T(4,128)S(1)}, u32[]{:S(2)}, u32[]{:S(2)}) %collective-permute-start.26) | collective-permute-done | bytes 92192 | tf_op jit(solution)/shard_map/ppermute | solution.py:440
  102.4 10.1 %up.1 = (f32[32,32,128]{2,1,0:T(8,128)}, f32[32,32,128]{2,1,0:T(8,128)}, f32[8,128]{1,0:T(8,128)}) custom-call(s32[3]{0:T(128)} %pad_add_fusion.pos, f32[30,8,256]{2,1,0:T(8,128)} %copy-done, f32[30,8,256]{2,1,0:T(8,128)} %copy-done.5, f32[30,8,256]{2,1,0:T(8,128)} %copy-done.4, f32[30,3,256]{2,1,0:T(4,128)} %copy-done.11, f32[30,3,256]{2,1,0:T(4,128)} %copy-done.10, ...), custom_call_target="tpu_custom_call" | custom-call | tf_op jit(solution)/shard_map/up/pallas_call | solution.py:543
  113.2 2.0 %collective-permute-start.28 = (f32[1,128]{1,0:T(1,128)S(1)}, f32[1,128]{1,0:T(1,128)S(1)}, u32[]{:S(2)}, u32[]{:S(2)}) collective-permute-start(f32[1,128]{1,0:T(1,128)S(1)} %slice.147), channel_id=1, source_target_pairs={{128,0},{192,64},{0,128},{64,192},{129,1},{193,65},{1,129},{65,193... | collective-permute-start | bytes 1544 | tf_op jit(solution)/shard_map/ppermute | solution.py:447
  115.2 2.7 %collective-permute-start.29 = (f32[1,128]{1,0:T(1,128)S(1)}, f32[1,128]{1,0:T(1,128)S(1)}, u32[]{:S(2)}, u32[]{:S(2)}) collective-permute-start(f32[1,128]{1,0:T(1,128)S(1)} %slice.147), channel_id=1, source_target_pairs={{192,0},{128,64},{64,128},{0,192},{193,1},{129,65},{65,129},{1,193... | collective-permute-start | bytes 1544 | tf_op jit(solution)/shard_map/ppermute | solution.py:447
  119.4 2.0 %collective-permute-done.27 = f32[1,128]{1,0:T(1,128)S(1)} collective-permute-done((f32[1,128]{1,0:T(1,128)S(1)}, f32[1,128]{1,0:T(1,128)S(1)}, u32[]{:S(2)}, u32[]{:S(2)}) %collective-permute-start.27) | collective-permute-done | bytes 544 | tf_op jit(solution)/shard_map/ppermute | solution.py:447
  123.6 2.6 %collective-permute-start.31 = (f32[1,128]{1,0:T(1,128)S(1)}, f32[1,128]{1,0:T(1,128)S(1)}, u32[]{:S(2)}, u32[]{:S(2)}) collective-permute-start(f32[1,128]{1,0:T(1,128)S(1)} %add_add_fusion.3), channel_id=1, source_target_pairs={{32,0},{40,8},{48,16},{56,24},{0,32},{8,40},{16,48},{24,56},{33,1}... | collective-permute-start | bytes 1544 | tf_op jit(solution)/shard_map/ppermute | solution.py:447
  126.2 2.4 %collective-permute-done.31 = f32[1,128]{1,0:T(1,128)S(1)} collective-permute-done((f32[1,128]{1,0:T(1,128)S(1)}, f32[1,128]{1,0:T(1,128)S(1)}, u32[]{:S(2)}, u32[]{:S(2)}) %collective-permute-start.31) | collective-permute-done | bytes 544 | tf_op jit(solution)/shard_map/ppermute | solution.py:447
  130.1 1.8 %collective-permute-start.33 = (f32[1,128]{1,0:T(1,128)S(1)}, f32[1,128]{1,0:T(1,128)S(1)}, u32[]{:S(2)}, u32[]{:S(2)}) collective-permute-start(f32[1,128]{1,0:T(1,128)S(1)} %add_add_fusion.2), channel_id=1, source_target_pairs={{1,0},{0,1},{3,2},{2,3},{5,4},{4,5},{7,6},{6,7},{9,8},{8,9},{11,10... | collective-permute-start | bytes 1544 | tf_op jit(solution)/shard_map/ppermute | solution.py:447
  133.6 3.8 %collective-permute-start.38 = (f32[1,128]{1,0:T(1,128)S(1)}, f32[1,128]{1,0:T(1,128)S(1)}, u32[]{:S(2)}, u32[]{:S(2)}) collective-permute-start(f32[1,128]{1,0:T(1,128)S(1)} %add_add_fusion.1), channel_id=1, source_target_pairs={{6,0},{7,1},{4,2},{5,3},{2,4},{3,5},{0,6},{1,7},{14,8},{15,9},{12,... | collective-permute-start | bytes 1544 | tf_op jit(solution)/shard_map/ppermute | solution.py:447
  137.5 2.8 %collective-permute-start.37 = (f32[1,128]{1,0:T(1,128)S(1)}, f32[1,128]{1,0:T(1,128)S(1)}, u32[]{:S(2)}, u32[]{:S(2)}) collective-permute-start(f32[1,128]{1,0:T(1,128)S(1)} %add_add_fusion.1), channel_id=1, source_target_pairs={{4,0},{5,1},{6,2},{7,3},{0,4},{1,5},{2,6},{3,7},{12,8},{13,9},{14,... | collective-permute-start | bytes 1544 | tf_op jit(solution)/shard_map/ppermute | solution.py:447
  140.3 4.6 %collective-permute-done.37 = f32[1,128]{1,0:T(1,128)S(1)} collective-permute-done((f32[1,128]{1,0:T(1,128)S(1)}, f32[1,128]{1,0:T(1,128)S(1)}, u32[]{:S(2)}, u32[]{:S(2)}) %collective-permute-start.37) | collective-permute-done | bytes 544 | tf_op jit(solution)/shard_map/ppermute | solution.py:447
  (139 shorter events, 44.9 us)
Async XLA Ops:
  3.1 14.4 %collective-permute-start.7 = (f32[8,192]{1,0:T(8,128)S(1)}, f32[8,192]{1,0:T(8,128)S(1)}, u32[]{:S(2)}, u32[]{:S(2)}) collective-permute-start(f32[8,192]{1,0:T(8,128)S(1)} %pad_maximum_fusion.5), channel_id=1, source_target_pairs={{7,0},{0,1},{1,2},{2,3},{3,4},{4,5},{5,6},{6,7},{15,8},{8,9},{9,10... | collective-permute-start | bytes 18440 | tf_op jit(solution)/shard_map/ppermute | solution.py:440
  5.0 20.3 %collective-permute-start.6 = (f32[8,192]{1,0:T(8,128)S(1)}, f32[8,192]{1,0:T(8,128)S(1)}, u32[]{:S(2)}, u32[]{:S(2)}) collective-permute-start(f32[8,192]{1,0:T(8,128)S(1)} %pad_maximum_fusion.5), channel_id=1, source_target_pairs={{1,0},{2,1},{3,2},{4,3},{5,4},{6,5},{7,6},{0,7},{9,8},{10,9},{11,1... | collective-permute-start | bytes 18440 | tf_op jit(solution)/shard_map/ppermute | solution.py:440
  9.8 4.3 %collective-permute-start.1 = (f32[4,32,128]{2,1,0:T(8,128)S(1)}, f32[4,32,128]{2,1,0:T(8,128)S(1)}, u32[]{:S(2)}, u32[]{:S(2)}) collective-permute-start(f32[4,32,128]{2,1,0:T(8,128)S(1)} %get-tuple-element.65), channel_id=1, source_target_pairs={{64,0},{128,64},{192,128},{0,192},{65,1},{129,65},{193,129},{1,193... | collective-permute-start | bytes 196616 | tf_op jit(solution)/shard_map/ppermute | solution.py:440
  10.3 5.3 %collective-permute-start = (f32[4,32,128]{2,1,0:T(8,128)S(1)}, f32[4,32,128]{2,1,0:T(8,128)S(1)}, u32[]{:S(2)}, u32[]{:S(2)}) collective-permute-start(f32[4,32,128]{2,1,0:T(8,128)S(1)} %get-tuple-element.66), channel_id=1, source_target_pairs={{192,0},{0,64},{64,128},{128,192},{193,1},{1,65},{65,129},{129,193... | collective-permute-start | bytes 196616 | tf_op jit(solution)/shard_map/ppermute | solution.py:440
  23.3 9.9 %collective-permute-start.4 = (f32[14,40,128]{2,1,0:T(8,128)}, f32[14,40,128]{2,1,0:T(8,128)S(1)}, u32[]{:S(2)}, u32[]{:S(2)}) collective-permute-start(f32[14,40,128]{2,1,0:T(8,128)} %get-tuple-element.34), channel_id=1, source_target_pairs={{1,0},{2,1},{3,2},{4,3},{5,4},{6,5},{7,6},{0,7},{9,8},{10,9},{11,1... | collective-permute-start | bytes 860168 | tf_op jit(solution)/shard_map/ppermute | solution.py:440
  25.3 10.9 %collective-permute-start.5 = (f32[14,40,128]{2,1,0:T(8,128)}, f32[14,40,128]{2,1,0:T(8,128)S(1)}, u32[]{:S(2)}, u32[]{:S(2)}) collective-permute-start(f32[14,40,128]{2,1,0:T(8,128)} %get-tuple-element.35), channel_id=1, source_target_pairs={{7,0},{0,1},{1,2},{2,3},{3,4},{4,5},{5,6},{6,7},{15,8},{8,9},{9,10... | collective-permute-start | bytes 860168 | tf_op jit(solution)/shard_map/ppermute | solution.py:440
  43.3 4.9 %collective-permute-start.9 = (f32[5,16,64]{2,1,0:T(8,128)S(1)}, f32[5,16,64]{2,1,0:T(8,128)S(1)}, u32[]{:S(2)}, u32[]{:S(2)}) collective-permute-start(f32[5,16,64]{2,1,0:T(8,128)S(1)} %get-tuple-element.74), channel_id=1, source_target_pairs={{64,0},{128,64},{192,128},{0,192},{65,1},{129,65},{193,129},{1,193... | collective-permute-start | bytes 61448 | tf_op jit(solution)/shard_map/ppermute | solution.py:440
  47.4 4.1 %collective-permute-start.8 = (f32[5,16,64]{2,1,0:T(8,128)S(1)}, f32[5,16,64]{2,1,0:T(8,128)S(1)}, u32[]{:S(2)}, u32[]{:S(2)}) collective-permute-start(f32[5,16,64]{2,1,0:T(8,128)S(1)} %get-tuple-element.75), channel_id=1, source_target_pairs={{192,0},{0,64},{64,128},{128,192},{193,1},{1,65},{65,129},{129,193... | collective-permute-start | bytes 61448 | tf_op jit(solution)/shard_map/ppermute | solution.py:440
  51.5 4.1 %collective-permute-start.10 = (f32[26,5,64]{2,1,0:T(8,128)S(1)}, f32[26,5,64]{2,1,0:T(8,128)S(1)}, u32[]{:S(2)}, u32[]{:S(2)}) collective-permute-start(f32[26,5,64]{2,1,0:T(8,128)S(1)} %pad_maximum_fusion), channel_id=1, source_target_pairs={{56,0},{0,8},{8,16},{16,24},{24,32},{32,40},{40,48},{48,56},{57,1}... | collective-permute-start | bytes 99848 | tf_op jit(solution)/shard_map/ppermute | solution.py:440
  51.5 4.1 %collective-permute-start.11 = (f32[26,5,64]{2,1,0:T(8,128)S(1)}, f32[26,5,64]{2,1,0:T(8,128)S(1)}, u32[]{:S(2)}, u32[]{:S(2)}) collective-permute-start(f32[26,5,64]{2,1,0:T(8,128)S(1)} %pad_maximum_fusion.1), channel_id=1, source_target_pairs={{8,0},{16,8},{24,16},{32,24},{40,32},{48,40},{56,48},{0,56},{9,1},... | collective-permute-start | bytes 99848 | tf_op jit(solution)/shard_map/ppermute | solution.py:440
  58.9 6.7 %collective-permute-start.12 = (f32[9,32,128]{2,1,0:T(8,128)}, f32[9,32,128]{2,1,0:T(8,128)S(1)}, u32[]{:S(2)}, u32[]{:S(2)}) collective-permute-start(f32[9,32,128]{2,1,0:T(8,128)} %get-tuple-element.42), channel_id=1, source_target_pairs={{1,0},{2,1},{3,2},{4,3},{5,4},{6,5},{7,6},{0,7},{9,8},{10,9},{11,1... | collective-permute-start | bytes 442376 | tf_op jit(solution)/shard_map/ppermute | solution.py:440
  59.2 7.7 %collective-permute-start.13 = (f32[9,32,128]{2,1,0:T(8,128)}, f32[9,32,128]{2,1,0:T(8,128)S(1)}, u32[]{:S(2)}, u32[]{:S(2)}) collective-permute-start(f32[9,32,128]{2,1,0:T(8,128)} %get-tuple-element.43), channel_id=1, source_target_pairs={{7,0},{0,1},{1,2},{2,3},{3,4},{4,5},{5,6},{6,7},{15,8},{8,9},{9,10... | collective-permute-start | bytes 442376 | tf_op jit(solution)/shard_map/ppermute | solution.py:440
  70.6 9.7 %collective-permute-start.19 = (f32[9,8,32]{2,1,0:T(8,128)}, f32[9,8,32]{2,1,0:T(8,128)S(1)}, u32[]{:S(2)}, u32[]{:S(2)}) collective-permute-start(f32[9,8,32]{2,1,0:T(8,128)} %get-tuple-element.47), channel_id=1, source_target_pairs={{7,0},{0,1},{1,2},{2,3},{3,4},{4,5},{5,6},{6,7},{15,8},{8,9},{9,10... | collective-permute-start | bytes 27656 | tf_op jit(solution)/shard_map/ppermute | solution.py:440
  71.1 11.5 %collective-permute-start.18 = (f32[9,8,32]{2,1,0:T(8,128)}, f32[9,8,32]{2,1,0:T(8,128)S(1)}, u32[]{:S(2)}, u32[]{:S(2)}) collective-permute-start(f32[9,8,32]{2,1,0:T(8,128)} %get-tuple-element.47), channel_id=1, source_target_pairs={{6,0},{7,1},{0,2},{1,3},{2,4},{3,5},{4,6},{5,7},{14,8},{15,9},{8,1... | collective-permute-start | bytes 27656 | tf_op jit(solution)/shard_map/ppermute | solution.py:440
  71.4 11.2 %collective-permute-start.17 = (f32[9,8,32]{2,1,0:T(8,128)}, f32[9,8,32]{2,1,0:T(8,128)S(1)}, u32[]{:S(2)}, u32[]{:S(2)}) collective-permute-start(f32[9,8,32]{2,1,0:T(8,128)} %get-tuple-element.47), channel_id=1, source_target_pairs={{5,0},{6,1},{7,2},{0,3},{1,4},{2,5},{3,6},{4,7},{13,8},{14,9},{15,... | collective-permute-start | bytes 27656 | tf_op jit(solution)/shard_map/ppermute | solution.py:440
  74.5 8.0 %collective-permute-start.16 = (f32[9,8,32]{2,1,0:T(8,128)}, f32[9,8,32]{2,1,0:T(8,128)S(1)}, u32[]{:S(2)}, u32[]{:S(2)}) collective-permute-start(f32[9,8,32]{2,1,0:T(8,128)} %get-tuple-element.47), channel_id=1, source_target_pairs={{3,0},{4,1},{5,2},{6,3},{7,4},{0,5},{1,6},{2,7},{11,8},{12,9},{13,... | collective-permute-start | bytes 27656 | tf_op jit(solution)/shard_map/ppermute | solution.py:440
  76.5 6.4 %collective-permute-start.15 = (f32[9,8,32]{2,1,0:T(8,128)}, f32[9,8,32]{2,1,0:T(8,128)S(1)}, u32[]{:S(2)}, u32[]{:S(2)}) collective-permute-start(f32[9,8,32]{2,1,0:T(8,128)} %get-tuple-element.47), channel_id=1, source_target_pairs={{2,0},{3,1},{4,2},{5,3},{6,4},{7,5},{0,6},{1,7},{10,8},{11,9},{12,... | collective-permute-start | bytes 27656 | tf_op jit(solution)/shard_map/ppermute | solution.py:440
  80.3 4.2 %collective-permute-start.14 = (f32[9,8,32]{2,1,0:T(8,128)}, f32[9,8,32]{2,1,0:T(8,128)S(1)}, u32[]{:S(2)}, u32[]{:S(2)}) collective-permute-start(f32[9,8,32]{2,1,0:T(8,128)} %get-tuple-element.47), channel_id=1, source_target_pairs={{1,0},{2,1},{3,2},{4,3},{5,4},{6,5},{7,6},{0,7},{9,8},{10,9},{11,1... | collective-permute-start | bytes 27656 | tf_op jit(solution)/shard_map/ppermute | solution.py:440
  85.4 6.0 %collective-permute-start.20 = (f32[8,8,256]{2,1,0:T(8,128)S(1)}, f32[8,8,256]{2,1,0:T(8,128)S(1)}, u32[]{:S(2)}, u32[]{:S(2)}) collective-permute-start(f32[8,8,256]{2,1,0:T(8,128)S(1)} %slice.161), channel_id=1, source_target_pairs={{128,0},{192,64},{0,128},{64,192},{129,1},{193,65},{1,129},{65,193... | collective-permute-start | bytes 196616 | tf_op jit(solution)/shard_map/ppermute | solution.py:440
  86.0 7.0 %collective-permute-start.22 = (f32[8,8,256]{2,1,0:T(8,128)S(1)}, f32[8,8,256]{2,1,0:T(8,128)S(1)}, u32[]{:S(2)}, u32[]{:S(2)}) collective-permute-start(f32[8,8,256]{2,1,0:T(8,128)S(1)} %slice.161), channel_id=1, source_target_pairs={{64,0},{128,64},{192,128},{0,192},{65,1},{129,65},{193,129},{1,193... | collective-permute-start | bytes 196616 | tf_op jit(solution)/shard_map/ppermute | solution.py:440
  88.1 4.9 %collective-permute-start.21 = (f32[8,8,256]{2,1,0:T(8,128)S(1)}, f32[8,8,256]{2,1,0:T(8,128)S(1)}, u32[]{:S(2)}, u32[]{:S(2)}) collective-permute-start(f32[8,8,256]{2,1,0:T(8,128)S(1)} %slice.161), channel_id=1, source_target_pairs={{192,0},{0,64},{64,128},{128,192},{193,1},{1,65},{65,129},{129,193... | collective-permute-start | bytes 196616 | tf_op jit(solution)/shard_map/ppermute | solution.py:440
  93.0 8.5 %collective-permute-start.24 = (f32[30,8,256]{2,1,0:T(8,128)S(1)}, f32[30,8,256]{2,1,0:T(8,128)S(1)}, u32[]{:S(2)}, u32[]{:S(2)}) collective-permute-start(f32[30,8,256]{2,1,0:T(8,128)S(1)} %slice_dynamic-update-slice_fusion.r2x), channel_id=1, source_target_pairs={{8,0},{16,8},{24,16},{32,24},{40,32},{48,40},{56,48},{0,56},{9,1},... | collective-permute-start | bytes 737288 | tf_op jit(solution)/shard_map/ppermute | solution.py:440
  93.0 8.5 %collective-permute-start.23 = (f32[30,8,256]{2,1,0:T(8,128)S(1)}, f32[30,8,256]{2,1,0:T(8,128)S(1)}, u32[]{:S(2)}, u32[]{:S(2)}) collective-permute-start(f32[30,8,256]{2,1,0:T(8,128)S(1)} %slice_dynamic-update-slice_fusion.r2x), channel_id=1, source_target_pairs={{56,0},{0,8},{8,16},{16,24},{24,32},{32,40},{40,48},{48,56},{57,1}... | collective-permute-start | bytes 737288 | tf_op jit(solution)/shard_map/ppermute | solution.py:440
  93.6 7.9 %collective-permute-start.26 = (f32[30,3,256]{2,1,0:T(4,128)S(1)}, f32[30,3,256]{2,1,0:T(4,128)S(1)}, u32[]{:S(2)}, u32[]{:S(2)}) collective-permute-start(f32[30,3,256]{2,1,0:T(4,128)S(1)} %get-tuple-element.67), channel_id=1, source_target_pairs={{16,0},{24,8},{32,16},{40,24},{48,32},{56,40},{0,48},{8,56},{17,1}... | collective-permute-start | bytes 276488 | tf_op jit(solution)/shard_map/ppermute | solution.py:440
  94.5 7.0 %collective-permute-start.25 = (f32[30,3,256]{2,1,0:T(4,128)S(1)}, f32[30,3,256]{2,1,0:T(4,128)S(1)}, u32[]{:S(2)}, u32[]{:S(2)}) collective-permute-start(f32[30,3,256]{2,1,0:T(4,128)S(1)} %get-tuple-element.68), channel_id=1, source_target_pairs={{48,0},{56,8},{0,16},{8,24},{16,32},{24,40},{32,48},{40,56},{49,1}... | collective-permute-start | bytes 276488 | tf_op jit(solution)/shard_map/ppermute | solution.py:440
  113.2 5.0 %collective-permute-start.28 = (f32[1,128]{1,0:T(1,128)S(1)}, f32[1,128]{1,0:T(1,128)S(1)}, u32[]{:S(2)}, u32[]{:S(2)}) collective-permute-start(f32[1,128]{1,0:T(1,128)S(1)} %slice.147), channel_id=1, source_target_pairs={{128,0},{192,64},{0,128},{64,192},{129,1},{193,65},{1,129},{65,193... | collective-permute-start | bytes 1544 | tf_op jit(solution)/shard_map/ppermute | solution.py:447
  115.2 4.2 %collective-permute-start.29 = (f32[1,128]{1,0:T(1,128)S(1)}, f32[1,128]{1,0:T(1,128)S(1)}, u32[]{:S(2)}, u32[]{:S(2)}) collective-permute-start(f32[1,128]{1,0:T(1,128)S(1)} %slice.147), channel_id=1, source_target_pairs={{192,0},{128,64},{64,128},{0,192},{193,1},{129,65},{65,129},{1,193... | collective-permute-start | bytes 1544 | tf_op jit(solution)/shard_map/ppermute | solution.py:447
  122.1 4.1 %collective-permute-start.32 = (f32[1,128]{1,0:T(1,128)S(1)}, f32[1,128]{1,0:T(1,128)S(1)}, u32[]{:S(2)}, u32[]{:S(2)}) collective-permute-start(f32[1,128]{1,0:T(1,128)S(1)} %add_add_fusion.3), channel_id=1, source_target_pairs={{48,0},{56,8},{32,16},{40,24},{16,32},{24,40},{0,48},{8,56},{49,1}... | collective-permute-start | bytes 1544 | tf_op jit(solution)/shard_map/ppermute | solution.py:447
  123.6 5.0 %collective-permute-start.31 = (f32[1,128]{1,0:T(1,128)S(1)}, f32[1,128]{1,0:T(1,128)S(1)}, u32[]{:S(2)}, u32[]{:S(2)}) collective-permute-start(f32[1,128]{1,0:T(1,128)S(1)} %add_add_fusion.3), channel_id=1, source_target_pairs={{32,0},{40,8},{48,16},{56,24},{0,32},{8,40},{16,48},{24,56},{33,1}... | collective-permute-start | bytes 1544 | tf_op jit(solution)/shard_map/ppermute | solution.py:447
  133.6 6.7 %collective-permute-start.38 = (f32[1,128]{1,0:T(1,128)S(1)}, f32[1,128]{1,0:T(1,128)S(1)}, u32[]{:S(2)}, u32[]{:S(2)}) collective-permute-start(f32[1,128]{1,0:T(1,128)S(1)} %add_add_fusion.1), channel_id=1, source_target_pairs={{6,0},{7,1},{4,2},{5,3},{2,4},{3,5},{0,6},{1,7},{14,8},{15,9},{12,... | collective-permute-start | bytes 1544 | tf_op jit(solution)/shard_map/ppermute | solution.py:447
  137.5 7.4 %collective-permute-start.37 = (f32[1,128]{1,0:T(1,128)S(1)}, f32[1,128]{1,0:T(1,128)S(1)}, u32[]{:S(2)}, u32[]{:S(2)}) collective-permute-start(f32[1,128]{1,0:T(1,128)S(1)} %add_add_fusion.1), channel_id=1, source_target_pairs={{4,0},{5,1},{6,2},{7,3},{0,4},{1,5},{2,6},{3,7},{12,8},{13,9},{14,... | collective-permute-start | bytes 1544 | tf_op jit(solution)/shard_map/ppermute | solution.py:447
  140.3 4.6 %collective-permute-start.36 = (f32[1,128]{1,0:T(1,128)S(1)}, f32[1,128]{1,0:T(1,128)S(1)}, u32[]{:S(2)}, u32[]{:S(2)}) collective-permute-start(f32[1,128]{1,0:T(1,128)S(1)} %add_add_fusion.1), channel_id=1, source_target_pairs={{2,0},{3,1},{0,2},{1,3},{6,4},{7,5},{4,6},{5,7},{10,8},{11,9},{8,1... | collective-permute-start | bytes 1544 | tf_op jit(solution)/shard_map/ppermute | solution.py:447
  (28 other events, 171.6 us)

commit v2 on v1

--- a/solution.py
+++ b/solution.py
@@ -12,7 +12,6 @@
 H0, H1, H2, H3 = 4, 5, 11, 4
 S0, S1, S2, S3 = 1.0, 0.25, 0.0625, 0.015625
 SLOT = 40
-VMEM_LIMIT = 56 * 2**20
 
 
 def place_0(p):
@@ -65,6 +64,10 @@
     hi, lo = halves(field.reshape(shape[0] * shape[1], shape[2]))
     out = jnp.dot(jnp.concatenate([hi, lo], axis=1), matrix, preferred_element_type=F32)
     return out.reshape(shape[0], shape[1], matrix.shape[1])
+
+
+def exact(a, b):
+    return jnp.dot(a, b, precision=lax.Precision.HIGHEST, preferred_element_type=F32)
 
 
 def operators(w, place, iz, level, reach, stiffness):
@@ -128,23 +131,37 @@
         dst[p:q] = times(mid, matrix) + right(p, q) + side[p:q] * near
 
 
-def weights_kernel(pos, w0, w1, b0, k0, m0, f0, k1, m1, f1):
-    iz = pos[2]
-    band, op, step, factor = operators(w0[...], place_0, iz, 0, 36, S0)
+def prepare_kernel(data, own, first, last, low, high):
+    own[...] = data[...]
+    first[...] = data[:H0]
+    last[...] = data[32 - H0 :]
+    low[...] = data[:, :H0]
+    high[...] = data[:, 32 - H0 :]
+
+
+def weights_0_kernel(left, own, right, b0, k0, m0, f0):
+    iz = lax.axis_index("gz")
+    lane = rows((8, 128), 1)
+    laid = jnp.concatenate([own[...], jnp.where(lane < 64, right[14, :8], left[14, :8])], axis=1)
+    band, op, step, factor = operators(laid, place_0, iz, 0, 36, S0)
     b0[...] = thrice(jnp.transpose(band))
     k0[...] = thrice(step)
     m0[...] = thrice(op)
     f0[...] = jnp.broadcast_to(factor, (8, 256))
-    lane = rows((8, 128), 1)
-    first, second = w1[:, :128], w1[:, 128:]
-    laid = jnp.concatenate([jnp.where(lane < 96, first, second), jnp.where(lane < 96, second, first)], axis=1)
-    band, op, step, factor = operators(laid, place_1, iz, 1, 41, S1)
+
+
+def weights_1_kernel(left, own, right, k1, k1u, m1, f1):
+    iz = lax.axis_index("gz")
+    wide = jnp.concatenate([left[14, :8], own[...], right[14, :8]], axis=1)
+    mean = jnp.where((rows((384, 256), 0) - 128) >> 1 == place_1(rows((384, 256), 1)), 0.5, 0.0)
+    band, op, step, factor = operators(exact(wide, mean), place_1, iz, 1, 41, S1)
     k1[...] = thrice(step[:, :128])
+    k1u[...] = thrice(step[:128, :128])
     m1[...] = thrice(op[:128, :128])
     f1[...] = jnp.broadcast_to(factor, (8, 256))
 
 
-def pack_kernel(width, reach, count, n, data, xlo, xhi, ylo, yhi, full, to_left, to_right):
+def pack_kernel(width, reach, count, n, data, xlo, xhi, ylo, yhi, extra, full, to_left, to_right):
     def plane(p):
         if p >= n + 2 * reach:
             return jnp.zeros(full.shape[1:], F32)
@@ -164,7 +181,13 @@
         return out
 
     lane = rows(full.shape[1:], 1)
-    for g in range(to_left.shape[0]):
+    groups = to_left.shape[0]
+    if extra is not None:
+        groups -= 1
+        for out in (to_left, to_right):
+            out[groups] = jnp.zeros(full.shape[1:], F32)
+            out[groups, :8] = extra[...]
+    for g in range(groups):
         left, right = None, None
         for i in range(3):
             p = 3 * g + i
@@ -179,12 +202,11 @@
         to_right[g] = right
 
 
-def down_0_kernel(pos, dxy, from_right, from_left, b0, k0, m0, f0, r1, e_out, r_out, stat, d, e0, side, g, gx):
-    ix, iy, iz = pos[0], pos[1], pos[2]
+def down_0_kernel(dxy, from_right, from_left, b0, k0, m0, f0, r1, r1_top, r1_bottom, e_out, r_out, stat, d, e0, side, g, gx):
+    ix, iy, iz = lax.axis_index("gx"), lax.axis_index("gy"), lax.axis_index("gz")
     lane = rows((40, 128), 1)
     for p in range(40):
         group, i = divmod(p, 3)
-        mask = plane_mask((1, 40, 128), 0, ix, iy, H0) if False else None
         xr = ix * 32 + p - H0
         y = iy * 32 + rows((40, 128), 0) - H0
         ok = jnp.where((y >= 0) & (y < NY), jnp.where((xr >= 0) & (xr < NX), 1.0, 0.0), 0.0)
@@ -224,11 +246,14 @@
     ]
     gy = ((gy[0] + gy[3]) + 3.0 * (gy[1] + gy[2])) * 0.125
     fold = restrict_matrix(place_0, 256, lambda q: q, 128, iz, 0, 36)
-    r1[...] = times_exact(gy, fold)[:, :, :64]
-
-
-def down_1_kernel(pos, rxy, from_right, from_left, k1, m1, f1, w2, msg, e_out, r_out, stat, e0, e0b, side, g, gx):
-    ix, iy, iz = pos[0], pos[1], pos[2]
+    out = times_exact(gy, fold)[:, :, :64]
+    r1[...] = out
+    r1_top[...] = out[:, 16 - H1 :]
+    r1_bottom[...] = out[:, :H1]
+
+
+def down_1_kernel(rxy, from_right, from_left, k1, m1, f1, w, msg, e_out, r_out, stat, e0, e0b, side, g, gx):
+    ix, iy, iz = lax.axis_index("gx"), lax.axis_index("gy"), lax.axis_index("gz")
     lane = rows((32, 128), 1)
     for p in range(26):
         group, i = divmod(p, 3)
@@ -273,31 +298,41 @@
     gy = ((gy[0] + gy[3]) + 3.0 * (gy[1] + gy[2])) * 0.125
     fold = restrict_matrix(place_1, 128, lambda q: q, 128, iz, 1, 32)
     msg[:8] = times_exact(gy, fold)[:, :, :32]
-    msg[8] = w2[...]
-
-
-def weights_2_kernel(pos, w2, w3, k2, k2u, m2, f2, k3, f3):
-    iz = pos[2]
-    lane = rows((8, 128), 1)
-    first, second = w2[:, :128], w2[:, 128:]
-    laid = jnp.concatenate([jnp.where(lane < 80, first, second), jnp.where(lane < 80, second, first)], axis=1)
-    band, op, step, factor = operators(laid, place_2, iz, 2, 69, S2)
+    mean = jnp.where(rows((128, 128), 0) >> 2 == rows((128, 128), 1), 0.25, 0.0)
+    msg[8] = exact(w[...], mean)[:, :32]
+
+
+def join_kernel(own, r1, r2, r3, l3, l2, l1, field, w):
+    first = jnp.concatenate([own[...], r1[...], r2[...], r3[...]], axis=2)
+    second = jnp.concatenate([jnp.zeros((9, 8, 32), F32), l3[...], l2[...], l1[...]], axis=2)
+    lane = rows((9, 8, 128), 2)
+    main, rest = jnp.where(lane < 80, first, second), jnp.where(lane < 80, second, first)
+    field[:, :, :128] = main[:8]
+    field[:, :, 128:] = rest[:8]
+    w[:, :128] = main[8]
+    w[:, 128:] = rest[8]
+
+
+def weights_2_kernel(w2, k2, k2u, m2, f2, k3, f3):
+    iz = lax.axis_index("gz")
+    band, op, step, factor = operators(w2[...], place_2, iz, 2, 69, S2)
     k2[...] = thrice(step)
     k2u[...] = thrice(step[:128, :128])
     m2[...] = thrice(op)
     f2[...] = jnp.broadcast_to(factor, (8, 256))
-    band, op, step, factor = operators(w3[...], place_3, iz, 3, 28, S3)
+    mean = jnp.where(place_2(rows((256, 128), 0)) >> 1 == place_3(rows((256, 128), 1)), 0.5, 0.0)
+    band, op, step, factor = operators(exact(w2[...], mean), place_3, iz, 3, 28, S3)
     k3[...] = thrice(step)
     f3[...] = jnp.broadcast_to(factor, (8, 128))
 
 
 def up_kernel(
-    pos, r2x, ya, yb, yc, yd, k2, k2u, m2, f2, k3, f3,
+    r2x, ya, yb, yc, yd, k2, k2u, m2, f2, k3, f3,
     k1, f1, e1s, r1s, k0, m0, f0, e0s, r0s, stat0, stat1,
     sol, res, stat,
-    ra, ea, eb, side2, gx2, r3, e3, side3, c3, cy2, ua, ub, side1, cy1, va, vb, side0, cy0,
+    ra, ea, eb, side2, gx2, r3, e3, side3, c3, cy2, ua, ub, side1, cy1, va, vb, side0, cy0, sol_v, res_v, sems,
 ):
-    ix, iy, iz = pos[0], pos[1], pos[2]
+    ix, iy, iz = lax.axis_index("gx"), lax.axis_index("gy"), lax.axis_index("gz")
     lane = rows((32, 128), 1)
     yrow = rows((32, 128), 0)
     for p in range(30):
@@ -307,9 +342,7 @@
             (y >= 0) & (y < NY // 4) & (yrow < 30), jnp.where((xr >= 0) & (xr < NX // 4), 1.0, 0.0), 0.0
         )
         full = jnp.concatenate([yc[p], ya[p], r2x[p], yb[p], yd[p], jnp.zeros((2, 256), F32)], axis=0)
-        first, second = full[:, :128], full[:, 128:]
-        main = jnp.where(lane < 80, first, second) * ok
-        rest = jnp.where(lane < 80, second, first) * ok
+        main, rest = full[:, :128] * ok, full[:, 128:] * ok
         ra[p, :, :128] = main
         ra[p, :, 128:] = rest
         ea[p, :, :128] = main * f2[0:1, :128]
@@ -418,6 +451,7 @@
     relax(vb, va, 3, 37, 9, k0[...], lambda p, q: fr0 * r0s[p:q], side0)
     total = jnp.zeros((32, 128), F32)
     last = m0[:, :128]
+    sends = []
     for p, q in chunks(4, 36, 8):
         mid = va[p:q]
         flat = va[p:q, :, :128]
@@ -425,14 +459,20 @@
             pltpu.roll(flat, 1, 1) + pltpu.roll(flat, 39, 1)
         )
         value = (r0s[p:q, :, :128] - times(mid, last) + S0 * near)[:, 4:36]
-        res[p - 4 : q - 4] = value
-        sol[p - 4 : q - 4] = va[p:q, 4:36, :128]
+        part = slice(p - 4, q - 4)
+        res_v[part] = value
+        sol_v[part] = va[p:q, 4:36, :128]
         total = total + jnp.sum(value * value, axis=0)
+        for i, (src, dst) in enumerate(((sol_v, sol), (res_v, res))):
+            sends.append(pltpu.make_async_copy(src.at[part], dst.at[part], sems.at[i, p // 8]))
+            sends[-1].start()
     sum3 = jnp.sum(total)
-    tile = rows((8, 128), 1)
+    tile = rows((1, 128), 1)
     stat[...] = jnp.where(
-        tile == 0, stat0[...], jnp.where(tile == 1, stat1[...], jnp.where(tile == 2, sum2, jnp.where(tile == 3, sum3, 0.0)))
+        tile == 0, stat0[0:1], jnp.where(tile == 1, stat1[0:1], jnp.where(tile == 2, sum2, jnp.where(tile == 3, sum3, 0.0)))
     )
+    for send in sends:
+        send.wait()
 
 
 def shift(x, axis, k):
@@ -440,126 +480,123 @@
     return lax.ppermute(x, axis, [((i + k) % n, i) for i in range(n)])
 
 
-def swap(x, axes, sizes, flip):
-    n = 1
-    for s in sizes:
-        n *= s
-    return lax.ppermute(x, axes, [(i ^ flip, i) for i in range(n)])
+def swap(x, axis, flip):
+    return lax.ppermute(x, axis, [(i ^ flip, i) for i in range(lax.axis_size(axis))])
 
 
 def f32(*shape):
-    return jax.ShapeDtypeStruct(shape, F32)
+    return pltpu.VMEM(shape, F32)
 
 
 def bf16(*shape):
-    return jax.ShapeDtypeStruct(shape, BF16)
+    return pltpu.VMEM(shape, BF16)
 
 
 def scratch(*shape):
     return pltpu.VMEM(shape, F32)
 
 
-def call(kernel, outs, scratches, n_in, name, scalars=True):
-    specs = [pl.BlockSpec(memory_space=pltpu.SMEM)] if scalars else []
-    specs += [pl.BlockSpec(memory_space=pltpu.VMEM)] * n_in
-    return pl.pallas_call(
-        kernel,
-        out_shape=outs,
-        in_specs=specs,
-        out_specs=[pl.BlockSpec(memory_space=pltpu.VMEM)] * len(outs),
-        scratch_shapes=scratches,
-        compiler_params=pltpu.CompilerParams(vmem_limit_bytes=VMEM_LIMIT),
-        name=name,
+def call(kernel, outs, scratches, name, limit=16, away=()):
+    def run(*operands):
+        operands = [x if x is None else pltpu.with_memory_space_constraint(x, pltpu.VMEM) for x in operands]
+        return pl.pallas_call(
+            kernel,
+            out_shape=[jax.ShapeDtypeStruct(o.shape, F32) if i in away else o for i, o in enumerate(outs)],
+            in_specs=[pl.BlockSpec(memory_space=pltpu.VMEM)] * len(operands),
+            out_specs=[pl.BlockSpec(memory_space=pl.ANY if i in away else pltpu.VMEM) for i in range(len(outs))],
+            scratch_shapes=scratches,
+            compiler_params=pltpu.CompilerParams(vmem_limit_bytes=limit * 2**20),
+            name=name,
+        )(*operands)
+
+    return run
+
+
+def pack(width, reach, count, n, height, groups, parts, extra, name):
+    def kernel(*refs):
+        if extra is None:
+            refs = refs[:5] + (None,) + refs[5:]
+        pack_kernel(width, reach, count, n, *refs)
+
+    outs = [f32(n + 2 * reach, height, 128), f32(groups, height, 128), f32(groups, height, 128)]
+    return call(kernel, outs, [], name)(*parts, *(() if extra is None else (extra,)))
+
+
+def sides(block, first, last, low, high, reach):
+    n = block.shape[0]
+    xlo = shift(last, "gx", -1)
+    xhi = shift(first, "gx", 1)
+    top = jnp.concatenate([xlo[:, n - reach :], high, xhi[:, n - reach :]], axis=0)
+    bottom = jnp.concatenate([xlo[:, :reach], low, xhi[:, :reach]], axis=0)
+    return block, xlo, xhi, shift(top, "gy", -1), shift(bottom, "gy", 1)
+
+
+def body(data, weights):
+    slab = f32(H0, 32, 128), f32(H0, 32, 128), f32(32, H0, 128), f32(32, H0, 128)
+    start = pl.pallas_call(
+        prepare_kernel,
+        out_shape=[f32(32, 32, 128), *slab],
+        in_specs=[pl.BlockSpec(memory_space=pltpu.VMEM)],
+        out_specs=[pl.BlockSpec(memory_space=pltpu.VMEM)] * 5,
+        name="prepare",
+    )(data)
+    dxy, to_left, to_right = pack(36, H0, 128, 32, 40, 15, sides(*start, H0), weights, "pack_data")
+    from_right, from_left = shift(to_left, "gz", 1), shift(to_right, "gz", -1)
+    b0, k0, m0, f0 = call(
+        weights_0_kernel, [bf16(768, 256), bf16(768, 256), bf16(768, 256), f32(8, 256)], [], "weights_0"
+    )(from_left, weights, from_right)
+    k1, k1u, m1, f1 = call(
+        weights_1_kernel, [bf16(768, 128), bf16(384, 128), bf16(384, 128), f32(8, 256)], [], "weights_1"
+    )(from_left, weights, from_right)
+    big = (40, 40, 256)
+    r1, r1_top, r1_bottom, e0s, r0s, stat0 = call(
+        down_0_kernel,
+        [f32(16, 16, 64), f32(16, H1, 64), f32(16, H1, 64), f32(*big), f32(*big), f32(8, 128)],
+        [scratch(*big), scratch(*big), scratch(*big), scratch(*big), scratch(16, 2, 40, 128)],
+        "down_0",
+    )(dxy, from_right, from_left, b0, k0, m0, f0)
+    rxy, to_left, to_right = pack(
+        37, H1, 64, 16, 32, 9, sides(r1, r1[:H1], r1[16 - H1 :], r1_bottom, r1_top, H1), None, "pack_r1"
     )
-
-
-def coarsen(w):
-    return 0.5 * (w[:, 0::2] + w[:, 1::2])
-
-
-def pack(width, reach, count, n, height, groups, parts, name):
-    def kernel(*refs):
-        pack_kernel(width, reach, count, n, *refs)
-
-    outs = [f32(n + 2 * reach, height, 128), f32(groups, height, 128), f32(groups, height, 128)]
-    return call(kernel, outs, [], 5, name, scalars=False)(*parts)
-
-
-def sides(block, reach):
-    n = block.shape[0]
-    xlo = shift(block[n - reach :], "gx", -1)
-    xhi = shift(block[:reach], "gx", 1)
-    top = jnp.concatenate([xlo[:, n - reach :], block[:, n - reach :], xhi[:, n - reach :]], axis=0)
-    bottom = jnp.concatenate([xlo[:, :reach], block[:, :reach], xhi[:, :reach]], axis=0)
-    return block, xlo, xhi, shift(top, "gy", -1), shift(bottom, "gy", 1)
-
-
-def body(data, weights):
-    pos = jnp.stack([lax.axis_index("gx"), lax.axis_index("gy"), lax.axis_index("gz")]).astype(jnp.int32)
-    w1 = coarsen(weights)
-    w2 = coarsen(w1)
-    both = jnp.concatenate([weights, w1], axis=1)
-    wl, wr = shift(both, "gz", -1), shift(both, "gz", 1)
-    wide0 = jnp.concatenate([weights, wr[:, :64], wl[:, 64:128]], axis=1)
-    wide1 = jnp.concatenate([w1, wr[:, 128:], wl[:, 128:], wl[:, 128:]], axis=1)
-    b0, k0, m0, f0, k1, m1, f1 = call(
-        weights_kernel,
-        [bf16(768, 256), bf16(768, 256), bf16(768, 256), f32(8, 256), bf16(768, 128), bf16(384, 128), f32(8, 256)],
-        [], 2, "weights_fine",
-    )(pos, wide0, wide1)
-    dxy, to_left, to_right = pack(36, H0, 128, 32, 40, 14, sides(data, H0), "pack_data")
-    from_right, from_left = shift(to_left, "gz", 1), shift(to_right, "gz", -1)
-    big = (40, 40, 256)
-    r1, e0s, r0s, stat0 = call(
-        down_0_kernel,
-        [f32(16, 16, 64), f32(*big), f32(*big), f32(8, 128)],
-        [scratch(*big), scratch(*big), scratch(*big), scratch(*big), scratch(16, 2, 40, 128)],
-        7, "down_0",
-    )(pos, dxy, from_right, from_left, b0, k0, m0, f0)
-    rxy, to_left, to_right = pack(37, H1, 64, 16, 32, 9, sides(r1, H1), "pack_r1")
     from_right, from_left = shift(to_left, "gz", 1), shift(to_right, "gz", -1)
     mid = (26, 32, 128)
     msg, e1s, r1s, stat1 = call(
         down_1_kernel,
         [f32(9, 8, 32), f32(*mid), f32(*mid), f32(8, 128)],
         [scratch(*mid), scratch(*mid), scratch(*mid), scratch(*mid), scratch(8, 32, 128)],
-        7, "down_1",
-    )(pos, rxy, from_right, from_left, k1, m1, f1, w2)
+        "down_1",
+    )(rxy, from_right, from_left, k1, m1, f1, weights)
     near = {k: shift(msg, "gz", k) for k in (1, -1, 2, -2, 3, -3)}
-    wide = jnp.concatenate([msg, near[1], near[2], near[3], jnp.zeros_like(msg), near[-3], near[-2], near[-1]], axis=2)
-    wide2 = wide[8]
+    r2z, wide2 = call(join_kernel, [f32(8, 8, 256), f32(8, 256)], [], "join")(
+        msg, near[1], near[2], near[3], near[-3], near[-2], near[-1]
+    )
     k2, k2u, m2, f2, k3, f3 = call(
         weights_2_kernel,
         [bf16(768, 256), bf16(384, 128), bf16(768, 256), f32(8, 256), bf16(384, 128), f32(8, 128)],
-        [], 2, "weights_coarse",
-    )(pos, wide2, coarsen(wide2))
-    r2z = wide[:8]
+        [], "weights_coarse",
+    )(wide2)
     x1, x2, x3 = (shift(r2z, "gx", k) for k in (1, 2, 3))
     r2x = jnp.concatenate([x2[5:], x3, r2z, x1, x2[:3]], axis=0)
     ya, yb = shift(r2x, "gy", -1), shift(r2x, "gy", 1)
     yc, yd = shift(r2x[:, 5:], "gy", -2), shift(r2x[:, :3], "gy", 2)
-    k1u = jnp.concatenate([k1[:128], k1[256:384], k1[512:640]], axis=0)
     lev2 = (30, 32, 256)
     sol, res, stat = call(
         up_kernel,
-        [f32(32, 32, 128), f32(32, 32, 128), f32(8, 128)],
+        [f32(32, 32, 128), f32(32, 32, 128), f32(1, 128)],
         [
             scratch(*lev2), scratch(*lev2), scratch(*lev2), scratch(*lev2), scratch(12, 2, 40, 128),
             scratch(14, 32, 128), scratch(12, 16, 128), scratch(12, 16, 128), scratch(12, 16, 128),
             scratch(12, 32, 128), scratch(*mid), scratch(*mid), scratch(*mid), scratch(14, 32, 128),
-            scratch(*big), scratch(*big), scratch(*big), scratch(20, 2, 40, 128),
+            scratch(*big), scratch(*big), scratch(*big), scratch(20, 2, 40, 128), scratch(32, 32, 128), scratch(32, 32, 128), pltpu.SemaphoreType.DMA((2, 5)),
         ],
-        22, "up",
-    )(pos, r2x, ya, yb, yc, yd, k2, k2u, m2, f2, k3, f3, k1u, f1, e1s, r1s, k0, m0, f0, e0s, r0s, stat0, stat1)
-    t = stat[:1]
-    for axes, sizes, flips in (
-        ("gx", (4,), (1, 2, 3)),
-        ("gy", (8,), (2, 4, 6)),
-        (("gy", "gz"), (8, 8), (1, 8, 9)),
-        ("gz", (8,), (2, 4, 6)),
-    ):
-        a, b, c = (swap(t, axes, sizes, f) for f in flips)
-        t = (t + a) + (b + c)
+        "up", 24, (0, 1),
+    )(r2x, ya, yb, yc, yd, k2, k2u, m2, f2, k3, f3, k1u, f1, e1s, r1s, k0, m0, f0, e0s, r0s, stat0, stat1)
+    t = stat
+    for axis, flips in (("gy", (1,)), ("gx", (1, 2, 3)), ("gy", (2, 4, 6)), ("gz", (1, 2, 3)), ("gz", (7,))):
+        others = [swap(t, axis, f) for f in flips]
+        t = t + others[0]
+        if len(others) > 1:
+            t = t + (others[1] + others[2])
     cells = jnp.array([NX * NY * NZ >> (3 * k) for k in (0, 1, 2, 0)], F32)
     return sol, res, jnp.sqrt(t[0, :4] / cells)
 

time: 146 us -> 121 us (0.83)
  the two profiles are of different devices: /device:TPU:10 before, /device:TPU:32 now
where the time goes in v2:
time: 121 us
  waiting for transfers between devices  51.4 us (42%)
  starting transfers between devices  50.9 us (42%)
  Pallas kernels  16 us (13%)
    ppermute x25, waiting for transfers between devices, shift(): return lax.ppermute(x, axis, [((i + k) % n, i) for i in range(n)])  40 us
    ppermute x25, starting transfers between devices, shift(): return lax.ppermute(x, axis, [((i + k) % n, i) for i in range(n)])  33.4 us
    ppermute x11, starting transfers between devices, swap(): lax.ppermute(x, axis, [(i ^ flip, i) for i in range(lax.axis_size(axis))])  17.4 us
    pallas_call x9, Pallas kernels, run(): pl.pallas_call(kernel, out_shape=[jax.ShapeDtypeStruct(o.shape, F32) if i...  14.9 us
    ppermute x11, waiting for transfers between devices, swap(): lax.ppermute(x, axis, [(i ^ flip, i) for i in range(lax.axis_size(axis))])  11.4 us
  transfers between devices with their start and end apart: 36, of which 25 were waited for; matrix products, arithmetic and copies ran while one was open for 0% of the time, Pallas kernels for 2%

profile of v2, /device:TPU:32, one launch (start us, length us, event | category | flops | bytes accessed | tf_op | source)
XLA Modules:
  0.0 120.5 jit_solution(9105693873154525914)
XLA Ops:
  1.7 1.7 %collective-permute-start = (f32[4,32,128]{2,1,0:T(8,128)S(1)}, f32[4,32,128]{2,1,0:T(8,128)S(1)}, u32[]{:S(2)}, u32[]{:S(2)}) collective-permute-start(f32[4,32,128]{2,1,0:T(8,128)S(1)} %get-tuple-element.44), channel_id=1, source_target_pairs={{192,0},{0,64},{64,128},{128,192},{193,1},{1,65},{65,129},{129,193... | collective-permute-start | bytes 196616 | tf_op jit(solution)/shard_map/ppermute | solution.py:480
  3.4 1.7 %collective-permute-start.1 = (f32[4,32,128]{2,1,0:T(8,128)S(1)}, f32[4,32,128]{2,1,0:T(8,128)S(1)}, u32[]{:S(2)}, u32[]{:S(2)}) collective-permute-start(f32[4,32,128]{2,1,0:T(8,128)S(1)} %get-tuple-element.45), channel_id=1, source_target_pairs={{64,0},{128,64},{192,128},{0,192},{65,1},{129,65},{193,129},{1,193... | collective-permute-start | bytes 196616 | tf_op jit(solution)/shard_map/ppermute | solution.py:480
  5.0 2.2 %collective-permute-done.refs_1_ = f32[4,32,128]{2,1,0:T(8,128)S(1)} collective-permute-done((f32[4,32,128]{2,1,0:T(8,128)S(1)}, f32[4,32,128]{2,1,0:T(8,128)S(1)}, u32[]{:S(2)}, u32[]{:S(2)}) %collective-permute-start) | collective-permute-done | bytes 65568 | tf_op jit(solution)/shard_map/ppermute | solution.py:480
  7.7 2.9 %collective-permute-start.3 = (f32[40,4,128]{2,1,0:T(4,128)S(1)}, f32[40,4,128]{2,1,0:T(4,128)S(1)}, u32[]{:S(2)}, u32[]{:S(2)}) collective-permute-start(f32[40,4,128]{2,1,0:T(4,128)S(1)} %pad_maximum_fusion.3), channel_id=1, source_target_pairs={{8,0},{16,8},{24,16},{32,24},{40,32},{48,40},{56,48},{0,56},{9,1},... | collective-permute-start | bytes 245768 | tf_op jit(solution)/shard_map/ppermute | solution.py:480
  10.7 2.1 %collective-permute-done.2.refs_3_ = f32[40,4,128]{2,1,0:T(4,128)S(1)} collective-permute-done((f32[40,4,128]{2,1,0:T(4,128)S(1)}, f32[40,4,128]{2,1,0:T(4,128)S(1)}, u32[]{:S(2)}, u32[]{:S(2)}) %collective-permute-start.2) | collective-permute-done | bytes 81952 | tf_op jit(solution)/shard_map/ppermute | solution.py:480
  16.0 7.8 %collective-permute-done.4.right.from_right = f32[15,40,128]{2,1,0:T(8,128)S(1)} collective-permute-done((f32[15,40,128]{2,1,0:T(8,128)S(1)}, f32[15,40,128]{2,1,0:T(8,128)S(1)}, u32[]{:S(2)}, u32[]{:S(2)}) %collective-permute-start.4) | collective-permute-done | bytes 307232 | tf_op jit(solution)/shard_map/ppermute | solution.py:480
  23.8 3.8 %collective-permute-done.5.left.from_left = f32[15,40,128]{2,1,0:T(8,128)S(1)} collective-permute-done((f32[15,40,128]{2,1,0:T(8,128)S(1)}, f32[15,40,128]{2,1,0:T(8,128)S(1)}, u32[]{:S(2)}, u32[]{:S(2)}) %collective-permute-start.5) | collective-permute-done | bytes 307232 | tf_op jit(solution)/shard_map/ppermute | solution.py:480
  28.2 3.2 %down_0.1 = (f32[16,16,64]{2,1,0:T(8,128)S(1)}, f32[16,5,64]{2,1,0:T(8,128)S(1)}, f32[16,5,64]{2,1,0:T(8,128)S(1)}, f32[40,40,256]{2,1,0:T(8,128)S(1)}, f32[40,4...) custom-call(f32[40,40,128]{2,1,0:T(8,128)S(1)} %get-tuple-element.48.dxy, ...), custom_call_target="tpu_custom_call" | custom-call | tf_op jit(solution)/shard_map/down_0/pallas_call | solution.py:502
  31.4 2.9 %collective-permute-start.7 = (f32[5,16,64]{2,1,0:T(8,128)S(1)}, f32[5,16,64]{2,1,0:T(8,128)S(1)}, u32[]{:S(2)}, u32[]{:S(2)}) collective-permute-start(f32[5,16,64]{2,1,0:T(8,128)S(1)} %get-tuple-element.85), channel_id=1, source_target_pairs={{64,0},{128,64},{192,128},{0,192},{65,1},{129,65},{193,129},{1,193... | collective-permute-start | bytes 61448 | tf_op jit(solution)/shard_map/ppermute | solution.py:480
  34.4 1.7 %collective-permute-done.7.refs_2_ = f32[5,16,64]{2,1,0:T(8,128)S(1)} collective-permute-done((f32[5,16,64]{2,1,0:T(8,128)S(1)}, f32[5,16,64]{2,1,0:T(8,128)S(1)}, u32[]{:S(2)}, u32[]{:S(2)}) %collective-permute-start.7) | collective-permute-done | bytes 20512 | tf_op jit(solution)/shard_map/ppermute | solution.py:480
  36.1 3.5 %collective-permute-done.6.refs_1_ = f32[5,16,64]{2,1,0:T(8,128)S(1)} collective-permute-done((f32[5,16,64]{2,1,0:T(8,128)S(1)}, f32[5,16,64]{2,1,0:T(8,128)S(1)}, u32[]{:S(2)}, u32[]{:S(2)}) %collective-permute-start.6) | collective-permute-done | bytes 20512 | tf_op jit(solution)/shard_map/ppermute | solution.py:480
  39.7 2.9 %collective-permute-start.9 = (f32[26,5,64]{2,1,0:T(8,128)S(1)}, f32[26,5,64]{2,1,0:T(8,128)S(1)}, u32[]{:S(2)}, u32[]{:S(2)}) collective-permute-start(f32[26,5,64]{2,1,0:T(8,128)S(1)} %pad_maximum_fusion.1), channel_id=1, source_target_pairs={{8,0},{16,8},{24,16},{32,24},{40,32},{48,40},{56,48},{0,56},{9,1},... | collective-permute-start | bytes 99848 | tf_op jit(solution)/shard_map/ppermute | solution.py:480
  42.6 2.4 %collective-permute-done.8.refs_3_ = f32[26,5,64]{2,1,0:T(8,128)S(1)} collective-permute-done((f32[26,5,64]{2,1,0:T(8,128)S(1)}, f32[26,5,64]{2,1,0:T(8,128)S(1)}, u32[]{:S(2)}, u32[]{:S(2)}) %collective-permute-start.8) | collective-permute-done | bytes 33312 | tf_op jit(solution)/shard_map/ppermute | solution.py:480
  45.2 3.0 %collective-permute-start.10 = (f32[9,32,128]{2,1,0:T(8,128)S(1)}, f32[9,32,128]{2,1,0:T(8,128)S(1)}, u32[]{:S(2)}, u32[]{:S(2)}) collective-permute-start(f32[9,32,128]{2,1,0:T(8,128)S(1)} %get-tuple-element.59), channel_id=1, source_target_pairs={{1,0},{2,1},{3,2},{4,3},{5,4},{6,5},{7,6},{0,7},{9,8},{10,9},{11,1... | collective-permute-start | bytes 442376 | tf_op jit(solution)/shard_map/ppermute | solution.py:480
  49.4 2.2 %collective-permute-done.10.from_right = f32[9,32,128]{2,1,0:T(8,128)S(1)} collective-permute-done((f32[9,32,128]{2,1,0:T(8,128)S(1)}, f32[9,32,128]{2,1,0:T(8,128)S(1)}, u32[]{:S(2)}, u32[]{:S(2)}) %collective-permute-start.10) | collective-permute-done | bytes 147488 | tf_op jit(solution)/shard_map/ppermute | solution.py:480
  51.6 2.2 %collective-permute-done.11.from_left = f32[9,32,128]{2,1,0:T(8,128)S(1)} collective-permute-done((f32[9,32,128]{2,1,0:T(8,128)S(1)}, f32[9,32,128]{2,1,0:T(8,128)S(1)}, u32[]{:S(2)}, u32[]{:S(2)}) %collective-permute-start.11) | collective-permute-done | bytes 147488 | tf_op jit(solution)/shard_map/ppermute | solution.py:480
  55.1 1.7 %collective-permute-start.16 = (f32[9,8,32]{2,1,0:T(8,128)S(1)}, f32[9,8,32]{2,1,0:T(8,128)S(1)}, u32[]{:S(2)}, u32[]{:S(2)}) collective-permute-start(f32[9,8,32]{2,1,0:T(8,128)S(1)} %get-tuple-element.64.own), channel_id=1, source_target_pairs={{6,0},{7,1},{0,2},{1,3},{2,4},{3,5},{4,6},{5,7},{14,8},{15,9},{8,1... | collective-permute-start | bytes 27656 | tf_op jit(solution)/shard_map/ppermute | solution.py:480
  56.8 2.1 %collective-permute-start.15 = (f32[9,8,32]{2,1,0:T(8,128)S(1)}, f32[9,8,32]{2,1,0:T(8,128)S(1)}, u32[]{:S(2)}, u32[]{:S(2)}) collective-permute-start(f32[9,8,32]{2,1,0:T(8,128)S(1)} %get-tuple-element.64.own), channel_id=1, source_target_pairs={{5,0},{6,1},{7,2},{0,3},{1,4},{2,5},{3,6},{4,7},{13,8},{14,9},{15,... | collective-permute-start | bytes 27656 | tf_op jit(solution)/shard_map/ppermute | solution.py:480
  58.9 2.9 %collective-permute-start.14 = (f32[9,8,32]{2,1,0:T(8,128)S(1)}, f32[9,8,32]{2,1,0:T(8,128)S(1)}, u32[]{:S(2)}, u32[]{:S(2)}) collective-permute-start(f32[9,8,32]{2,1,0:T(8,128)S(1)} %get-tuple-element.64.own), channel_id=1, source_target_pairs={{3,0},{4,1},{5,2},{6,3},{7,4},{0,5},{1,6},{2,7},{11,8},{12,9},{13,... | collective-permute-start | bytes 27656 | tf_op jit(solution)/shard_map/ppermute | solution.py:480
  63.0 2.9 %collective-permute-start.12 = (f32[9,8,32]{2,1,0:T(8,128)S(1)}, f32[9,8,32]{2,1,0:T(8,128)S(1)}, u32[]{:S(2)}, u32[]{:S(2)}) collective-permute-start(f32[9,8,32]{2,1,0:T(8,128)S(1)} %get-tuple-element.64.own), channel_id=1, source_target_pairs={{1,0},{2,1},{3,2},{4,3},{5,4},{6,5},{7,6},{0,7},{9,8},{10,9},{11,1... | collective-permute-start | bytes 27656 | tf_op jit(solution)/shard_map/ppermute | solution.py:480
  70.0 3.7 %collective-permute-done.18 = f32[8,8,256]{2,1,0:T(8,128)S(1)} collective-permute-done((f32[8,8,256]{2,1,0:T(8,128)S(1)}, f32[8,8,256]{2,1,0:T(8,128)S(1)}, u32[]{:S(2)}, u32[]{:S(2)}) %collective-permute-start.18) | collective-permute-done | bytes 65568 | tf_op jit(solution)/shard_map/ppermute | solution.py:480
  78.3 3.6 %collective-permute-done.24.yd = f32[30,3,256]{2,1,0:T(4,128)S(1)} collective-permute-done((f32[30,3,256]{2,1,0:T(4,128)S(1)}, f32[30,3,256]{2,1,0:T(4,128)S(1)}, u32[]{:S(2)}, u32[]{:S(2)}) %collective-permute-start.24) | collective-permute-done | bytes 92192 | tf_op jit(solution)/shard_map/ppermute | solution.py:480
  81.9 1.8 %collective-permute-done.23.yc = f32[30,3,256]{2,1,0:T(4,128)S(1)} collective-permute-done((f32[30,3,256]{2,1,0:T(4,128)S(1)}, f32[30,3,256]{2,1,0:T(4,128)S(1)}, u32[]{:S(2)}, u32[]{:S(2)}) %collective-permute-start.23) | collective-permute-done | bytes 92192 | tf_op jit(solution)/shard_map/ppermute | solution.py:480
  83.7 7.4 %up.1 = (f32[32,32,128]{2,1,0:T(8,128)}, f32[32,32,128]{2,1,0:T(8,128)}, f32[1,128]{1,0:T(1,128)S(1)}) custom-call(f32[30,8,256]{2,1,0:T(8,128)S(1)} %slice_dynamic-update-slice_fusion.r2x, f32[30,8,256]{2,1,0:T(8,128)S(1)} %collective-permute-done.21.ya, f32[30,8,256]{2,1,0:T(8,128)S(1)} %collective-permute-done.22.yb, ...), custom_call_target="tpu_custom_call" | custom-call | tf_op jit(solution)/shard_map/up/pallas_call | solution.py:502
  94.0 2.6 %collective-permute-start.26 = (f32[1,128]{1,0:T(1,128)S(1)}, f32[1,128]{1,0:T(1,128)S(1)}, u32[]{:S(2)}, u32[]{:S(2)}) collective-permute-start(f32[1,128]{1,0:T(1,128)S(1)} %add.33), channel_id=1, source_target_pairs={{64,0},{0,64},{192,128},{128,192},{65,1},{1,65},{193,129},{129,193... | collective-permute-start | bytes 1544 | tf_op jit(solution)/shard_map/ppermute | solution.py:484
  97.2 1.7 %collective-permute-done.27 = f32[1,128]{1,0:T(1,128)S(1)} collective-permute-done((f32[1,128]{1,0:T(1,128)S(1)}, f32[1,128]{1,0:T(1,128)S(1)}, u32[]{:S(2)}, u32[]{:S(2)}) %collective-permute-start.27) | collective-permute-done | bytes 544 | tf_op jit(solution)/shard_map/ppermute | solution.py:484
  101.1 2.0 %collective-permute-start.29 = (f32[1,128]{1,0:T(1,128)S(1)}, f32[1,128]{1,0:T(1,128)S(1)}, u32[]{:S(2)}, u32[]{:S(2)}) collective-permute-start(f32[1,128]{1,0:T(1,128)S(1)} %add_add_fusion.2), channel_id=1, source_target_pairs={{16,0},{24,8},{0,16},{8,24},{48,32},{56,40},{32,48},{40,56},{17,1}... | collective-permute-start | bytes 1544 | tf_op jit(solution)/shard_map/ppermute | solution.py:484
  105.1 2.4 %collective-permute-start.34 = (f32[1,128]{1,0:T(1,128)S(1)}, f32[1,128]{1,0:T(1,128)S(1)}, u32[]{:S(2)}, u32[]{:S(2)}) collective-permute-start(f32[1,128]{1,0:T(1,128)S(1)} %add_add_fusion.1), channel_id=1, source_target_pairs={{3,0},{2,1},{1,2},{0,3},{7,4},{6,5},{5,6},{4,7},{11,8},{10,9},{9,1... | collective-permute-start | bytes 1544 | tf_op jit(solution)/shard_map/ppermute | solution.py:484
  107.5 2.4 %collective-permute-start.33 = (f32[1,128]{1,0:T(1,128)S(1)}, f32[1,128]{1,0:T(1,128)S(1)}, u32[]{:S(2)}, u32[]{:S(2)}) collective-permute-start(f32[1,128]{1,0:T(1,128)S(1)} %add_add_fusion.1), channel_id=1, source_target_pairs={{2,0},{3,1},{0,2},{1,3},{6,4},{7,5},{4,6},{5,7},{10,8},{11,9},{8,1... | collective-permute-start | bytes 1544 | tf_op jit(solution)/shard_map/ppermute | solution.py:484
  109.9 2.0 %collective-permute-done.33 = f32[1,128]{1,0:T(1,128)S(1)} collective-permute-done((f32[1,128]{1,0:T(1,128)S(1)}, f32[1,128]{1,0:T(1,128)S(1)}, u32[]{:S(2)}, u32[]{:S(2)}) %collective-permute-start.33) | collective-permute-done | bytes 544 | tf_op jit(solution)/shard_map/ppermute | solution.py:484
  113.4 3.9 %collective-permute-start.35 = (f32[1,128]{1,0:T(1,128)S(1)}, f32[1,128]{1,0:T(1,128)S(1)}, u32[]{:S(2)}, u32[]{:S(2)}) collective-permute-start(f32[1,128]{1,0:T(1,128)S(1)} %add_add_fusion), channel_id=1, source_target_pairs={{7,0},{6,1},{5,2},{4,3},{3,4},{2,5},{1,6},{0,7},{15,8},{14,9},{13,... | collective-permute-start | bytes 1544 | tf_op jit(solution)/shard_map/ppermute | solution.py:484
  117.3 2.7 %collective-permute-done.35 = f32[1,128]{1,0:T(1,128)S(1)} collective-permute-done((f32[1,128]{1,0:T(1,128)S(1)}, f32[1,128]{1,0:T(1,128)S(1)}, u32[]{:S(2)}, u32[]{:S(2)}) %collective-permute-start.35) | collective-permute-done | bytes 544 | tf_op jit(solution)/shard_map/ppermute | solution.py:484
  (77 shorter events, 27.7 us)
Async XLA Ops:
  1.7 5.6 %collective-permute-start = (f32[4,32,128]{2,1,0:T(8,128)S(1)}, f32[4,32,128]{2,1,0:T(8,128)S(1)}, u32[]{:S(2)}, u32[]{:S(2)}) collective-permute-start(f32[4,32,128]{2,1,0:T(8,128)S(1)} %get-tuple-element.44), channel_id=1, source_target_pairs={{192,0},{0,64},{64,128},{128,192},{193,1},{1,65},{65,129},{129,193... | collective-permute-start | bytes 196616 | tf_op jit(solution)/shard_map/ppermute | solution.py:480
  7.7 5.1 %collective-permute-start.2 = (f32[40,4,128]{2,1,0:T(4,128)S(1)}, f32[40,4,128]{2,1,0:T(4,128)S(1)}, u32[]{:S(2)}, u32[]{:S(2)}) collective-permute-start(f32[40,4,128]{2,1,0:T(4,128)S(1)} %pad_maximum_fusion.2), channel_id=1, source_target_pairs={{56,0},{0,8},{8,16},{16,24},{24,32},{32,40},{40,48},{48,56},{57,1}... | collective-permute-start | bytes 245768 | tf_op jit(solution)/shard_map/ppermute | solution.py:480
  7.7 5.0 %collective-permute-start.3 = (f32[40,4,128]{2,1,0:T(4,128)S(1)}, f32[40,4,128]{2,1,0:T(4,128)S(1)}, u32[]{:S(2)}, u32[]{:S(2)}) collective-permute-start(f32[40,4,128]{2,1,0:T(4,128)S(1)} %pad_maximum_fusion.3), channel_id=1, source_target_pairs={{8,0},{16,8},{24,16},{32,24},{40,32},{48,40},{56,48},{0,56},{9,1},... | collective-permute-start | bytes 245768 | tf_op jit(solution)/shard_map/ppermute | solution.py:480
  13.9 9.9 %collective-permute-start.4 = (f32[15,40,128]{2,1,0:T(8,128)S(1)}, f32[15,40,128]{2,1,0:T(8,128)S(1)}, u32[]{:S(2)}, u32[]{:S(2)}) collective-permute-start(f32[15,40,128]{2,1,0:T(8,128)S(1)} %get-tuple-element.49), channel_id=1, source_target_pairs={{1,0},{2,1},{3,2},{4,3},{5,4},{6,5},{7,6},{0,7},{9,8},{10,9},{11,1... | collective-permute-start | bytes 921608 | tf_op jit(solution)/shard_map/ppermute | solution.py:480
  15.5 12.1 %collective-permute-start.5 = (f32[15,40,128]{2,1,0:T(8,128)S(1)}, f32[15,40,128]{2,1,0:T(8,128)S(1)}, u32[]{:S(2)}, u32[]{:S(2)}) collective-permute-start(f32[15,40,128]{2,1,0:T(8,128)S(1)} %get-tuple-element.50), channel_id=1, source_target_pairs={{7,0},{0,1},{1,2},{2,3},{3,4},{4,5},{5,6},{6,7},{15,8},{8,9},{9,10... | collective-permute-start | bytes 921608 | tf_op jit(solution)/shard_map/ppermute | solution.py:480
  31.4 4.6 %collective-permute-start.7 = (f32[5,16,64]{2,1,0:T(8,128)S(1)}, f32[5,16,64]{2,1,0:T(8,128)S(1)}, u32[]{:S(2)}, u32[]{:S(2)}) collective-permute-start(f32[5,16,64]{2,1,0:T(8,128)S(1)} %get-tuple-element.85), channel_id=1, source_target_pairs={{64,0},{128,64},{192,128},{0,192},{65,1},{129,65},{193,129},{1,193... | collective-permute-start | bytes 61448 | tf_op jit(solution)/shard_map/ppermute | solution.py:480
  34.4 5.2 %collective-permute-start.6 = (f32[5,16,64]{2,1,0:T(8,128)S(1)}, f32[5,16,64]{2,1,0:T(8,128)S(1)}, u32[]{:S(2)}, u32[]{:S(2)}) collective-permute-start(f32[5,16,64]{2,1,0:T(8,128)S(1)} %get-tuple-element.86), channel_id=1, source_target_pairs={{192,0},{0,64},{64,128},{128,192},{193,1},{1,65},{65,129},{129,193... | collective-permute-start | bytes 61448 | tf_op jit(solution)/shard_map/ppermute | solution.py:480
  39.6 5.4 %collective-permute-start.8 = (f32[26,5,64]{2,1,0:T(8,128)S(1)}, f32[26,5,64]{2,1,0:T(8,128)S(1)}, u32[]{:S(2)}, u32[]{:S(2)}) collective-permute-start(f32[26,5,64]{2,1,0:T(8,128)S(1)} %pad_maximum_fusion), channel_id=1, source_target_pairs={{56,0},{0,8},{8,16},{16,24},{24,32},{32,40},{40,48},{48,56},{57,1}... | collective-permute-start | bytes 99848 | tf_op jit(solution)/shard_map/ppermute | solution.py:480
  39.7 5.3 %collective-permute-start.9 = (f32[26,5,64]{2,1,0:T(8,128)S(1)}, f32[26,5,64]{2,1,0:T(8,128)S(1)}, u32[]{:S(2)}, u32[]{:S(2)}) collective-permute-start(f32[26,5,64]{2,1,0:T(8,128)S(1)} %pad_maximum_fusion.1), channel_id=1, source_target_pairs={{8,0},{16,8},{24,16},{32,24},{40,32},{48,40},{56,48},{0,56},{9,1},... | collective-permute-start | bytes 99848 | tf_op jit(solution)/shard_map/ppermute | solution.py:480
  45.2 6.3 %collective-permute-start.10 = (f32[9,32,128]{2,1,0:T(8,128)S(1)}, f32[9,32,128]{2,1,0:T(8,128)S(1)}, u32[]{:S(2)}, u32[]{:S(2)}) collective-permute-start(f32[9,32,128]{2,1,0:T(8,128)S(1)} %get-tuple-element.59), channel_id=1, source_target_pairs={{1,0},{2,1},{3,2},{4,3},{5,4},{6,5},{7,6},{0,7},{9,8},{10,9},{11,1... | collective-permute-start | bytes 442376 | tf_op jit(solution)/shard_map/ppermute | solution.py:480
  48.3 5.5 %collective-permute-start.11 = (f32[9,32,128]{2,1,0:T(8,128)S(1)}, f32[9,32,128]{2,1,0:T(8,128)S(1)}, u32[]{:S(2)}, u32[]{:S(2)}) collective-permute-start(f32[9,32,128]{2,1,0:T(8,128)S(1)} %get-tuple-element.60), channel_id=1, source_target_pairs={{7,0},{0,1},{1,2},{2,3},{3,4},{4,5},{5,6},{6,7},{15,8},{8,9},{9,10... | collective-permute-start | bytes 442376 | tf_op jit(solution)/shard_map/ppermute | solution.py:480
  54.7 8.3 %collective-permute-start.17 = (f32[9,8,32]{2,1,0:T(8,128)S(1)}, f32[9,8,32]{2,1,0:T(8,128)S(1)}, u32[]{:S(2)}, u32[]{:S(2)}) collective-permute-start(f32[9,8,32]{2,1,0:T(8,128)S(1)} %get-tuple-element.64.own), channel_id=1, source_target_pairs={{7,0},{0,1},{1,2},{2,3},{3,4},{4,5},{5,6},{6,7},{15,8},{8,9},{9,10... | collective-permute-start | bytes 27656 | tf_op jit(solution)/shard_map/ppermute | solution.py:480
  55.1 10.9 %collective-permute-start.16 = (f32[9,8,32]{2,1,0:T(8,128)S(1)}, f32[9,8,32]{2,1,0:T(8,128)S(1)}, u32[]{:S(2)}, u32[]{:S(2)}) collective-permute-start(f32[9,8,32]{2,1,0:T(8,128)S(1)} %get-tuple-element.64.own), channel_id=1, source_target_pairs={{6,0},{7,1},{0,2},{1,3},{2,4},{3,5},{4,6},{5,7},{14,8},{15,9},{8,1... | collective-permute-start | bytes 27656 | tf_op jit(solution)/shard_map/ppermute | solution.py:480
  56.8 9.2 %collective-permute-start.15 = (f32[9,8,32]{2,1,0:T(8,128)S(1)}, f32[9,8,32]{2,1,0:T(8,128)S(1)}, u32[]{:S(2)}, u32[]{:S(2)}) collective-permute-start(f32[9,8,32]{2,1,0:T(8,128)S(1)} %get-tuple-element.64.own), channel_id=1, source_target_pairs={{5,0},{6,1},{7,2},{0,3},{1,4},{2,5},{3,6},{4,7},{13,8},{14,9},{15,... | collective-permute-start | bytes 27656 | tf_op jit(solution)/shard_map/ppermute | solution.py:480
  58.9 7.7 %collective-permute-start.14 = (f32[9,8,32]{2,1,0:T(8,128)S(1)}, f32[9,8,32]{2,1,0:T(8,128)S(1)}, u32[]{:S(2)}, u32[]{:S(2)}) collective-permute-start(f32[9,8,32]{2,1,0:T(8,128)S(1)} %get-tuple-element.64.own), channel_id=1, source_target_pairs={{3,0},{4,1},{5,2},{6,3},{7,4},{0,5},{1,6},{2,7},{11,8},{12,9},{13,... | collective-permute-start | bytes 27656 | tf_op jit(solution)/shard_map/ppermute | solution.py:480
  61.8 5.2 %collective-permute-start.13 = (f32[9,8,32]{2,1,0:T(8,128)S(1)}, f32[9,8,32]{2,1,0:T(8,128)S(1)}, u32[]{:S(2)}, u32[]{:S(2)}) collective-permute-start(f32[9,8,32]{2,1,0:T(8,128)S(1)} %get-tuple-element.64.own), channel_id=1, source_target_pairs={{2,0},{3,1},{4,2},{5,3},{6,4},{7,5},{0,6},{1,7},{10,8},{11,9},{12,... | collective-permute-start | bytes 27656 | tf_op jit(solution)/shard_map/ppermute | solution.py:480
  63.0 4.6 %collective-permute-start.12 = (f32[9,8,32]{2,1,0:T(8,128)S(1)}, f32[9,8,32]{2,1,0:T(8,128)S(1)}, u32[]{:S(2)}, u32[]{:S(2)}) collective-permute-start(f32[9,8,32]{2,1,0:T(8,128)S(1)} %get-tuple-element.64.own), channel_id=1, source_target_pairs={{1,0},{2,1},{3,2},{4,3},{5,4},{6,5},{7,6},{0,7},{9,8},{10,9},{11,1... | collective-permute-start | bytes 27656 | tf_op jit(solution)/shard_map/ppermute | solution.py:480
  67.8 5.9 %collective-permute-start.18 = (f32[8,8,256]{2,1,0:T(8,128)S(1)}, f32[8,8,256]{2,1,0:T(8,128)S(1)}, u32[]{:S(2)}, u32[]{:S(2)}) collective-permute-start(f32[8,8,256]{2,1,0:T(8,128)S(1)} %get-tuple-element.65), channel_id=1, source_target_pairs={{128,0},{192,64},{0,128},{64,192},{129,1},{193,65},{1,129},{65,193... | collective-permute-start | bytes 196616 | tf_op jit(solution)/shard_map/ppermute | solution.py:480
  67.9 6.9 %collective-permute-start.20 = (f32[8,8,256]{2,1,0:T(8,128)S(1)}, f32[8,8,256]{2,1,0:T(8,128)S(1)}, u32[]{:S(2)}, u32[]{:S(2)}) collective-permute-start(f32[8,8,256]{2,1,0:T(8,128)S(1)} %get-tuple-element.65), channel_id=1, source_target_pairs={{64,0},{128,64},{192,128},{0,192},{65,1},{129,65},{193,129},{1,193... | collective-permute-start | bytes 196616 | tf_op jit(solution)/shard_map/ppermute | solution.py:480
  69.3 5.5 %collective-permute-start.19 = (f32[8,8,256]{2,1,0:T(8,128)S(1)}, f32[8,8,256]{2,1,0:T(8,128)S(1)}, u32[]{:S(2)}, u32[]{:S(2)}) collective-permute-start(f32[8,8,256]{2,1,0:T(8,128)S(1)} %get-tuple-element.65), channel_id=1, source_target_pairs={{192,0},{0,64},{64,128},{128,192},{193,1},{1,65},{65,129},{129,193... | collective-permute-start | bytes 196616 | tf_op jit(solution)/shard_map/ppermute | solution.py:480
  74.8 8.9 %collective-permute-start.22 = (f32[30,8,256]{2,1,0:T(8,128)S(1)}, f32[30,8,256]{2,1,0:T(8,128)S(1)}, u32[]{:S(2)}, u32[]{:S(2)}) collective-permute-start(f32[30,8,256]{2,1,0:T(8,128)S(1)} %slice_dynamic-update-slice_fusion.r2x), channel_id=1, source_target_pairs={{8,0},{16,8},{24,16},{32,24},{40,32},{48,40},{56,48},{0,56},{9,1},... | collective-permute-start | bytes 737288 | tf_op jit(solution)/shard_map/ppermute | solution.py:480
  74.9 8.8 %collective-permute-start.21 = (f32[30,8,256]{2,1,0:T(8,128)S(1)}, f32[30,8,256]{2,1,0:T(8,128)S(1)}, u32[]{:S(2)}, u32[]{:S(2)}) collective-permute-start(f32[30,8,256]{2,1,0:T(8,128)S(1)} %slice_dynamic-update-slice_fusion.r2x), channel_id=1, source_target_pairs={{56,0},{0,8},{8,16},{16,24},{24,32},{32,40},{40,48},{48,56},{57,1}... | collective-permute-start | bytes 737288 | tf_op jit(solution)/shard_map/ppermute | solution.py:480
  75.4 6.5 %collective-permute-start.24 = (f32[30,3,256]{2,1,0:T(4,128)S(1)}, f32[30,3,256]{2,1,0:T(4,128)S(1)}, u32[]{:S(2)}, u32[]{:S(2)}) collective-permute-start(f32[30,3,256]{2,1,0:T(4,128)S(1)} %get-tuple-element.83), channel_id=1, source_target_pairs={{16,0},{24,8},{32,16},{40,24},{48,32},{56,40},{0,48},{8,56},{17,1}... | collective-permute-start | bytes 276488 | tf_op jit(solution)/shard_map/ppermute | solution.py:480
  76.2 7.5 %collective-permute-start.23 = (f32[30,3,256]{2,1,0:T(4,128)S(1)}, f32[30,3,256]{2,1,0:T(4,128)S(1)}, u32[]{:S(2)}, u32[]{:S(2)}) collective-permute-start(f32[30,3,256]{2,1,0:T(4,128)S(1)} %get-tuple-element.84), channel_id=1, source_target_pairs={{48,0},{56,8},{0,16},{8,24},{16,32},{24,40},{32,48},{40,56},{49,1}... | collective-permute-start | bytes 276488 | tf_op jit(solution)/shard_map/ppermute | solution.py:480
  92.4 4.8 %collective-permute-start.28 = (f32[1,128]{1,0:T(1,128)S(1)}, f32[1,128]{1,0:T(1,128)S(1)}, u32[]{:S(2)}, u32[]{:S(2)}) collective-permute-start(f32[1,128]{1,0:T(1,128)S(1)} %add.33), channel_id=1, source_target_pairs={{192,0},{128,64},{64,128},{0,192},{193,1},{129,65},{65,129},{1,193... | collective-permute-start | bytes 1544 | tf_op jit(solution)/shard_map/ppermute | solution.py:484
  93.9 5.0 %collective-permute-start.27 = (f32[1,128]{1,0:T(1,128)S(1)}, f32[1,128]{1,0:T(1,128)S(1)}, u32[]{:S(2)}, u32[]{:S(2)}) collective-permute-start(f32[1,128]{1,0:T(1,128)S(1)} %add.33), channel_id=1, source_target_pairs={{128,0},{192,64},{0,128},{64,192},{129,1},{193,65},{1,129},{65,193... | collective-permute-start | bytes 1544 | tf_op jit(solution)/shard_map/ppermute | solution.py:484
  94.0 5.0 %collective-permute-start.26 = (f32[1,128]{1,0:T(1,128)S(1)}, f32[1,128]{1,0:T(1,128)S(1)}, u32[]{:S(2)}, u32[]{:S(2)}) collective-permute-start(f32[1,128]{1,0:T(1,128)S(1)} %add.33), channel_id=1, source_target_pairs={{64,0},{0,64},{192,128},{128,192},{65,1},{1,65},{193,129},{129,193... | collective-permute-start | bytes 1544 | tf_op jit(solution)/shard_map/ppermute | solution.py:484
  98.9 4.8 %collective-permute-start.31 = (f32[1,128]{1,0:T(1,128)S(1)}, f32[1,128]{1,0:T(1,128)S(1)}, u32[]{:S(2)}, u32[]{:S(2)}) collective-permute-start(f32[1,128]{1,0:T(1,128)S(1)} %add_add_fusion.2), channel_id=1, source_target_pairs={{48,0},{56,8},{32,16},{40,24},{16,32},{24,40},{0,48},{8,56},{49,1}... | collective-permute-start | bytes 1544 | tf_op jit(solution)/shard_map/ppermute | solution.py:484
  100.1 5.0 %collective-permute-start.30 = (f32[1,128]{1,0:T(1,128)S(1)}, f32[1,128]{1,0:T(1,128)S(1)}, u32[]{:S(2)}, u32[]{:S(2)}) collective-permute-start(f32[1,128]{1,0:T(1,128)S(1)} %add_add_fusion.2), channel_id=1, source_target_pairs={{32,0},{40,8},{48,16},{56,24},{0,32},{8,40},{16,48},{24,56},{33,1}... | collective-permute-start | bytes 1544 | tf_op jit(solution)/shard_map/ppermute | solution.py:484
  105.1 4.8 %collective-permute-start.34 = (f32[1,128]{1,0:T(1,128)S(1)}, f32[1,128]{1,0:T(1,128)S(1)}, u32[]{:S(2)}, u32[]{:S(2)}) collective-permute-start(f32[1,128]{1,0:T(1,128)S(1)} %add_add_fusion.1), channel_id=1, source_target_pairs={{3,0},{2,1},{1,2},{0,3},{7,4},{6,5},{5,6},{4,7},{11,8},{10,9},{9,1... | collective-permute-start | bytes 1544 | tf_op jit(solution)/shard_map/ppermute | solution.py:484
  107.5 4.4 %collective-permute-start.33 = (f32[1,128]{1,0:T(1,128)S(1)}, f32[1,128]{1,0:T(1,128)S(1)}, u32[]{:S(2)}, u32[]{:S(2)}) collective-permute-start(f32[1,128]{1,0:T(1,128)S(1)} %add_add_fusion.1), channel_id=1, source_target_pairs={{2,0},{3,1},{0,2},{1,3},{6,4},{7,5},{4,6},{5,7},{10,8},{11,9},{8,1... | collective-permute-start | bytes 1544 | tf_op jit(solution)/shard_map/ppermute | solution.py:484
  113.4 6.5 %collective-permute-start.35 = (f32[1,128]{1,0:T(1,128)S(1)}, f32[1,128]{1,0:T(1,128)S(1)}, u32[]{:S(2)}, u32[]{:S(2)}) collective-permute-start(f32[1,128]{1,0:T(1,128)S(1)} %add_add_fusion), channel_id=1, source_target_pairs={{7,0},{6,1},{5,2},{4,3},{3,4},{2,5},{1,6},{0,7},{15,8},{14,9},{13,... | collective-permute-start | bytes 1544 | tf_op jit(solution)/shard_map/ppermute | solution.py:484
  (7 other events, 70.3 us)

commit v3 on v2

--- a/solution.py
+++ b/solution.py
@@ -12,6 +12,7 @@
 H0, H1, H2, H3 = 4, 5, 11, 4
 S0, S1, S2, S3 = 1.0, 0.25, 0.0625, 0.015625
 SLOT = 40
+TAILS = {1: (0, 28), 2: (56, 20), 3: (96, 12), 4: (120, 4)}
 
 
 def place_0(p):
@@ -131,18 +132,105 @@
         dst[p:q] = times(mid, matrix) + right(p, q) + side[p:q] * near
 
 
-def prepare_kernel(data, own, first, last, low, high):
+def pack_lanes(planes, height, width, count, to_left, to_right):
+    lane = rows((height, 128), 1)
+    for g in range(-(-len(planes) // 3)):
+        left, right = None, None
+        for i, value in enumerate(planes[3 * g : 3 * g + 3]):
+            a = pltpu.roll(value, SLOT * i, 1) if i else value
+            b = pltpu.roll(value, (SLOT * i + width - count) % 128, 1)
+            left = a if i == 0 else jnp.where(lane < SLOT * i, left, a)
+            right = b if i == 0 else jnp.where(lane < SLOT * i, right, b)
+        to_left[g] = left
+        to_right[g] = right
+
+
+def prepare_kernel(data, weights, own, to_left, to_right):
     own[...] = data[...]
-    first[...] = data[:H0]
-    last[...] = data[32 - H0 :]
-    low[...] = data[:, :H0]
-    high[...] = data[:, 32 - H0 :]
+    pack_lanes([data[p] for p in range(32)], 32, 36, 128, to_left, to_right)
+    for out in (to_left, to_right):
+        out[11] = jnp.concatenate([weights[...], jnp.zeros((24, 128), F32)], axis=0)
+
+
+def spread_0_kernel(own, from_right, from_left, tail, first, last):
+    lane = rows((32, 128), 1)
+    packed = [jnp.zeros((32, 128), F32)] * 2
+    for p in range(32):
+        group, i = divmod(p, 3)
+        right = pltpu.roll(from_right[group], 128 - SLOT * i, 1) if i else from_right[group]
+        left = pltpu.roll(from_left[group], (92 - SLOT * i) % 128, 1)
+        value = jnp.where(lane < 36, right, jnp.where(lane >= 92, left, 0.0))
+        tail[p] = value
+        for side, far in ((0, p + 1), (1, 32 - p)):
+            if far <= H0:
+                begin, reach = TAILS[far]
+                moved = pltpu.roll(value, begin + reach, 1)
+                packed[side] = jnp.where((lane >= begin) & (lane < begin + 2 * reach), moved, packed[side])
+    first[:H0] = own[:H0]
+    first[H0] = packed[0]
+    last[:H0] = own[32 - H0 :]
+    last[H0] = packed[1]
+
+
+def edges_0_kernel(own, tail, xlo, xhi, low, high):
+    lane = rows((4, 128), 1)
+
+    def ends(ref, p):
+        value = ref[p]
+        return value[:H0], value[32 - H0 :]
+
+    def tails(p):
+        if H0 <= p < 32 + H0:
+            return ends(tail, p - H0)
+        source = xlo if p < H0 else xhi
+        begin, reach = TAILS[H0 - p if p < H0 else p - 31 - H0]
+        out = []
+        for value in ends(source, H0):
+            moved = pltpu.roll(value, (128 - begin - reach) % 128, 1)
+            out.append(jnp.where((lane < reach) | (lane >= 128 - reach), moved, 0.0))
+        return out
+
+    kept = None
+    for p in range(40):
+        if p < H0:
+            a, b = ends(xlo, p)
+        elif p < 32 + H0:
+            a, b = ends(own, p - H0)
+        else:
+            a, b = ends(xhi, p - 32 - H0)
+        low[p] = a
+        high[p] = b
+        moved = [pltpu.roll(v, 28 if p % 2 == 0 else 92, 1) for v in tails(p)]
+        if p % 2 == 0:
+            kept = moved
+        else:
+            low[40 + p // 2] = jnp.where(lane < 64, kept[0], moved[0])
+            high[40 + p // 2] = jnp.where(lane < 64, kept[1], moved[1])
+
+
+def gather_0_kernel(own, tail, xlo, xhi, field):
+    ix = lax.axis_index("gx")
+    lane = rows((32, 128), 1)
+    for p in range(40):
+        if H0 <= p < 32 + H0:
+            field[p, 4:36, :128] = own[p - H0]
+            field[p, 4:36, 128:] = tail[p - H0]
+        else:
+            source, q = (xlo, p) if p < H0 else (xhi, p - 32 - H0)
+            begin, reach = TAILS[H0 - p if p < H0 else p - 31 - H0]
+            xr = ix * 32 + p - H0
+            ok = jnp.where((xr >= 0) & (xr < NX), 1.0, 0.0)
+            moved = pltpu.roll(source[H0], (128 - begin - reach) % 128, 1)
+            field[p, 4:36, :128] = source[q] * ok
+            field[p, 4:36, 128:] = jnp.where((lane < reach) | (lane >= 128 - reach), moved, 0.0) * ok
+        field[p, :4] = jnp.zeros((4, 256), F32)
+        field[p, 36:] = jnp.zeros((4, 256), F32)
 
 
 def weights_0_kernel(left, own, right, b0, k0, m0, f0):
     iz = lax.axis_index("gz")
     lane = rows((8, 128), 1)
-    laid = jnp.concatenate([own[...], jnp.where(lane < 64, right[14, :8], left[14, :8])], axis=1)
+    laid = jnp.concatenate([own[...], jnp.where(lane < 64, right[11, :8], left[11, :8])], axis=1)
     band, op, step, factor = operators(laid, place_0, iz, 0, 36, S0)
     b0[...] = thrice(jnp.transpose(band))
     k0[...] = thrice(step)
@@ -152,7 +240,7 @@
 
 def weights_1_kernel(left, own, right, k1, k1u, m1, f1):
     iz = lax.axis_index("gz")
-    wide = jnp.concatenate([left[14, :8], own[...], right[14, :8]], axis=1)
+    wide = jnp.concatenate([left[11, :8], own[...], right[11, :8]], axis=1)
     mean = jnp.where((rows((384, 256), 0) - 128) >> 1 == place_1(rows((384, 256), 1)), 0.5, 0.0)
     band, op, step, factor = operators(exact(wide, mean), place_1, iz, 1, 41, S1)
     k1[...] = thrice(step[:, :128])
@@ -161,62 +249,58 @@
     f1[...] = jnp.broadcast_to(factor, (8, 256))
 
 
-def pack_kernel(width, reach, count, n, data, xlo, xhi, ylo, yhi, extra, full, to_left, to_right):
-    def plane(p):
-        if p >= n + 2 * reach:
-            return jnp.zeros(full.shape[1:], F32)
-        if p < reach:
-            mid = xlo[p]
-        elif p < reach + n:
-            mid = data[p - reach]
+def spread_1_kernel(own, from_right, from_left, main, rest, first, last):
+    lane = rows((16, 128), 1)
+    for p in range(16):
+        group, i = divmod(p, 3)
+        right = pltpu.roll(from_right[group], (64 - SLOT * i) % 128, 1)
+        left = pltpu.roll(from_left[group], (91 - SLOT * i) % 128, 1)
+        one = jnp.where(lane < 64, own[p], jnp.where(lane < 101, right, 0.0))
+        two = jnp.where(lane >= 91, left, 0.0)
+        main[p] = jnp.where(lane < 96, one, two)
+        rest[p] = jnp.where(lane < 96, two, one)
+    first[:H1] = main[:H1]
+    first[H1] = rest[0]
+    last[:H1] = main[16 - H1 :]
+    last[H1] = rest[15]
+
+
+def edges_1_kernel(main, rest, xlo, xhi, low, high):
+    for p in range(26):
+        if p < H1:
+            value, tail = xlo[p], xlo[H1] if p == H1 - 1 else None
+        elif p < 16 + H1:
+            value, tail = main[p - H1], rest[p - H1]
         else:
-            mid = xhi[p - reach - n]
-        parts = [ylo[p], mid, yhi[p]]
-        rest = full.shape[1] - n - 2 * reach
-        if rest:
-            parts.append(jnp.zeros((rest, count), F32))
-        out = jnp.concatenate(parts, axis=0)
-        if count < 128:
-            out = jnp.concatenate([out, jnp.zeros((full.shape[1], 128 - count), F32)], axis=1)
-        return out
-
-    lane = rows(full.shape[1:], 1)
-    groups = to_left.shape[0]
-    if extra is not None:
-        groups -= 1
-        for out in (to_left, to_right):
-            out[groups] = jnp.zeros(full.shape[1:], F32)
-            out[groups, :8] = extra[...]
-    for g in range(groups):
-        left, right = None, None
-        for i in range(3):
-            p = 3 * g + i
-            value = plane(p)
-            if p < full.shape[0]:
-                full[p] = value
-            a = pltpu.roll(value, SLOT * i, 1) if i else value
-            b = pltpu.roll(value, (SLOT * i + width - count) % 128, 1)
-            left = a if i == 0 else jnp.where(lane < SLOT * i, left, a)
-            right = b if i == 0 else jnp.where(lane < SLOT * i, right, b)
-        to_left[g] = left
-        to_right[g] = right
-
-
-def down_0_kernel(dxy, from_right, from_left, b0, k0, m0, f0, r1, r1_top, r1_bottom, e_out, r_out, stat, d, e0, side, g, gx):
+            value, tail = xhi[p - 16 - H1], xhi[H1] if p == 16 + H1 else None
+        low[p, :H1] = value[:H1]
+        high[p, :H1] = value[16 - H1 :]
+        none = jnp.zeros((8 - H1, 128), F32)
+        low[p, H1:] = none
+        high[p, H1:] = none
+        if tail is not None:
+            low[p, H1 : H1 + 1] = tail[0:1]
+            high[p, H1 : H1 + 1] = tail[15:16]
+
+
+def down_0_kernel(
+    field, ylo, yhi, b0, k0, m0, f0, r1, to_left, to_right, e_out, r_out, stat, d, e0, side, g, gx
+):
     ix, iy, iz = lax.axis_index("gx"), lax.axis_index("gy"), lax.axis_index("gz")
-    lane = rows((40, 128), 1)
+    low_ok = jnp.where(iy > 0, 1.0, 0.0)
+    high_ok = jnp.where(iy < 7, 1.0, 0.0)
+    y = iy * 32 + rows((40, 256), 0) - H0
+    column = jnp.where((y >= 0) & (y < NY), f0[0:1, :] * S0, 0.0)
+    lane = rows((4, 128), 1)
     for p in range(40):
-        group, i = divmod(p, 3)
         xr = ix * 32 + p - H0
-        y = iy * 32 + rows((40, 128), 0) - H0
-        ok = jnp.where((y >= 0) & (y < NY), jnp.where((xr >= 0) & (xr < NX), 1.0, 0.0), 0.0)
-        right = pltpu.roll(from_right[group], (128 - SLOT * i) % 128, 1) if i else from_right[group]
-        left = pltpu.roll(from_left[group], (92 - SLOT * i) % 128, 1)
-        d[p, :, :128] = dxy[p] * ok
-        d[p, :, 128:] = jnp.where(lane < 36, right, jnp.where(lane >= 92, left, 0.0)) * ok
-        fs = f0[0:1, :] * S0
-        side[p, :, :128] = ok * fs[:, :128]
-        side[p, :, 128:] = ok * fs[:, 128:]
+        ok = jnp.where((xr >= 0) & (xr < NX), 1.0, 0.0)
+        d[p, 4:36] = field[p, 4:36]
+        for edge, part, good in ((ylo, slice(0, 4), low_ok), (yhi, slice(36, 40), high_ok)):
+            moved = pltpu.roll(edge[40 + p // 2], 100 if p % 2 == 0 else 36, 1)
+            d[p, part, :128] = edge[p] * (ok * good)
+            d[p, part, 128:] = jnp.where((lane < 28) | (lane >= 100), moved, 0.0) * (ok * good)
+        side[p] = column * ok
     factor = f0[0:1, :].reshape(1, 1, 256)
     for p, q in chunks(0, 40, 8):
         r = times(d[p:q], b0[...])
@@ -246,29 +330,31 @@
     ]
     gy = ((gy[0] + gy[3]) + 3.0 * (gy[1] + gy[2])) * 0.125
     fold = restrict_matrix(place_0, 256, lambda q: q, 128, iz, 0, 36)
-    out = times_exact(gy, fold)[:, :, :64]
+    out = times_exact(gy, fold)
     r1[...] = out
-    r1_top[...] = out[:, 16 - H1 :]
-    r1_bottom[...] = out[:, :H1]
-
-
-def down_1_kernel(rxy, from_right, from_left, k1, m1, f1, w, msg, e_out, r_out, stat, e0, e0b, side, g, gx):
+    pack_lanes([out[i] for i in range(16)], 16, 37, 64, to_left, to_right)
+
+
+def down_1_kernel(wide, tail, xlo, xhi, ylo, yhi, k1, m1, f1, w, msg, e_out, r_out, stat, e0, e0b, side, g, gx):
     ix, iy, iz = lax.axis_index("gx"), lax.axis_index("gy"), lax.axis_index("gz")
     lane = rows((32, 128), 1)
+    yrow = rows((32, 128), 0)
+    y = iy * 16 + yrow - H1
+    inner = jnp.where((y >= 0) & (y < NY // 2) & (yrow < 26), 1.0, 0.0)
     for p in range(26):
-        group, i = divmod(p, 3)
         xr = ix * 16 + p - H1
-        yrow = rows((32, 128), 0)
-        y = iy * 16 + yrow - H1
-        ok = jnp.where(
-            (y >= 0) & (y < NY // 2) & (yrow < 26), jnp.where((xr >= 0) & (xr < NX // 2), 1.0, 0.0), 0.0
-        )
-        right = pltpu.roll(from_right[group], (64 - SLOT * i) % 128, 1)
-        left = pltpu.roll(from_left[group], (91 - SLOT * i) % 128, 1)
-        first = jnp.where(lane < 64, rxy[p], jnp.where(lane < 101, right, 0.0))
-        second = jnp.where(lane >= 91, left, 0.0)
-        main = jnp.where(lane < 96, first, second) * ok
-        rest = jnp.where(lane < 96, second, first) * ok
+        ok = inner * jnp.where((xr >= 0) & (xr < NX // 2), 1.0, 0.0)
+        if p < H1:
+            value, extra = xlo[p], xlo[H1] if p == H1 - 1 else jnp.zeros((16, 128), F32)
+        elif p < 16 + H1:
+            value, extra = wide[p - H1], tail[p - H1]
+        else:
+            value, extra = xhi[p - 16 - H1], xhi[H1] if p == 16 + H1 else jnp.zeros((16, 128), F32)
+        main = jnp.concatenate([ylo[p, :H1], value, yhi[p, :H1], jnp.zeros((6, 128), F32)], axis=0) * ok
+        rest = jnp.concatenate(
+            [jnp.zeros((4, 128), F32), ylo[p, H1 : H1 + 1], extra, yhi[p, H1 : H1 + 1], jnp.zeros((10, 128), F32)],
+            axis=0,
+        ) * ok
         r_out[p] = main
         e0[p] = main * f1[0:1, :128]
         e0b[p] = rest * f1[0:1, 128:]
@@ -297,20 +383,45 @@
     gy = [gx[:, pl.ds(4 + a, 8, stride=2), :] for a in range(4)]
     gy = ((gy[0] + gy[3]) + 3.0 * (gy[1] + gy[2])) * 0.125
     fold = restrict_matrix(place_1, 128, lambda q: q, 128, iz, 1, 32)
-    msg[:8] = times_exact(gy, fold)[:, :, :32]
+    out = times_exact(gy, fold)[:, :, :32]
+    for k in range(2):
+        msg[k] = jnp.concatenate([out[4 * k + i] for i in range(4)], axis=1)
     mean = jnp.where(rows((128, 128), 0) >> 2 == rows((128, 128), 1), 0.25, 0.0)
-    msg[8] = exact(w[...], mean)[:, :32]
-
-
-def join_kernel(own, r1, r2, r3, l3, l2, l1, field, w):
-    first = jnp.concatenate([own[...], r1[...], r2[...], r3[...]], axis=2)
-    second = jnp.concatenate([jnp.zeros((9, 8, 32), F32), l3[...], l2[...], l1[...]], axis=2)
-    lane = rows((9, 8, 128), 2)
-    main, rest = jnp.where(lane < 80, first, second), jnp.where(lane < 80, second, first)
-    field[:, :, :128] = main[:8]
-    field[:, :, 128:] = rest[:8]
-    w[:, :128] = main[8]
-    w[:, 128:] = rest[8]
+    msg[2] = exact(w[...], mean)
+
+
+def join_kernel(own, r1, r2, r3, l3, l2, l1, both, w):
+    lane = rows((8, 128), 1)
+    blocks = (own, r1, r2, r3), (None, l3, l2, l1)
+    for p in range(9):
+        k, i = divmod(p, 4)
+        part = slice(32 * i, 32 * i + 32)
+        first, second = (
+            jnp.concatenate([jnp.zeros((8, 32), F32) if b is None else b[k, :, part] for b in group], axis=1)
+            for group in blocks
+        )
+        main, rest = jnp.where(lane < 80, first, second), jnp.where(lane < 80, second, first)
+        if p < 8:
+            both[p] = main
+            both[8 + p] = rest
+        else:
+            w[:, :128] = main
+            w[:, 128:] = rest
+
+
+def edges_2_kernel(own, x1, x2, x3, near, low, high):
+    near[:3] = x2[5:]
+    near[3:11] = x3[:8]
+    near[11:19] = own[:8]
+    near[19:27] = x1[:8]
+    near[27:30] = x2[:3]
+    near[30:36] = x3[10:]
+    near[36:44] = own[8:]
+    near[44:50] = x1[8:14]
+    for i in range(18):
+        value = near[i + 6]
+        low[i] = value[:3]
+        high[i] = value[5:]
 
 
 def weights_2_kernel(w2, k2, k2u, m2, f2, k3, f3):
@@ -330,7 +441,7 @@
     r2x, ya, yb, yc, yd, k2, k2u, m2, f2, k3, f3,
     k1, f1, e1s, r1s, k0, m0, f0, e0s, r0s, stat0, stat1,
     sol, res, stat,
-    ra, ea, eb, side2, gx2, r3, e3, side3, c3, cy2, ua, ub, side1, cy1, va, vb, side0, cy0, sol_v, res_v, sems,
+    ra, ea, eb, side2, gx2, r3, e3, side3, c3, cy2, ua, ub, side1, cy1, va, vb, side0, cy0,
 ):
     ix, iy, iz = lax.axis_index("gx"), lax.axis_index("gy"), lax.axis_index("gz")
     lane = rows((32, 128), 1)
@@ -341,8 +452,14 @@
         ok = jnp.where(
             (y >= 0) & (y < NY // 4) & (yrow < 30), jnp.where((xr >= 0) & (xr < NX // 4), 1.0, 0.0), 0.0
         )
-        full = jnp.concatenate([yc[p], ya[p], r2x[p], yb[p], yd[p], jnp.zeros((2, 256), F32)], axis=0)
-        main, rest = full[:, :128] * ok, full[:, 128:] * ok
+        three, two = jnp.zeros((3, 128), F32), jnp.zeros((2, 128), F32)
+        far = 6 <= p < 24
+        main = jnp.concatenate(
+            [yc[p - 6] if far else three, ya[p], r2x[p], yb[p], yd[p - 6] if far else three, two], axis=0
+        ) * ok
+        rest = jnp.zeros((32, 128), F32)
+        if 5 <= p < 25:
+            rest = jnp.concatenate([three, ya[p + 25], r2x[p + 25], yb[p + 25], three, two], axis=0) * ok
         ra[p, :, :128] = main
         ra[p, :, 128:] = rest
         ea[p, :, :128] = main * f2[0:1, :128]
@@ -451,7 +568,6 @@
     relax(vb, va, 3, 37, 9, k0[...], lambda p, q: fr0 * r0s[p:q], side0)
     total = jnp.zeros((32, 128), F32)
     last = m0[:, :128]
-    sends = []
     for p, q in chunks(4, 36, 8):
         mid = va[p:q]
         flat = va[p:q, :, :128]
@@ -460,17 +576,20 @@
         )
         value = (r0s[p:q, :, :128] - times(mid, last) + S0 * near)[:, 4:36]
         part = slice(p - 4, q - 4)
-        res_v[part] = value
-        sol_v[part] = va[p:q, 4:36, :128]
+        res[part] = value
+        sol[part] = va[p:q, 4:36, :128]
         total = total + jnp.sum(value * value, axis=0)
-        for i, (src, dst) in enumerate(((sol_v, sol), (res_v, res))):
-            sends.append(pltpu.make_async_copy(src.at[part], dst.at[part], sems.at[i, p // 8]))
-            sends[-1].start()
     sum3 = jnp.sum(total)
     tile = rows((1, 128), 1)
     stat[...] = jnp.where(
         tile == 0, stat0[0:1], jnp.where(tile == 1, stat1[0:1], jnp.where(tile == 2, sum2, jnp.where(tile == 3, sum3, 0.0)))
     )
+
+
+def store_kernel(a, b, a_out, b_out, sems):
+    sends = [pltpu.make_async_copy(x, y, sems.at[i]) for i, (x, y) in enumerate(((a, a_out), (b, b_out)))]
+    for send in sends:
+        send.start()
     for send in sends:
         send.wait()
 
@@ -496,9 +615,9 @@
     return pltpu.VMEM(shape, F32)
 
 
-def call(kernel, outs, scratches, name, limit=16, away=()):
+def call(kernel, outs, scratches, name, limit=16, away=(), home=()):
     def run(*operands):
-        operands = [x if x is None else pltpu.with_memory_space_constraint(x, pltpu.VMEM) for x in operands]
+        operands = [x if i in home else pltpu.with_memory_space_constraint(x, pltpu.VMEM) for i, x in enumerate(operands)]
         return pl.pallas_call(
             kernel,
             out_shape=[jax.ShapeDtypeStruct(o.shape, F32) if i in away else o for i, o in enumerate(outs)],
@@ -512,36 +631,18 @@
     return run
 
 
-def pack(width, reach, count, n, height, groups, parts, extra, name):
-    def kernel(*refs):
-        if extra is None:
-            refs = refs[:5] + (None,) + refs[5:]
-        pack_kernel(width, reach, count, n, *refs)
-
-    outs = [f32(n + 2 * reach, height, 128), f32(groups, height, 128), f32(groups, height, 128)]
-    return call(kernel, outs, [], name)(*parts, *(() if extra is None else (extra,)))
-
-
-def sides(block, first, last, low, high, reach):
-    n = block.shape[0]
-    xlo = shift(last, "gx", -1)
-    xhi = shift(first, "gx", 1)
-    top = jnp.concatenate([xlo[:, n - reach :], high, xhi[:, n - reach :]], axis=0)
-    bottom = jnp.concatenate([xlo[:, :reach], low, xhi[:, :reach]], axis=0)
-    return block, xlo, xhi, shift(top, "gy", -1), shift(bottom, "gy", 1)
-
-
 def body(data, weights):
-    slab = f32(H0, 32, 128), f32(H0, 32, 128), f32(32, H0, 128), f32(32, H0, 128)
-    start = pl.pallas_call(
-        prepare_kernel,
-        out_shape=[f32(32, 32, 128), *slab],
-        in_specs=[pl.BlockSpec(memory_space=pltpu.VMEM)],
-        out_specs=[pl.BlockSpec(memory_space=pltpu.VMEM)] * 5,
-        name="prepare",
-    )(data)
-    dxy, to_left, to_right = pack(36, H0, 128, 32, 40, 15, sides(*start, H0), weights, "pack_data")
+    own, to_left, to_right = call(
+        prepare_kernel, [f32(32, 32, 128), f32(12, 32, 128), f32(12, 32, 128)], [], "prepare", home=(0, 1)
+    )(data, weights)
     from_right, from_left = shift(to_left, "gz", 1), shift(to_right, "gz", -1)
+    tail, first, last = call(
+        spread_0_kernel, [f32(32, 32, 128), f32(5, 32, 128), f32(5, 32, 128)], [], "spread_0"
+    )(own, from_right, from_left)
+    xlo, xhi = shift(last, "gx", -1), shift(first, "gx", 1)
+    low, high = call(edges_0_kernel, [f32(60, 4, 128), f32(60, 4, 128)], [], "edges_0")(own, tail, xlo, xhi)
+    ylo, yhi = shift(high, "gy", -1), shift(low, "gy", 1)
+    (field,) = call(gather_0_kernel, [f32(40, 40, 256)], [], "gather_0")(own, tail, xlo, xhi)
     b0, k0, m0, f0 = call(
         weights_0_kernel, [bf16(768, 256), bf16(768, 256), bf16(768, 256), f32(8, 256)], [], "weights_0"
     )(from_left, weights, from_right)
@@ -549,25 +650,28 @@
         weights_1_kernel, [bf16(768, 128), bf16(384, 128), bf16(384, 128), f32(8, 256)], [], "weights_1"
     )(from_left, weights, from_right)
     big = (40, 40, 256)
-    r1, r1_top, r1_bottom, e0s, r0s, stat0 = call(
+    r1, to_left, to_right, e0s, r0s, stat0 = call(
         down_0_kernel,
-        [f32(16, 16, 64), f32(16, H1, 64), f32(16, H1, 64), f32(*big), f32(*big), f32(8, 128)],
+        [f32(16, 16, 128), f32(6, 16, 128), f32(6, 16, 128), f32(*big), f32(*big), f32(8, 128)],
         [scratch(*big), scratch(*big), scratch(*big), scratch(*big), scratch(16, 2, 40, 128)],
         "down_0",
-    )(dxy, from_right, from_left, b0, k0, m0, f0)
-    rxy, to_left, to_right = pack(
-        37, H1, 64, 16, 32, 9, sides(r1, r1[:H1], r1[16 - H1 :], r1_bottom, r1_top, H1), None, "pack_r1"
-    )
+    )(field, ylo, yhi, b0, k0, m0, f0)
     from_right, from_left = shift(to_left, "gz", 1), shift(to_right, "gz", -1)
+    wide1, tail1, first, last = call(
+        spread_1_kernel, [f32(16, 16, 128), f32(16, 16, 128), f32(6, 16, 128), f32(6, 16, 128)], [], "spread_1"
+    )(r1, from_right, from_left)
+    xlo, xhi = shift(last, "gx", -1), shift(first, "gx", 1)
+    low, high = call(edges_1_kernel, [f32(26, 8, 128), f32(26, 8, 128)], [], "edges_1")(wide1, tail1, xlo, xhi)
+    ylo, yhi = shift(high, "gy", -1), shift(low, "gy", 1)
     mid = (26, 32, 128)
     msg, e1s, r1s, stat1 = call(
         down_1_kernel,
-        [f32(9, 8, 32), f32(*mid), f32(*mid), f32(8, 128)],
+        [f32(3, 8, 128), f32(*mid), f32(*mid), f32(8, 128)],
         [scratch(*mid), scratch(*mid), scratch(*mid), scratch(*mid), scratch(8, 32, 128)],
         "down_1",
-    )(rxy, from_right, from_left, k1, m1, f1, weights)
+    )(wide1, tail1, xlo, xhi, ylo, yhi, k1, m1, f1, weights)
     near = {k: shift(msg, "gz", k) for k in (1, -1, 2, -2, 3, -3)}
-    r2z, wide2 = call(join_kernel, [f32(8, 8, 256), f32(8, 256)], [], "join")(
+    r2z, wide2 = call(join_kernel, [f32(16, 8, 128), f32(8, 256)], [], "join")(
         msg, near[1], near[2], near[3], near[-3], near[-2], near[-1]
     )
     k2, k2u, m2, f2, k3, f3 = call(
@@ -575,10 +679,12 @@
         [bf16(768, 256), bf16(384, 128), bf16(768, 256), f32(8, 256), bf16(384, 128), f32(8, 128)],
         [], "weights_coarse",
     )(wide2)
-    x1, x2, x3 = (shift(r2z, "gx", k) for k in (1, 2, 3))
-    r2x = jnp.concatenate([x2[5:], x3, r2z, x1, x2[:3]], axis=0)
+    x1, x2, x3 = shift(r2z, "gx", 1), shift(r2z[:8], "gx", 2), shift(r2z, "gx", 3)
+    r2x, low, high = call(edges_2_kernel, [f32(50, 8, 128), f32(18, 3, 128), f32(18, 3, 128)], [], "edges_2")(
+        r2z, x1, x2, x3
+    )
     ya, yb = shift(r2x, "gy", -1), shift(r2x, "gy", 1)
-    yc, yd = shift(r2x[:, 5:], "gy", -2), shift(r2x[:, :3], "gy", 2)
+    yc, yd = shift(high, "gy", -2), shift(low, "gy", 2)
     lev2 = (30, 32, 256)
     sol, res, stat = call(
         up_kernel,
@@ -587,10 +693,13 @@
             scratch(*lev2), scratch(*lev2), scratch(*lev2), scratch(*lev2), scratch(12, 2, 40, 128),
             scratch(14, 32, 128), scratch(12, 16, 128), scratch(12, 16, 128), scratch(12, 16, 128),
             scratch(12, 32, 128), scratch(*mid), scratch(*mid), scratch(*mid), scratch(14, 32, 128),
-            scratch(*big), scratch(*big), scratch(*big), scratch(20, 2, 40, 128), scratch(32, 32, 128), scratch(32, 32, 128), pltpu.SemaphoreType.DMA((2, 5)),
+            scratch(*big), scratch(*big), scratch(*big), scratch(20, 2, 40, 128),
         ],
-        "up", 24, (0, 1),
+        "up", 24,
     )(r2x, ya, yb, yc, yd, k2, k2u, m2, f2, k3, f3, k1u, f1, e1s, r1s, k0, m0, f0, e0s, r0s, stat0, stat1)
+    sol, res = call(
+        store_kernel, [f32(32, 32, 128), f32(32, 32, 128)], [pltpu.SemaphoreType.DMA((2,))], "store", 4, (0, 1)
+    )(sol, res)
     t = stat
     for axis, flips in (("gy", (1,)), ("gx", (1, 2, 3)), ("gy", (2, 4, 6)), ("gz", (1, 2, 3)), ("gz", (7,))):
         others = [swap(t, axis, f) for f in flips]

time: 121 us -> 114 us (0.942)
  waiting for transfers between devices: 51.4 us -> 40.4 us
  starting transfers between devices: 50.9 us -> 54.5 us
    ppermute x25, waiting for transfers between devices: 40 us -> 28.4 us  [shift(): return lax.ppermute(x, axis, [((i + k) % n, i) for i in range(n)])]
    ppermute x25, starting transfers between devices: 33.4 us -> 37.5 us  [shift(): return lax.ppermute(x, axis, [((i + k) % n, i) for i in range(n)])]
    pallas_call x9 -> x15, Pallas kernels: 14.9 us -> 15.8 us  [run(): pl.pallas_call(kernel, out_shape=[jax.ShapeDtypeStruct(o.shape, F32) if i...]
  transfers between devices with their start and end apart: 36 -> 36, of which waited for: 25 -> 23; matrix products, arithmetic and copies ran while one was open for 0% -> 0% of each run, Pallas kernels for 2% -> 3%
where the time goes in v3:
time: 114 us
  starting transfers between devices  54.5 us (48%)
  waiting for transfers between devices  40.4 us (35%)
  Pallas kernels  15.8 us (14%)
  local copies, waits for them, and re-layouts  1.73 us (2%)
    ppermute x25, starting transfers between devices, shift(): return lax.ppermute(x, axis, [((i + k) % n, i) for i in range(n)])  37.5 us
    ppermute x25, waiting for transfers between devices, shift(): return lax.ppermute(x, axis, [((i + k) % n, i) for i in range(n)])  28.4 us
    ppermute x11, starting transfers between devices, swap(): lax.ppermute(x, axis, [(i ^ flip, i) for i in range(lax.axis_size(axis))])  17 us
    pallas_call x15, Pallas kernels, run(): pl.pallas_call(kernel, out_shape=[jax.ShapeDtypeStruct(o.shape, F32) if i...  15.8 us
    ppermute x11, waiting for transfers between devices, swap(): lax.ppermute(x, axis, [(i ^ flip, i) for i in range(lax.axis_size(axis))])  12 us
  transfers between devices with their start and end apart: 36, of which 23 were waited for; matrix products, arithmetic and copies ran while one was open for 0% of the time, Pallas kernels for 3%

profile of v3, /device:TPU:32, one launch (start us, length us, event | category | flops | bytes accessed | tf_op | source)
XLA Modules:
  0.0 113.8 jit_solution(3997069390207135885)
XLA Ops:
  2.7 1.9 %collective-permute-start = (f32[12,32,128]{2,1,0:T(8,128)S(1)}, f32[12,32,128]{2,1,0:T(8,128)S(1)}, u32[]{:S(2)}, u32[]{:S(2)}) collective-permute-start(f32[12,32,128]{2,1,0:T(8,128)S(1)} %get-tuple-element.52), channel_id=1, source_target_pairs={{1,0},{2,1},{3,2},{4,3},{5,4},{6,5},{7,6},{0,7},{9,8},{10,9},{11,1... | collective-permute-start | bytes 589832 | tf_op jit(solution)/shard_map/ppermute | solution.py:599
  4.8 4.8 %collective-permute-done.from_right.right = f32[12,32,128]{2,1,0:T(8,128)S(1)} collective-permute-done((f32[12,32,128]{2,1,0:T(8,128)S(1)}, f32[12,32,128]{2,1,0:T(8,128)S(1)}, u32[]{:S(2)}, u32[]{:S(2)}) %collective-permute-start) | collective-permute-done | bytes 196640 | tf_op jit(solution)/shard_map/ppermute | solution.py:599
  9.5 3.8 %collective-permute-done.1.from_left.left = f32[12,32,128]{2,1,0:T(8,128)S(1)} collective-permute-done((f32[12,32,128]{2,1,0:T(8,128)S(1)}, f32[12,32,128]{2,1,0:T(8,128)S(1)}, u32[]{:S(2)}, u32[]{:S(2)}) %collective-permute-start.1) | collective-permute-done | bytes 196640 | tf_op jit(solution)/shard_map/ppermute | solution.py:599
  13.7 1.7 %collective-permute-start.2 = (f32[5,32,128]{2,1,0:T(8,128)S(1)}, f32[5,32,128]{2,1,0:T(8,128)S(1)}, u32[]{:S(2)}, u32[]{:S(2)}) collective-permute-start(f32[5,32,128]{2,1,0:T(8,128)S(1)} %get-tuple-element.55), channel_id=1, source_target_pairs={{192,0},{0,64},{64,128},{128,192},{193,1},{1,65},{65,129},{129,193... | collective-permute-start | bytes 245768 | tf_op jit(solution)/shard_map/ppermute | solution.py:599
  15.4 1.7 %collective-permute-start.3 = (f32[5,32,128]{2,1,0:T(8,128)S(1)}, f32[5,32,128]{2,1,0:T(8,128)S(1)}, u32[]{:S(2)}, u32[]{:S(2)}) collective-permute-start(f32[5,32,128]{2,1,0:T(8,128)S(1)} %get-tuple-element.56), channel_id=1, source_target_pairs={{64,0},{128,64},{192,128},{0,192},{65,1},{129,65},{193,129},{1,193... | collective-permute-start | bytes 245768 | tf_op jit(solution)/shard_map/ppermute | solution.py:599
  17.0 2.4 %collective-permute-done.2.xlo = f32[5,32,128]{2,1,0:T(8,128)S(1)} collective-permute-done((f32[5,32,128]{2,1,0:T(8,128)S(1)}, f32[5,32,128]{2,1,0:T(8,128)S(1)}, u32[]{:S(2)}, u32[]{:S(2)}) %collective-permute-start.2) | collective-permute-done | bytes 81952 | tf_op jit(solution)/shard_map/ppermute | solution.py:599
  20.0 2.9 %collective-permute-start.5 = (f32[60,4,128]{2,1,0:T(4,128)S(1)}, f32[60,4,128]{2,1,0:T(4,128)S(1)}, u32[]{:S(2)}, u32[]{:S(2)}) collective-permute-start(f32[60,4,128]{2,1,0:T(4,128)S(1)} %get-tuple-element.58), channel_id=1, source_target_pairs={{8,0},{16,8},{24,16},{32,24},{40,32},{48,40},{56,48},{0,56},{9,1},... | collective-permute-start | bytes 368648 | tf_op jit(solution)/shard_map/ppermute | solution.py:599
  23.8 1.7 %collective-permute-done.4.ylo = f32[60,4,128]{2,1,0:T(4,128)S(1)} collective-permute-done((f32[60,4,128]{2,1,0:T(4,128)S(1)}, f32[60,4,128]{2,1,0:T(4,128)S(1)}, u32[]{:S(2)}, u32[]{:S(2)}) %collective-permute-start.4) | collective-permute-done | bytes 122912 | tf_op jit(solution)/shard_map/ppermute | solution.py:599
  25.5 3.4 %down_0.1 = (f32[16,16,128]{2,1,0:T(8,128)S(1)}, f32[6,16,128]{2,1,0:T(8,128)S(1)}, f32[6,16,128]{2,1,0:T(8,128)S(1)}, f32[40,40,256]{2,1,0:T(8,128)S(1)}, f32[4...) custom-call(f32[40,40,256]{2,1,0:T(8,128)S(1)} %gather_0.1.field, f32[60,4,128]{2,1,0:T(4,128)S(1)} %collective-permute-done.4.ylo, ...), custom_call_target="tpu_custom_call" | custom-call | tf_op jit(solution)/shard_map/down_0/pallas_call | solution.py:621
  28.9 3.1 %collective-permute-start.6 = (f32[6,16,128]{2,1,0:T(8,128)S(1)}, f32[6,16,128]{2,1,0:T(8,128)S(1)}, u32[]{:S(2)}, u32[]{:S(2)}) collective-permute-start(f32[6,16,128]{2,1,0:T(8,128)S(1)} %get-tuple-element.64), channel_id=1, source_target_pairs={{1,0},{2,1},{3,2},{4,3},{5,4},{6,5},{7,6},{0,7},{9,8},{10,9},{11,1... | collective-permute-start | bytes 147464 | tf_op jit(solution)/shard_map/ppermute | solution.py:599
  32.0 1.7 %collective-permute-done.6.from_right = f32[6,16,128]{2,1,0:T(8,128)S(1)} collective-permute-done((f32[6,16,128]{2,1,0:T(8,128)S(1)}, f32[6,16,128]{2,1,0:T(8,128)S(1)}, u32[]{:S(2)}, u32[]{:S(2)}) %collective-permute-start.6) | collective-permute-done | bytes 49184 | tf_op jit(solution)/shard_map/ppermute | solution.py:599
  33.7 2.3 %collective-permute-done.7.from_left = f32[6,16,128]{2,1,0:T(8,128)S(1)} collective-permute-done((f32[6,16,128]{2,1,0:T(8,128)S(1)}, f32[6,16,128]{2,1,0:T(8,128)S(1)}, u32[]{:S(2)}, u32[]{:S(2)}) %collective-permute-start.7) | collective-permute-done | bytes 49184 | tf_op jit(solution)/shard_map/ppermute | solution.py:599
  36.2 1.7 %collective-permute-start.8 = (f32[6,16,128]{2,1,0:T(8,128)S(1)}, f32[6,16,128]{2,1,0:T(8,128)S(1)}, u32[]{:S(2)}, u32[]{:S(2)}) collective-permute-start(f32[6,16,128]{2,1,0:T(8,128)S(1)} %get-tuple-element.68), channel_id=1, source_target_pairs={{192,0},{0,64},{64,128},{128,192},{193,1},{1,65},{65,129},{129,193... | collective-permute-start | bytes 147464 | tf_op jit(solution)/shard_map/ppermute | solution.py:599
  37.9 1.7 %collective-permute-start.9 = (f32[6,16,128]{2,1,0:T(8,128)S(1)}, f32[6,16,128]{2,1,0:T(8,128)S(1)}, u32[]{:S(2)}, u32[]{:S(2)}) collective-permute-start(f32[6,16,128]{2,1,0:T(8,128)S(1)} %get-tuple-element.69), channel_id=1, source_target_pairs={{64,0},{128,64},{192,128},{0,192},{65,1},{129,65},{193,129},{1,193... | collective-permute-start | bytes 147464 | tf_op jit(solution)/shard_map/ppermute | solution.py:599
  39.5 2.1 %collective-permute-done.8.xlo = f32[6,16,128]{2,1,0:T(8,128)S(1)} collective-permute-done((f32[6,16,128]{2,1,0:T(8,128)S(1)}, f32[6,16,128]{2,1,0:T(8,128)S(1)}, u32[]{:S(2)}, u32[]{:S(2)}) %collective-permute-start.8) | collective-permute-done | bytes 49184 | tf_op jit(solution)/shard_map/ppermute | solution.py:599
  42.0 2.9 %collective-permute-start.11 = (f32[26,8,128]{2,1,0:T(8,128)S(1)}, f32[26,8,128]{2,1,0:T(8,128)S(1)}, u32[]{:S(2)}, u32[]{:S(2)}) collective-permute-start(f32[26,8,128]{2,1,0:T(8,128)S(1)} %get-tuple-element.71), channel_id=1, source_target_pairs={{8,0},{16,8},{24,16},{32,24},{40,32},{48,40},{56,48},{0,56},{9,1},... | collective-permute-start | bytes 319496 | tf_op jit(solution)/shard_map/ppermute | solution.py:599
  48.4 2.2 %collective-permute-start.16 = (f32[3,8,128]{2,1,0:T(8,128)S(1)}, f32[3,8,128]{2,1,0:T(8,128)S(1)}, u32[]{:S(2)}, u32[]{:S(2)}) collective-permute-start(f32[3,8,128]{2,1,0:T(8,128)S(1)} %get-tuple-element.75.own), channel_id=1, source_target_pairs={{6,0},{7,1},{0,2},{1,3},{2,4},{3,5},{4,6},{5,7},{14,8},{15,9},{8,1... | collective-permute-start | bytes 36872 | tf_op jit(solution)/shard_map/ppermute | solution.py:599
  52.2 3.4 %collective-permute-start.14 = (f32[3,8,128]{2,1,0:T(8,128)S(1)}, f32[3,8,128]{2,1,0:T(8,128)S(1)}, u32[]{:S(2)}, u32[]{:S(2)}) collective-permute-start(f32[3,8,128]{2,1,0:T(8,128)S(1)} %get-tuple-element.75.own), channel_id=1, source_target_pairs={{3,0},{4,1},{5,2},{6,3},{7,4},{0,5},{1,6},{2,7},{11,8},{12,9},{13,... | collective-permute-start | bytes 36872 | tf_op jit(solution)/shard_map/ppermute | solution.py:599
  56.4 3.1 %collective-permute-start.12 = (f32[3,8,128]{2,1,0:T(8,128)S(1)}, f32[3,8,128]{2,1,0:T(8,128)S(1)}, u32[]{:S(2)}, u32[]{:S(2)}) collective-permute-start(f32[3,8,128]{2,1,0:T(8,128)S(1)} %get-tuple-element.75.own), channel_id=1, source_target_pairs={{1,0},{2,1},{3,2},{4,3},{5,4},{6,5},{7,6},{0,7},{9,8},{10,9},{11,1... | collective-permute-start | bytes 36872 | tf_op jit(solution)/shard_map/ppermute | solution.py:599
  62.4 2.0 %collective-permute-start.18 = (f32[16,8,128]{2,1,0:T(8,128)S(1)}, f32[16,8,128]{2,1,0:T(8,128)S(1)}, u32[]{:S(2)}, u32[]{:S(2)}) collective-permute-start(f32[16,8,128]{2,1,0:T(8,128)S(1)} %get-tuple-element.76.own), channel_id=1, source_target_pairs={{64,0},{128,64},{192,128},{0,192},{65,1},{129,65},{193,129},{1,193... | collective-permute-start | bytes 196616 | tf_op jit(solution)/shard_map/ppermute | solution.py:599
  65.9 3.9 %collective-permute-done.19.x2 = f32[8,8,128]{2,1,0:T(8,128)S(1)} collective-permute-done((f32[8,8,128]{2,1,0:T(8,128)S(1)}, f32[8,8,128]{2,1,0:T(8,128)S(1)}, u32[]{:S(2)}, u32[]{:S(2)}) %collective-permute-start.19) | collective-permute-done | bytes 32800 | tf_op jit(solution)/shard_map/ppermute | solution.py:599
  70.4 3.2 %collective-permute-start.24 = (f32[18,3,128]{2,1,0:T(4,128)S(1)}, f32[18,3,128]{2,1,0:T(4,128)S(1)}, u32[]{:S(2)}, u32[]{:S(2)}) collective-permute-start(f32[18,3,128]{2,1,0:T(4,128)S(1)} %get-tuple-element.79), channel_id=1, source_target_pairs={{16,0},{24,8},{32,16},{40,24},{48,32},{56,40},{0,48},{8,56},{17,1}... | collective-permute-start | bytes 82952 | tf_op jit(solution)/shard_map/ppermute | solution.py:599
  76.7 6.5 %up.1 = (f32[32,32,128]{2,1,0:T(8,128)S(1)}, f32[32,32,128]{2,1,0:T(8,128)S(1)}, f32[1,128]{1,0:T(1,128)S(1)}) custom-call(f32[50,8,128]{2,1,0:T(8,128)S(1)} %get-tuple-element.77.r2x, f32[50,8,128]{2,1,0:T(8,128)S(1)} %collective-permute-done.21.ya, f32[50,8,128]{2,1,0:T(8,128)S(1)} %collective-permute-done.22.yb, ...), custom_call_target="tpu_custom_call" | custom-call | tf_op jit(solution)/shard_map/up/pallas_call | solution.py:621
  86.6 2.0 %collective-permute-start.26 = (f32[1,128]{1,0:T(1,128)S(1)}, f32[1,128]{1,0:T(1,128)S(1)}, u32[]{:S(2)}, u32[]{:S(2)}) collective-permute-start(f32[1,128]{1,0:T(1,128)S(1)} %add.33), channel_id=1, source_target_pairs={{64,0},{0,64},{192,128},{128,192},{65,1},{1,65},{193,129},{129,193... | collective-permute-start | bytes 1544 | tf_op jit(solution)/shard_map/ppermute | solution.py:603
  89.2 1.9 %collective-permute-done.27 = f32[1,128]{1,0:T(1,128)S(1)} collective-permute-done((f32[1,128]{1,0:T(1,128)S(1)}, f32[1,128]{1,0:T(1,128)S(1)}, u32[]{:S(2)}, u32[]{:S(2)}) %collective-permute-start.27) | collective-permute-done | bytes 544 | tf_op jit(solution)/shard_map/ppermute | solution.py:603
  91.2 2.2 %collective-permute-start.31 = (f32[1,128]{1,0:T(1,128)S(1)}, f32[1,128]{1,0:T(1,128)S(1)}, u32[]{:S(2)}, u32[]{:S(2)}) collective-permute-start(f32[1,128]{1,0:T(1,128)S(1)} %add_add_fusion.2), channel_id=1, source_target_pairs={{48,0},{56,8},{32,16},{40,24},{16,32},{24,40},{0,48},{8,56},{49,1}... | collective-permute-start | bytes 1544 | tf_op jit(solution)/shard_map/ppermute | solution.py:603
  93.4 2.0 %collective-permute-start.29 = (f32[1,128]{1,0:T(1,128)S(1)}, f32[1,128]{1,0:T(1,128)S(1)}, u32[]{:S(2)}, u32[]{:S(2)}) collective-permute-start(f32[1,128]{1,0:T(1,128)S(1)} %add_add_fusion.2), channel_id=1, source_target_pairs={{16,0},{24,8},{0,16},{8,24},{48,32},{56,40},{32,48},{40,56},{17,1}... | collective-permute-start | bytes 1544 | tf_op jit(solution)/shard_map/ppermute | solution.py:603
  96.0 2.4 %collective-permute-done.30 = f32[1,128]{1,0:T(1,128)S(1)} collective-permute-done((f32[1,128]{1,0:T(1,128)S(1)}, f32[1,128]{1,0:T(1,128)S(1)}, u32[]{:S(2)}, u32[]{:S(2)}) %collective-permute-start.30) | collective-permute-done | bytes 544 | tf_op jit(solution)/shard_map/ppermute | solution.py:603
  100.0 3.2 %collective-permute-start.33 = (f32[1,128]{1,0:T(1,128)S(1)}, f32[1,128]{1,0:T(1,128)S(1)}, u32[]{:S(2)}, u32[]{:S(2)}) collective-permute-start(f32[1,128]{1,0:T(1,128)S(1)} %add_add_fusion.1), channel_id=1, source_target_pairs={{2,0},{3,1},{0,2},{1,3},{6,4},{7,5},{4,6},{5,7},{10,8},{11,9},{8,1... | collective-permute-start | bytes 1544 | tf_op jit(solution)/shard_map/ppermute | solution.py:603
  104.7 2.0 %collective-permute-done.32 = f32[1,128]{1,0:T(1,128)S(1)} collective-permute-done((f32[1,128]{1,0:T(1,128)S(1)}, f32[1,128]{1,0:T(1,128)S(1)}, u32[]{:S(2)}, u32[]{:S(2)}) %collective-permute-start.32) | collective-permute-done | bytes 544 | tf_op jit(solution)/shard_map/ppermute | solution.py:603
  106.7 3.6 %collective-permute-start.35 = (f32[1,128]{1,0:T(1,128)S(1)}, f32[1,128]{1,0:T(1,128)S(1)}, u32[]{:S(2)}, u32[]{:S(2)}) collective-permute-start(f32[1,128]{1,0:T(1,128)S(1)} %add_add_fusion), channel_id=1, source_target_pairs={{7,0},{6,1},{5,2},{4,3},{3,4},{2,5},{1,6},{0,7},{15,8},{14,9},{13,... | collective-permute-start | bytes 1544 | tf_op jit(solution)/shard_map/ppermute | solution.py:603
  111.3 2.0 %collective-permute-done.35 = f32[1,128]{1,0:T(1,128)S(1)} collective-permute-done((f32[1,128]{1,0:T(1,128)S(1)}, f32[1,128]{1,0:T(1,128)S(1)}, u32[]{:S(2)}, u32[]{:S(2)}) %collective-permute-start.35) | collective-permute-done | bytes 544 | tf_op jit(solution)/shard_map/ppermute | solution.py:603
  (70 shorter events, 27.6 us)
Async XLA Ops:
  2.7 6.9 %collective-permute-start = (f32[12,32,128]{2,1,0:T(8,128)S(1)}, f32[12,32,128]{2,1,0:T(8,128)S(1)}, u32[]{:S(2)}, u32[]{:S(2)}) collective-permute-start(f32[12,32,128]{2,1,0:T(8,128)S(1)} %get-tuple-element.52), channel_id=1, source_target_pairs={{1,0},{2,1},{3,2},{4,3},{5,4},{6,5},{7,6},{0,7},{9,8},{10,9},{11,1... | collective-permute-start | bytes 589832 | tf_op jit(solution)/shard_map/ppermute | solution.py:599
  4.6 8.7 %collective-permute-start.1 = (f32[12,32,128]{2,1,0:T(8,128)S(1)}, f32[12,32,128]{2,1,0:T(8,128)S(1)}, u32[]{:S(2)}, u32[]{:S(2)}) collective-permute-start(f32[12,32,128]{2,1,0:T(8,128)S(1)} %get-tuple-element.53), channel_id=1, source_target_pairs={{7,0},{0,1},{1,2},{2,3},{3,4},{4,5},{5,6},{6,7},{15,8},{8,9},{9,10... | collective-permute-start | bytes 589832 | tf_op jit(solution)/shard_map/ppermute | solution.py:599
  13.7 5.7 %collective-permute-start.2 = (f32[5,32,128]{2,1,0:T(8,128)S(1)}, f32[5,32,128]{2,1,0:T(8,128)S(1)}, u32[]{:S(2)}, u32[]{:S(2)}) collective-permute-start(f32[5,32,128]{2,1,0:T(8,128)S(1)} %get-tuple-element.55), channel_id=1, source_target_pairs={{192,0},{0,64},{64,128},{128,192},{193,1},{1,65},{65,129},{129,193... | collective-permute-start | bytes 245768 | tf_op jit(solution)/shard_map/ppermute | solution.py:599
  15.4 4.4 %collective-permute-start.3 = (f32[5,32,128]{2,1,0:T(8,128)S(1)}, f32[5,32,128]{2,1,0:T(8,128)S(1)}, u32[]{:S(2)}, u32[]{:S(2)}) collective-permute-start(f32[5,32,128]{2,1,0:T(8,128)S(1)} %get-tuple-element.56), channel_id=1, source_target_pairs={{64,0},{128,64},{192,128},{0,192},{65,1},{129,65},{193,129},{1,193... | collective-permute-start | bytes 245768 | tf_op jit(solution)/shard_map/ppermute | solution.py:599
  20.0 5.5 %collective-permute-start.4 = (f32[60,4,128]{2,1,0:T(4,128)S(1)}, f32[60,4,128]{2,1,0:T(4,128)S(1)}, u32[]{:S(2)}, u32[]{:S(2)}) collective-permute-start(f32[60,4,128]{2,1,0:T(4,128)S(1)} %get-tuple-element.57), channel_id=1, source_target_pairs={{56,0},{0,8},{8,16},{16,24},{24,32},{32,40},{40,48},{48,56},{57,1}... | collective-permute-start | bytes 368648 | tf_op jit(solution)/shard_map/ppermute | solution.py:599
  20.0 5.5 %collective-permute-start.5 = (f32[60,4,128]{2,1,0:T(4,128)S(1)}, f32[60,4,128]{2,1,0:T(4,128)S(1)}, u32[]{:S(2)}, u32[]{:S(2)}) collective-permute-start(f32[60,4,128]{2,1,0:T(4,128)S(1)} %get-tuple-element.58), channel_id=1, source_target_pairs={{8,0},{16,8},{24,16},{32,24},{40,32},{48,40},{56,48},{0,56},{9,1},... | collective-permute-start | bytes 368648 | tf_op jit(solution)/shard_map/ppermute | solution.py:599
  28.9 4.8 %collective-permute-start.6 = (f32[6,16,128]{2,1,0:T(8,128)S(1)}, f32[6,16,128]{2,1,0:T(8,128)S(1)}, u32[]{:S(2)}, u32[]{:S(2)}) collective-permute-start(f32[6,16,128]{2,1,0:T(8,128)S(1)} %get-tuple-element.64), channel_id=1, source_target_pairs={{1,0},{2,1},{3,2},{4,3},{5,4},{6,5},{7,6},{0,7},{9,8},{10,9},{11,1... | collective-permute-start | bytes 147464 | tf_op jit(solution)/shard_map/ppermute | solution.py:599
  36.2 5.4 %collective-permute-start.8 = (f32[6,16,128]{2,1,0:T(8,128)S(1)}, f32[6,16,128]{2,1,0:T(8,128)S(1)}, u32[]{:S(2)}, u32[]{:S(2)}) collective-permute-start(f32[6,16,128]{2,1,0:T(8,128)S(1)} %get-tuple-element.68), channel_id=1, source_target_pairs={{192,0},{0,64},{64,128},{128,192},{193,1},{1,65},{65,129},{129,193... | collective-permute-start | bytes 147464 | tf_op jit(solution)/shard_map/ppermute | solution.py:599
  42.0 5.4 %collective-permute-start.10 = (f32[26,8,128]{2,1,0:T(8,128)S(1)}, f32[26,8,128]{2,1,0:T(8,128)S(1)}, u32[]{:S(2)}, u32[]{:S(2)}) collective-permute-start(f32[26,8,128]{2,1,0:T(8,128)S(1)} %get-tuple-element.70), channel_id=1, source_target_pairs={{56,0},{0,8},{8,16},{16,24},{24,32},{32,40},{40,48},{48,56},{57,1}... | collective-permute-start | bytes 319496 | tf_op jit(solution)/shard_map/ppermute | solution.py:599
  42.0 5.3 %collective-permute-start.11 = (f32[26,8,128]{2,1,0:T(8,128)S(1)}, f32[26,8,128]{2,1,0:T(8,128)S(1)}, u32[]{:S(2)}, u32[]{:S(2)}) collective-permute-start(f32[26,8,128]{2,1,0:T(8,128)S(1)} %get-tuple-element.71), channel_id=1, source_target_pairs={{8,0},{16,8},{24,16},{32,24},{40,32},{48,40},{56,48},{0,56},{9,1},... | collective-permute-start | bytes 319496 | tf_op jit(solution)/shard_map/ppermute | solution.py:599
  48.3 8.1 %collective-permute-start.17 = (f32[3,8,128]{2,1,0:T(8,128)S(1)}, f32[3,8,128]{2,1,0:T(8,128)S(1)}, u32[]{:S(2)}, u32[]{:S(2)}) collective-permute-start(f32[3,8,128]{2,1,0:T(8,128)S(1)} %get-tuple-element.75.own), channel_id=1, source_target_pairs={{7,0},{0,1},{1,2},{2,3},{3,4},{4,5},{5,6},{6,7},{15,8},{8,9},{9,10... | collective-permute-start | bytes 36872 | tf_op jit(solution)/shard_map/ppermute | solution.py:599
  48.4 11.2 %collective-permute-start.16 = (f32[3,8,128]{2,1,0:T(8,128)S(1)}, f32[3,8,128]{2,1,0:T(8,128)S(1)}, u32[]{:S(2)}, u32[]{:S(2)}) collective-permute-start(f32[3,8,128]{2,1,0:T(8,128)S(1)} %get-tuple-element.75.own), channel_id=1, source_target_pairs={{6,0},{7,1},{0,2},{1,3},{2,4},{3,5},{4,6},{5,7},{14,8},{15,9},{8,1... | collective-permute-start | bytes 36872 | tf_op jit(solution)/shard_map/ppermute | solution.py:599
  50.6 9.0 %collective-permute-start.15 = (f32[3,8,128]{2,1,0:T(8,128)S(1)}, f32[3,8,128]{2,1,0:T(8,128)S(1)}, u32[]{:S(2)}, u32[]{:S(2)}) collective-permute-start(f32[3,8,128]{2,1,0:T(8,128)S(1)} %get-tuple-element.75.own), channel_id=1, source_target_pairs={{5,0},{6,1},{7,2},{0,3},{1,4},{2,5},{3,6},{4,7},{13,8},{14,9},{15,... | collective-permute-start | bytes 36872 | tf_op jit(solution)/shard_map/ppermute | solution.py:599
  52.2 7.4 %collective-permute-start.14 = (f32[3,8,128]{2,1,0:T(8,128)S(1)}, f32[3,8,128]{2,1,0:T(8,128)S(1)}, u32[]{:S(2)}, u32[]{:S(2)}) collective-permute-start(f32[3,8,128]{2,1,0:T(8,128)S(1)} %get-tuple-element.75.own), channel_id=1, source_target_pairs={{3,0},{4,1},{5,2},{6,3},{7,4},{0,5},{1,6},{2,7},{11,8},{12,9},{13,... | collective-permute-start | bytes 36872 | tf_op jit(solution)/shard_map/ppermute | solution.py:599
  55.6 4.6 %collective-permute-start.13 = (f32[3,8,128]{2,1,0:T(8,128)S(1)}, f32[3,8,128]{2,1,0:T(8,128)S(1)}, u32[]{:S(2)}, u32[]{:S(2)}) collective-permute-start(f32[3,8,128]{2,1,0:T(8,128)S(1)} %get-tuple-element.75.own), channel_id=1, source_target_pairs={{2,0},{3,1},{4,2},{5,3},{6,4},{7,5},{0,6},{1,7},{10,8},{11,9},{12,... | collective-permute-start | bytes 36872 | tf_op jit(solution)/shard_map/ppermute | solution.py:599
  56.4 4.6 %collective-permute-start.12 = (f32[3,8,128]{2,1,0:T(8,128)S(1)}, f32[3,8,128]{2,1,0:T(8,128)S(1)}, u32[]{:S(2)}, u32[]{:S(2)}) collective-permute-start(f32[3,8,128]{2,1,0:T(8,128)S(1)} %get-tuple-element.75.own), channel_id=1, source_target_pairs={{1,0},{2,1},{3,2},{4,3},{5,4},{6,5},{7,6},{0,7},{9,8},{10,9},{11,1... | collective-permute-start | bytes 36872 | tf_op jit(solution)/shard_map/ppermute | solution.py:599
  61.1 8.7 %collective-permute-start.20 = (f32[16,8,128]{2,1,0:T(8,128)S(1)}, f32[16,8,128]{2,1,0:T(8,128)S(1)}, u32[]{:S(2)}, u32[]{:S(2)}) collective-permute-start(f32[16,8,128]{2,1,0:T(8,128)S(1)} %get-tuple-element.76.own), channel_id=1, source_target_pairs={{192,0},{0,64},{64,128},{128,192},{193,1},{1,65},{65,129},{129,193... | collective-permute-start | bytes 196616 | tf_op jit(solution)/shard_map/ppermute | solution.py:599
  62.4 7.4 %collective-permute-start.18 = (f32[16,8,128]{2,1,0:T(8,128)S(1)}, f32[16,8,128]{2,1,0:T(8,128)S(1)}, u32[]{:S(2)}, u32[]{:S(2)}) collective-permute-start(f32[16,8,128]{2,1,0:T(8,128)S(1)} %get-tuple-element.76.own), channel_id=1, source_target_pairs={{64,0},{128,64},{192,128},{0,192},{65,1},{129,65},{193,129},{1,193... | collective-permute-start | bytes 196616 | tf_op jit(solution)/shard_map/ppermute | solution.py:599
  64.4 5.4 %collective-permute-start.19 = (f32[8,8,128]{2,1,0:T(8,128)S(1)}, f32[8,8,128]{2,1,0:T(8,128)S(1)}, u32[]{:S(2)}, u32[]{:S(2)}) collective-permute-start(f32[8,8,128]{2,1,0:T(8,128)S(1)} %slice.6), channel_id=1, source_target_pairs={{128,0},{192,64},{0,128},{64,192},{129,1},{193,65},{1,129},{65,193... | collective-permute-start | bytes 98312 | tf_op jit(solution)/shard_map/ppermute | solution.py:599
  69.9 6.1 %collective-permute-start.22 = (f32[50,8,128]{2,1,0:T(8,128)S(1)}, f32[50,8,128]{2,1,0:T(8,128)S(1)}, u32[]{:S(2)}, u32[]{:S(2)}) collective-permute-start(f32[50,8,128]{2,1,0:T(8,128)S(1)} %get-tuple-element.77.r2x), channel_id=1, source_target_pairs={{8,0},{16,8},{24,16},{32,24},{40,32},{48,40},{56,48},{0,56},{9,1},... | collective-permute-start | bytes 614408 | tf_op jit(solution)/shard_map/ppermute | solution.py:599
  69.9 6.8 %collective-permute-start.21 = (f32[50,8,128]{2,1,0:T(8,128)S(1)}, f32[50,8,128]{2,1,0:T(8,128)S(1)}, u32[]{:S(2)}, u32[]{:S(2)}) collective-permute-start(f32[50,8,128]{2,1,0:T(8,128)S(1)} %get-tuple-element.77.r2x), channel_id=1, source_target_pairs={{56,0},{0,8},{8,16},{16,24},{24,32},{32,40},{40,48},{48,56},{57,1}... | collective-permute-start | bytes 614408 | tf_op jit(solution)/shard_map/ppermute | solution.py:599
  70.4 5.6 %collective-permute-start.23 = (f32[18,3,128]{2,1,0:T(4,128)S(1)}, f32[18,3,128]{2,1,0:T(4,128)S(1)}, u32[]{:S(2)}, u32[]{:S(2)}) collective-permute-start(f32[18,3,128]{2,1,0:T(4,128)S(1)} %get-tuple-element.78), channel_id=1, source_target_pairs={{48,0},{56,8},{0,16},{8,24},{16,32},{24,40},{32,48},{40,56},{49,1}... | collective-permute-start | bytes 82952 | tf_op jit(solution)/shard_map/ppermute | solution.py:599
  70.4 5.6 %collective-permute-start.24 = (f32[18,3,128]{2,1,0:T(4,128)S(1)}, f32[18,3,128]{2,1,0:T(4,128)S(1)}, u32[]{:S(2)}, u32[]{:S(2)}) collective-permute-start(f32[18,3,128]{2,1,0:T(4,128)S(1)} %get-tuple-element.79), channel_id=1, source_target_pairs={{16,0},{24,8},{32,16},{40,24},{48,32},{56,40},{0,48},{8,56},{17,1}... | collective-permute-start | bytes 82952 | tf_op jit(solution)/shard_map/ppermute | solution.py:599
  84.4 4.8 %collective-permute-start.28 = (f32[1,128]{1,0:T(1,128)S(1)}, f32[1,128]{1,0:T(1,128)S(1)}, u32[]{:S(2)}, u32[]{:S(2)}) collective-permute-start(f32[1,128]{1,0:T(1,128)S(1)} %add.33), channel_id=1, source_target_pairs={{192,0},{128,64},{64,128},{0,192},{193,1},{129,65},{65,129},{1,193... | collective-permute-start | bytes 1544 | tf_op jit(solution)/shard_map/ppermute | solution.py:603
  86.1 5.0 %collective-permute-start.27 = (f32[1,128]{1,0:T(1,128)S(1)}, f32[1,128]{1,0:T(1,128)S(1)}, u32[]{:S(2)}, u32[]{:S(2)}) collective-permute-start(f32[1,128]{1,0:T(1,128)S(1)} %add.33), channel_id=1, source_target_pairs={{128,0},{192,64},{0,128},{64,192},{129,1},{193,65},{1,129},{65,193... | collective-permute-start | bytes 1544 | tf_op jit(solution)/shard_map/ppermute | solution.py:603
  86.6 4.6 %collective-permute-start.26 = (f32[1,128]{1,0:T(1,128)S(1)}, f32[1,128]{1,0:T(1,128)S(1)}, u32[]{:S(2)}, u32[]{:S(2)}) collective-permute-start(f32[1,128]{1,0:T(1,128)S(1)} %add.33), channel_id=1, source_target_pairs={{64,0},{0,64},{192,128},{128,192},{65,1},{1,65},{193,129},{129,193... | collective-permute-start | bytes 1544 | tf_op jit(solution)/shard_map/ppermute | solution.py:603
  91.2 4.8 %collective-permute-start.31 = (f32[1,128]{1,0:T(1,128)S(1)}, f32[1,128]{1,0:T(1,128)S(1)}, u32[]{:S(2)}, u32[]{:S(2)}) collective-permute-start(f32[1,128]{1,0:T(1,128)S(1)} %add_add_fusion.2), channel_id=1, source_target_pairs={{48,0},{56,8},{32,16},{40,24},{16,32},{24,40},{0,48},{8,56},{49,1}... | collective-permute-start | bytes 1544 | tf_op jit(solution)/shard_map/ppermute | solution.py:603
  93.4 5.0 %collective-permute-start.30 = (f32[1,128]{1,0:T(1,128)S(1)}, f32[1,128]{1,0:T(1,128)S(1)}, u32[]{:S(2)}, u32[]{:S(2)}) collective-permute-start(f32[1,128]{1,0:T(1,128)S(1)} %add_add_fusion.2), channel_id=1, source_target_pairs={{32,0},{40,8},{48,16},{56,24},{0,32},{8,40},{16,48},{24,56},{33,1}... | collective-permute-start | bytes 1544 | tf_op jit(solution)/shard_map/ppermute | solution.py:603
  93.4 5.0 %collective-permute-start.29 = (f32[1,128]{1,0:T(1,128)S(1)}, f32[1,128]{1,0:T(1,128)S(1)}, u32[]{:S(2)}, u32[]{:S(2)}) collective-permute-start(f32[1,128]{1,0:T(1,128)S(1)} %add_add_fusion.2), channel_id=1, source_target_pairs={{16,0},{24,8},{0,16},{8,24},{48,32},{56,40},{32,48},{40,56},{17,1}... | collective-permute-start | bytes 1544 | tf_op jit(solution)/shard_map/ppermute | solution.py:603
  98.4 4.7 %collective-permute-start.34 = (f32[1,128]{1,0:T(1,128)S(1)}, f32[1,128]{1,0:T(1,128)S(1)}, u32[]{:S(2)}, u32[]{:S(2)}) collective-permute-start(f32[1,128]{1,0:T(1,128)S(1)} %add_add_fusion.1), channel_id=1, source_target_pairs={{3,0},{2,1},{1,2},{0,3},{7,4},{6,5},{5,6},{4,7},{11,8},{10,9},{9,1... | collective-permute-start | bytes 1544 | tf_op jit(solution)/shard_map/ppermute | solution.py:603
  100.0 4.7 %collective-permute-start.33 = (f32[1,128]{1,0:T(1,128)S(1)}, f32[1,128]{1,0:T(1,128)S(1)}, u32[]{:S(2)}, u32[]{:S(2)}) collective-permute-start(f32[1,128]{1,0:T(1,128)S(1)} %add_add_fusion.1), channel_id=1, source_target_pairs={{2,0},{3,1},{0,2},{1,3},{6,4},{7,5},{4,6},{5,7},{10,8},{11,9},{8,1... | collective-permute-start | bytes 1544 | tf_op jit(solution)/shard_map/ppermute | solution.py:603
  106.7 6.5 %collective-permute-start.35 = (f32[1,128]{1,0:T(1,128)S(1)}, f32[1,128]{1,0:T(1,128)S(1)}, u32[]{:S(2)}, u32[]{:S(2)}) collective-permute-start(f32[1,128]{1,0:T(1,128)S(1)} %add_add_fusion), channel_id=1, source_target_pairs={{7,0},{6,1},{5,2},{4,3},{3,4},{2,5},{1,6},{0,7},{15,8},{14,9},{13,... | collective-permute-start | bytes 1544 | tf_op jit(solution)/shard_map/ppermute | solution.py:603
  (8 other events, 71.8 us)

commit v4 on v3

--- a/solution.py
+++ b/solution.py
@@ -122,12 +122,13 @@
     return mid, (ref[a + 1 : b + 1] + ref[a - 1 : b - 1]) + (pltpu.roll(mid, 1, 1) + pltpu.roll(mid, count - 1, 1))
 
 
-def chunks(a, b, step):
-    return [(c, min(c + step, b)) for c in range(a, b, step)]
-
-
-def relax(src, dst, a, b, step, matrix, right, side):
-    for p, q in chunks(a, b, step):
+def chunks(a, b):
+    mid = (a + b + 1) // 2
+    return [(a, mid), (mid, b)]
+
+
+def relax(src, dst, a, b, matrix, right, side):
+    for p, q in chunks(a, b):
         mid, near = around(src, p, q)
         dst[p:q] = times(mid, matrix) + right(p, q) + side[p:q] * near
 
@@ -145,20 +146,52 @@
         to_right[g] = right
 
 
-def prepare_kernel(data, weights, own, to_left, to_right):
-    own[...] = data[...]
-    pack_lanes([data[p] for p in range(32)], 32, 36, 128, to_left, to_right)
-    for out in (to_left, to_right):
-        out[11] = jnp.concatenate([weights[...], jnp.zeros((24, 128), F32)], axis=0)
+def prepare_kernel(data, weights, own, w, to_left, to_right, sems):
+    copies = [
+        pltpu.make_async_copy(data.at[pl.ds(8 * g, 8)], own.at[pl.ds(8 * g, 8)], sems.at[g]) for g in range(4)
+    ]
+    copies.append(pltpu.make_async_copy(weights, w, sems.at[4]))
+    for copy in copies:
+        copy.start()
+    lane = rows((32, 128), 1)
+    thin = [jnp.zeros((32, 128), F32)] * 2
+    for g in range(8):
+        if g % 2 == 0:
+            copies[g // 2].wait()
+        left, right = own[4 * g], None
+        for i in range(4):
+            p = 4 * g + i
+            value = own[p]
+            if i:
+                left = jnp.where(lane < 32 * i, left, pltpu.roll(value, 32 * i, 1))
+            b = pltpu.roll(value, 32 * i + 32, 1) if i < 3 else value
+            right = b if i == 0 else jnp.where(lane < 32 * i, right, b)
+            here = (lane >= 4 * p) & (lane < 4 * p + 4)
+            thin[0] = jnp.where(here, pltpu.roll(value, (4 * p - 32) % 128, 1) if p != 8 else value, thin[0])
+            thin[1] = jnp.where(here, pltpu.roll(value, (4 * p - 92) % 128, 1) if p != 23 else value, thin[1])
+        to_left[32 * g : 32 * g + 32] = left
+        to_right[32 * g : 32 * g + 32] = right
+    to_left[256:288] = thin[0]
+    to_right[256:288] = thin[1]
+    copies[4].wait()
+    to_left[288:296] = w[...]
+    to_right[288:296] = w[...]
+
+
+def turned(value, amount):
+    return pltpu.roll(value, amount % 128, 1) if amount % 128 else value
 
 
 def spread_0_kernel(own, from_right, from_left, tail, first, last):
     lane = rows((32, 128), 1)
     packed = [jnp.zeros((32, 128), F32)] * 2
+    thin_right, thin_left = from_right[256:288], from_left[256:288]
     for p in range(32):
-        group, i = divmod(p, 3)
-        right = pltpu.roll(from_right[group], 128 - SLOT * i, 1) if i else from_right[group]
-        left = pltpu.roll(from_left[group], (92 - SLOT * i) % 128, 1)
+        g, i = divmod(p, 4)
+        right = turned(from_right[32 * g : 32 * g + 32], -32 * i)
+        left = turned(from_left[32 * g : 32 * g + 32], 96 - 32 * i)
+        right = jnp.where(lane < 32, right, turned(thin_right, 32 - 4 * p))
+        left = jnp.where(lane < 96, turned(thin_left, 92 - 4 * p), left)
         value = jnp.where(lane < 36, right, jnp.where(lane >= 92, left, 0.0))
         tail[p] = value
         for side, far in ((0, p + 1), (1, 32 - p)):
@@ -227,26 +260,41 @@
         field[p, 36:] = jnp.zeros((4, 256), F32)
 
 
-def weights_0_kernel(left, own, right, b0, k0, m0, f0):
-    iz = lax.axis_index("gz")
+def weights_0_kernel(left, own, right, b0, k0, m0, f0, fold, grow, side):
+    ix, iy, iz = lax.axis_index("gx"), lax.axis_index("gy"), lax.axis_index("gz")
     lane = rows((8, 128), 1)
-    laid = jnp.concatenate([own[...], jnp.where(lane < 64, right[11, :8], left[11, :8])], axis=1)
+    laid = jnp.concatenate([own[...], jnp.where(lane < 64, right[288:296], left[288:296])], axis=1)
     band, op, step, factor = operators(laid, place_0, iz, 0, 36, S0)
     b0[...] = thrice(jnp.transpose(band))
     k0[...] = thrice(step)
     m0[...] = thrice(op)
     f0[...] = jnp.broadcast_to(factor, (8, 256))
-
-
-def weights_1_kernel(left, own, right, k1, k1u, m1, f1):
-    iz = lax.axis_index("gz")
-    wide = jnp.concatenate([left[11, :8], own[...], right[11, :8]], axis=1)
+    fold[...] = restrict_matrix(place_0, 256, lambda q: q, 128, iz, 0, 36)
+    grow[...] = prolong_matrix(place_1, 128, place_0, 256, iz, 0, 36)
+    y = iy * 32 + rows((40, 256), 0) - H0
+    column = jnp.where((y >= 0) & (y < NY), factor * S0, 0.0)
+    for p in range(40):
+        xr = ix * 32 + p - H0
+        side[p] = column * jnp.where((xr >= 0) & (xr < NX), 1.0, 0.0)
+
+
+def weights_1_kernel(left, own, right, k1, k1u, m1, f1, fold, grow, side):
+    ix, iy, iz = lax.axis_index("gx"), lax.axis_index("gy"), lax.axis_index("gz")
+    wide = jnp.concatenate([left[288:296], own[...], right[288:296]], axis=1)
     mean = jnp.where((rows((384, 256), 0) - 128) >> 1 == place_1(rows((384, 256), 1)), 0.5, 0.0)
     band, op, step, factor = operators(exact(wide, mean), place_1, iz, 1, 41, S1)
     k1[...] = thrice(step[:, :128])
     k1u[...] = thrice(step[:128, :128])
     m1[...] = thrice(op[:128, :128])
     f1[...] = jnp.broadcast_to(factor, (8, 256))
+    fold[...] = restrict_matrix(place_1, 128, lambda q: q, 128, iz, 1, 32)
+    grow[...] = prolong_matrix(place_2, 128, place_1, 128, iz, 1, 41)
+    yrow = rows((32, 128), 0)
+    y = iy * 16 + yrow - H1
+    column = jnp.where((y >= 0) & (y < NY // 2) & (yrow < 26), factor[:, :128] * S1, 0.0)
+    for p in range(26):
+        xr = ix * 16 + p - H1
+        side[p] = column * jnp.where((xr >= 0) & (xr < NX // 2), 1.0, 0.0)
 
 
 def spread_1_kernel(own, from_right, from_left, main, rest, first, last):
@@ -284,13 +332,11 @@
 
 
 def down_0_kernel(
-    field, ylo, yhi, b0, k0, m0, f0, r1, to_left, to_right, e_out, r_out, stat, d, e0, side, g, gx
+    field, ylo, yhi, b0, k0, m0, f0, fold, side, r1, to_left, to_right, e_out, r_out, stat, d, e0, g, gx
 ):
     ix, iy, iz = lax.axis_index("gx"), lax.axis_index("gy"), lax.axis_index("gz")
     low_ok = jnp.where(iy > 0, 1.0, 0.0)
     high_ok = jnp.where(iy < 7, 1.0, 0.0)
-    y = iy * 32 + rows((40, 256), 0) - H0
-    column = jnp.where((y >= 0) & (y < NY), f0[0:1, :] * S0, 0.0)
     lane = rows((4, 128), 1)
     for p in range(40):
         xr = ix * 32 + p - H0
@@ -300,17 +346,16 @@
             moved = pltpu.roll(edge[40 + p // 2], 100 if p % 2 == 0 else 36, 1)
             d[p, part, :128] = edge[p] * (ok * good)
             d[p, part, 128:] = jnp.where((lane < 28) | (lane >= 100), moved, 0.0) * (ok * good)
-        side[p] = column * ok
     factor = f0[0:1, :].reshape(1, 1, 256)
-    for p, q in chunks(0, 40, 8):
+    for p, q in chunks(0, 40):
         r = times(d[p:q], b0[...])
         r_out[p:q] = r
         e0[p:q] = r * factor
-    relax(e0, e_out, 1, 39, 10, k0[...], lambda p, q: e0[p:q], side)
+    relax(e0, e_out, 1, 39, k0[...], lambda p, q: e0[p:q], side)
     e_out[0] = jnp.zeros((40, 256), F32)
     e_out[39] = jnp.zeros((40, 256), F32)
     total = jnp.zeros((40, 128), F32)
-    for p, q in chunks(3, 37, 9):
+    for p, q in chunks(3, 37):
         mid, near = around(e_out, p, q)
         value = r_out[p:q] - times(mid, m0[...]) + S0 * near
         x = ix * 32 + rows(value.shape, 0) + (p - H0)
@@ -329,13 +374,12 @@
         jnp.concatenate([gx[:, t, pl.ds(3 + a, 16, stride=2), :] for t in range(2)], axis=2) for a in range(4)
     ]
     gy = ((gy[0] + gy[3]) + 3.0 * (gy[1] + gy[2])) * 0.125
-    fold = restrict_matrix(place_0, 256, lambda q: q, 128, iz, 0, 36)
-    out = times_exact(gy, fold)
+    out = times_exact(gy, fold[...])
     r1[...] = out
     pack_lanes([out[i] for i in range(16)], 16, 37, 64, to_left, to_right)
 
 
-def down_1_kernel(wide, tail, xlo, xhi, ylo, yhi, k1, m1, f1, w, msg, e_out, r_out, stat, e0, e0b, side, g, gx):
+def down_1_kernel(wide, tail, xlo, xhi, ylo, yhi, k1, m1, f1, fold, side, w, msg, e_out, r_out, stat, e0, e0b, g, gx):
     ix, iy, iz = lax.axis_index("gx"), lax.axis_index("gy"), lax.axis_index("gz")
     lane = rows((32, 128), 1)
     yrow = rows((32, 128), 0)
@@ -358,15 +402,14 @@
         r_out[p] = main
         e0[p] = main * f1[0:1, :128]
         e0b[p] = rest * f1[0:1, 128:]
-        side[p] = ok * (f1[0:1, :128] * S1)
-    for p, q in chunks(1, 25, 8):
+    for p, q in chunks(1, 25):
         mid, near = around(e0, p, q)
         both = jnp.concatenate([mid, e0b[p:q]], axis=2)
         e_out[p:q] = times(both, k1[...]) + mid + side[p:q] * near
     e_out[0] = jnp.zeros((32, 128), F32)
     e_out[25] = jnp.zeros((32, 128), F32)
     total = jnp.zeros((32, 128), F32)
-    for p, q in chunks(4, 22, 9):
+    for p, q in chunks(4, 22):
         mid, near = around(e_out, p, q)
         value = r_out[p:q] - times(mid, m1[...]) + S1 * near
         x = ix * 16 + rows(value.shape, 0) + (p - H1)
@@ -382,8 +425,7 @@
         gx[i] = ((g[2 * i + 4] + g[2 * i + 7]) + 3.0 * (g[2 * i + 5] + g[2 * i + 6])) * 0.125
     gy = [gx[:, pl.ds(4 + a, 8, stride=2), :] for a in range(4)]
     gy = ((gy[0] + gy[3]) + 3.0 * (gy[1] + gy[2])) * 0.125
-    fold = restrict_matrix(place_1, 128, lambda q: q, 128, iz, 1, 32)
-    out = times_exact(gy, fold)[:, :, :32]
+    out = times_exact(gy, fold[...])[:, :, :32]
     for k in range(2):
         msg[k] = jnp.concatenate([out[4 * k + i] for i in range(4)], axis=1)
     mean = jnp.where(rows((128, 128), 0) >> 2 == rows((128, 128), 1), 0.25, 0.0)
@@ -424,13 +466,21 @@
         high[i] = value[5:]
 
 
-def weights_2_kernel(w2, k2, k2u, m2, f2, k3, f3):
-    iz = lax.axis_index("gz")
+def weights_2_kernel(w2, k2, k2u, m2, f2, k3, f3, fold, grow, side):
+    ix, iy, iz = lax.axis_index("gx"), lax.axis_index("gy"), lax.axis_index("gz")
     band, op, step, factor = operators(w2[...], place_2, iz, 2, 69, S2)
     k2[...] = thrice(step)
     k2u[...] = thrice(step[:128, :128])
     m2[...] = thrice(op)
     f2[...] = jnp.broadcast_to(factor, (8, 256))
+    fold[...] = restrict_matrix(place_2, 256, place_3, 128, iz, 2, 65)
+    grow[...] = prolong_matrix(place_3, 128, place_2, 128, iz, 2, 69)
+    yrow = rows((32, 256), 0)
+    y = iy * 8 + yrow - H2
+    column = jnp.where((y >= 0) & (y < NY // 4) & (yrow < 30), factor * S2, 0.0)
+    for p in range(30):
+        xr = ix * 8 + p - H2
+        side[p] = column * jnp.where((xr >= 0) & (xr < NX // 4), 1.0, 0.0)
     mean = jnp.where(place_2(rows((256, 128), 0)) >> 1 == place_3(rows((256, 128), 1)), 0.5, 0.0)
     band, op, step, factor = operators(exact(w2[...], mean), place_3, iz, 3, 28, S3)
     k3[...] = thrice(step)
@@ -438,10 +488,10 @@
 
 
 def up_kernel(
-    r2x, ya, yb, yc, yd, k2, k2u, m2, f2, k3, f3,
-    k1, f1, e1s, r1s, k0, m0, f0, e0s, r0s, stat0, stat1,
+    r2x, ya, yb, yc, yd, k2, k2u, m2, f2, k3, f3, fold2, grow2, side2,
+    k1, f1, e1s, r1s, grow1, side1, k0, m0, f0, e0s, r0s, grow0, side0, stat0, stat1,
     sol, res, stat,
-    ra, ea, eb, side2, gx2, r3, e3, side3, c3, cy2, ua, ub, side1, cy1, va, vb, side0, cy0,
+    ra, ea, eb, gx2, r3, e3, side3, c3, cy2, ua, ub, cy1, va, vb, cy0,
 ):
     ix, iy, iz = lax.axis_index("gx"), lax.axis_index("gy"), lax.axis_index("gz")
     lane = rows((32, 128), 1)
@@ -464,11 +514,9 @@
         ra[p, :, 128:] = rest
         ea[p, :, :128] = main * f2[0:1, :128]
         ea[p, :, 128:] = rest * f2[0:1, 128:]
-        side2[p, :, :128] = ok * (f2[0:1, :128] * S2)
-        side2[p, :, 128:] = ok * (f2[0:1, 128:] * S2)
-    relax(ea, eb, 1, 29, 10, k2[...], lambda p, q: ea[p:q], side2)
+    relax(ea, eb, 1, 29, k2[...], lambda p, q: ea[p:q], side2)
     total = jnp.zeros((32, 128), F32)
-    for p, q in chunks(2, 28, 13):
+    for p, q in chunks(2, 28):
         mid, near = around(eb, p, q)
         value = ra[p:q] - times(mid, m2[...]) + S2 * near
         x = ix * 8 + rows(value.shape, 0) + (p - H2)
@@ -489,21 +537,18 @@
         jnp.concatenate([gx2[:, t, pl.ds(2 + a, 16, stride=2), :] for t in range(2)], axis=2) for a in range(4)
     ]
     gy = ((gy[0] + gy[3]) + 3.0 * (gy[1] + gy[2])) * 0.125
-    fold = restrict_matrix(place_2, 256, place_3, 128, iz, 2, 65)
     mask = plane_mask((12, 16, 128), 3, ix, iy, H3)
-    right3 = times_exact(gy, fold) * mask
+    right3 = times_exact(gy, fold2[...]) * mask
     factor3 = f3[0:1, :].reshape(1, 1, 128)
     e3[...] = right3 * factor3
     side3[...] = mask * (factor3 * S3)
     c3[...] = jnp.zeros((12, 16, 128), F32)
-    relax(e3, c3, 1, 11, 10, k3[...], lambda p, q: e3[p:q], side3)
-    grow = prolong_matrix(place_3, 128, place_2, 128, iz, 2, 69)
-    cz = times_exact(c3[...], grow)
+    relax(e3, c3, 1, 11, k3[...], lambda p, q: e3[p:q], side3)
+    cz = times_exact(c3[...], grow2[...])
     below, above = pltpu.roll(cz, 1, 1), pltpu.roll(cz, 15, 1)
     cy2[...] = jnp.zeros((12, 32, 128), F32)
     cy2[:, pl.ds(3, 12, stride=2), :] = (0.75 * cz + 0.25 * below)[:, :12]
     cy2[:, pl.ds(4, 12, stride=2), :] = (0.75 * cz + 0.25 * above)[:, :12]
-    ua2, ub2 = r3, gx2
     fr2 = f2[0:1, :128].reshape(1, 1, 128)
     for xf in range(6, 24):
         f = xf - H2
@@ -515,7 +560,7 @@
         ea[xf, :, :128] = eb[xf, :, :128] + ok * (0.75 * cy2[j] + 0.25 * cy2[other])
 
     def relax_2(src, dst, a, b):
-        for p, q in chunks(a, b, 8):
+        for p, q in chunks(a, b):
             mid = src[p:q, :, :128]
             near = (src[p + 1 : q + 1, :, :128] + src[p - 1 : q - 1, :, :128]) + (
                 pltpu.roll(mid, 1, 1) + pltpu.roll(mid, 31, 1)
@@ -524,51 +569,45 @@
 
     relax_2(ea, eb, 7, 23)
     relax_2(eb, ea, 8, 22)
-    grow = prolong_matrix(place_2, 128, place_1, 128, iz, 1, 41)
     for p in range(14):
         r3[p] = ea[8 + p, :, :128]
-    r3[...] = times_exact(r3[...], grow)
+    r3[...] = times_exact(r3[...], grow1[...])
     cy1[...] = jnp.zeros((14, 32, 128), F32)
     cy1[:, pl.ds(1, 12, stride=2), :] = 0.75 * r3[:, 9:21, :] + 0.25 * r3[:, 8:20, :]
     cy1[:, pl.ds(2, 12, stride=2), :] = 0.75 * r3[:, 9:21, :] + 0.25 * r3[:, 10:22, :]
     fr1 = f1[0:1, :128].reshape(1, 1, 128)
-    for xf in range(26):
+    for xf in range(1, 25):
         f = xf - H1
         xr = ix * 16 + f
         y = iy * 16 + yrow - H1
         ok = jnp.where((y >= 0) & (y < NY // 2), jnp.where((xr >= 0) & (xr < NX // 2), 1.0, 0.0), 0.0)
-        side1[xf] = ok * (f1[0:1, :128] * S1)
-        if 1 <= xf <= 24:
-            j = f // 2 + 3
-            other = j - 1 if f % 2 == 0 else j + 1
-            ua[xf] = e1s[xf] + ok * (0.75 * cy1[j] + 0.25 * cy1[other])
-    relax(ua, ub, 2, 24, 11, k1[...], lambda p, q: fr1 * r1s[p:q], side1)
-    relax(ub, ua, 3, 23, 10, k1[...], lambda p, q: fr1 * r1s[p:q], side1)
-    grow = prolong_matrix(place_1, 128, place_0, 256, iz, 0, 36)
-    for p, q in chunks(0, 20, 10):
-        cz = times_exact(ua[3 + p : 3 + q], grow)
+        j = f // 2 + 3
+        other = j - 1 if f % 2 == 0 else j + 1
+        ua[xf] = e1s[xf] + ok * (0.75 * cy1[j] + 0.25 * cy1[other])
+    relax(ua, ub, 2, 24, k1[...], lambda p, q: fr1 * r1s[p:q], side1)
+    relax(ub, ua, 3, 23, k1[...], lambda p, q: fr1 * r1s[p:q], side1)
+    for p, q in chunks(0, 20):
+        cz = times_exact(ua[3 + p : 3 + q], grow0[...])
         for t in range(2):
             part = cz[:, :, 128 * t : 128 * t + 128]
             cy0[p:q, t, pl.ds(0, 20, stride=2), :] = 0.75 * part[:, 3:23] + 0.25 * part[:, 2:22]
             cy0[p:q, t, pl.ds(1, 20, stride=2), :] = 0.75 * part[:, 3:23] + 0.25 * part[:, 4:24]
     fr0 = f0[0:1, :].reshape(1, 1, 256)
-    for xf in range(40):
+    for xf in range(1, 39):
         f = xf - H0
         xr = ix * 32 + f
         y = iy * 32 + rows((40, 128), 0) - H0
         ok = jnp.where((y >= 0) & (y < NY), jnp.where((xr >= 0) & (xr < NX), 1.0, 0.0), 0.0)
         for t in range(2):
             part = slice(128 * t, 128 * t + 128)
-            side0[xf, :, part] = ok * (f0[0:1, part] * S0)
-            if 1 <= xf <= 38:
-                j = f // 2 + 2
-                other = j - 1 if f % 2 == 0 else j + 1
-                va[xf, :, part] = e0s[xf, :, part] + ok * (0.75 * cy0[j, t] + 0.25 * cy0[other, t])
-    relax(va, vb, 2, 38, 9, k0[...], lambda p, q: fr0 * r0s[p:q], side0)
-    relax(vb, va, 3, 37, 9, k0[...], lambda p, q: fr0 * r0s[p:q], side0)
+            j = f // 2 + 2
+            other = j - 1 if f % 2 == 0 else j + 1
+            va[xf, :, part] = e0s[xf, :, part] + ok * (0.75 * cy0[j, t] + 0.25 * cy0[other, t])
+    relax(va, vb, 2, 38, k0[...], lambda p, q: fr0 * r0s[p:q], side0)
+    relax(vb, va, 3, 37, k0[...], lambda p, q: fr0 * r0s[p:q], side0)
     total = jnp.zeros((32, 128), F32)
     last = m0[:, :128]
-    for p, q in chunks(4, 36, 8):
+    for p, q in chunks(4, 36):
         mid = va[p:q]
         flat = va[p:q, :, :128]
         near = (va[p + 1 : q + 1, :, :128] + va[p - 1 : q - 1, :, :128]) + (
@@ -617,11 +656,14 @@
 
 def call(kernel, outs, scratches, name, limit=16, away=(), home=()):
     def run(*operands):
-        operands = [x if i in home else pltpu.with_memory_space_constraint(x, pltpu.VMEM) for i, x in enumerate(operands)]
+        operands = [
+            pltpu.with_memory_space_constraint(x, pltpu.HBM if i in home else pltpu.VMEM)
+            for i, x in enumerate(operands)
+        ]
         return pl.pallas_call(
             kernel,
             out_shape=[jax.ShapeDtypeStruct(o.shape, F32) if i in away else o for i, o in enumerate(outs)],
-            in_specs=[pl.BlockSpec(memory_space=pltpu.VMEM)] * len(operands),
+            in_specs=[pl.BlockSpec(memory_space=pltpu.HBM if i in home else pltpu.VMEM) for i in range(len(operands))],
             out_specs=[pl.BlockSpec(memory_space=pl.ANY if i in away else pltpu.VMEM) for i in range(len(outs))],
             scratch_shapes=scratches,
             compiler_params=pltpu.CompilerParams(vmem_limit_bytes=limit * 2**20),
@@ -632,8 +674,10 @@
 
 
 def body(data, weights):
-    own, to_left, to_right = call(
-        prepare_kernel, [f32(32, 32, 128), f32(12, 32, 128), f32(12, 32, 128)], [], "prepare", home=(0, 1)
+    own, w, to_left, to_right = call(
+        prepare_kernel,
+        [f32(32, 32, 128), f32(8, 128), f32(296, 128), f32(296, 128)],
+        [pltpu.SemaphoreType.DMA((5,))], "prepare", home=(0, 1),
     )(data, weights)
     from_right, from_left = shift(to_left, "gz", 1), shift(to_right, "gz", -1)
     tail, first, last = call(
@@ -643,19 +687,29 @@
     low, high = call(edges_0_kernel, [f32(60, 4, 128), f32(60, 4, 128)], [], "edges_0")(own, tail, xlo, xhi)
     ylo, yhi = shift(high, "gy", -1), shift(low, "gy", 1)
     (field,) = call(gather_0_kernel, [f32(40, 40, 256)], [], "gather_0")(own, tail, xlo, xhi)
-    b0, k0, m0, f0 = call(
-        weights_0_kernel, [bf16(768, 256), bf16(768, 256), bf16(768, 256), f32(8, 256)], [], "weights_0"
-    )(from_left, weights, from_right)
-    k1, k1u, m1, f1 = call(
-        weights_1_kernel, [bf16(768, 128), bf16(384, 128), bf16(384, 128), f32(8, 256)], [], "weights_1"
-    )(from_left, weights, from_right)
+    b0, k0, m0, f0, r00, p00, side0 = call(
+        weights_0_kernel,
+        [
+            bf16(768, 256), bf16(768, 256), bf16(768, 256), f32(8, 256), bf16(512, 128), bf16(256, 256),
+            f32(40, 40, 256),
+        ],
+        [], "weights_0",
+    )(from_left, w, from_right)
+    k1, k1u, m1, f1, r01, p01, side1 = call(
+        weights_1_kernel,
+        [
+            bf16(768, 128), bf16(384, 128), bf16(384, 128), f32(8, 256), bf16(256, 128), bf16(256, 128),
+            f32(26, 32, 128),
+        ],
+        [], "weights_1",
+    )(from_left, w, from_right)
     big = (40, 40, 256)
     r1, to_left, to_right, e0s, r0s, stat0 = call(
         down_0_kernel,
         [f32(16, 16, 128), f32(6, 16, 128), f32(6, 16, 128), f32(*big), f32(*big), f32(8, 128)],
-        [scratch(*big), scratch(*big), scratch(*big), scratch(*big), scratch(16, 2, 40, 128)],
+        [scratch(*big), scratch(*big), scratch(*big), scratch(16, 2, 40, 128)],
         "down_0",
-    )(field, ylo, yhi, b0, k0, m0, f0)
+    )(field, ylo, yhi, b0, k0, m0, f0, r00, side0)
     from_right, from_left = shift(to_left, "gz", 1), shift(to_right, "gz", -1)
     wide1, tail1, first, last = call(
         spread_1_kernel, [f32(16, 16, 128), f32(16, 16, 128), f32(6, 16, 128), f32(6, 16, 128)], [], "spread_1"
@@ -667,16 +721,19 @@
     msg, e1s, r1s, stat1 = call(
         down_1_kernel,
         [f32(3, 8, 128), f32(*mid), f32(*mid), f32(8, 128)],
-        [scratch(*mid), scratch(*mid), scratch(*mid), scratch(*mid), scratch(8, 32, 128)],
+        [scratch(*mid), scratch(*mid), scratch(*mid), scratch(8, 32, 128)],
         "down_1",
-    )(wide1, tail1, xlo, xhi, ylo, yhi, k1, m1, f1, weights)
+    )(wide1, tail1, xlo, xhi, ylo, yhi, k1, m1, f1, r01, side1, w)
     near = {k: shift(msg, "gz", k) for k in (1, -1, 2, -2, 3, -3)}
     r2z, wide2 = call(join_kernel, [f32(16, 8, 128), f32(8, 256)], [], "join")(
         msg, near[1], near[2], near[3], near[-3], near[-2], near[-1]
     )
-    k2, k2u, m2, f2, k3, f3 = call(
+    k2, k2u, m2, f2, k3, f3, r02, p02, side2 = call(
         weights_2_kernel,
-        [bf16(768, 256), bf16(384, 128), bf16(768, 256), f32(8, 256), bf16(384, 128), f32(8, 128)],
+        [
+            bf16(768, 256), bf16(384, 128), bf16(768, 256), f32(8, 256), bf16(384, 128), f32(8, 128),
+            bf16(512, 128), bf16(256, 128), f32(30, 32, 256),
+        ],
         [], "weights_coarse",
     )(wide2)
     x1, x2, x3 = shift(r2z, "gx", 1), shift(r2z[:8], "gx", 2), shift(r2z, "gx", 3)
@@ -690,18 +747,21 @@
         up_kernel,
         [f32(32, 32, 128), f32(32, 32, 128), f32(1, 128)],
         [
-            scratch(*lev2), scratch(*lev2), scratch(*lev2), scratch(*lev2), scratch(12, 2, 40, 128),
+            scratch(*lev2), scratch(*lev2), scratch(*lev2), scratch(12, 2, 40, 128),
             scratch(14, 32, 128), scratch(12, 16, 128), scratch(12, 16, 128), scratch(12, 16, 128),
-            scratch(12, 32, 128), scratch(*mid), scratch(*mid), scratch(*mid), scratch(14, 32, 128),
-            scratch(*big), scratch(*big), scratch(*big), scratch(20, 2, 40, 128),
+            scratch(12, 32, 128), scratch(*mid), scratch(*mid), scratch(14, 32, 128),
+            scratch(*big), scratch(*big), scratch(20, 2, 40, 128),
         ],
         "up", 24,
-    )(r2x, ya, yb, yc, yd, k2, k2u, m2, f2, k3, f3, k1u, f1, e1s, r1s, k0, m0, f0, e0s, r0s, stat0, stat1)
+    )(
+        r2x, ya, yb, yc, yd, k2, k2u, m2, f2, k3, f3, r02, p02, side2,
+        k1u, f1, e1s, r1s, p01, side1, k0, m0, f0, e0s, r0s, p00, side0, stat0, stat1,
+    )
     sol, res = call(
         store_kernel, [f32(32, 32, 128), f32(32, 32, 128)], [pltpu.SemaphoreType.DMA((2,))], "store", 4, (0, 1)
     )(sol, res)
     t = stat
-    for axis, flips in (("gy", (1,)), ("gx", (1, 2, 3)), ("gy", (2, 4, 6)), ("gz", (1, 2, 3)), ("gz", (7,))):
+    for axis, flips in (("gy", (1,)), ("gx", (1,)), ("gx", (3,)), ("gy", (2,)), ("gy", (6,)), ("gz", (1, 2, 3)), ("gz", (7,))):
         others = [swap(t, axis, f) for f in flips]
         t = t + others[0]
         if len(others) > 1:

time: 114 us -> 115 us (level)
  waiting for transfers between devices: 40.4 us -> 46.1 us
  starting transfers between devices: 54.5 us -> 49.9 us
  local copies, waits for them, and re-layouts: 1.73 us -> 0.01 us
  Pallas kernels: 15.8 us -> 17.1 us
    ppermute x11 -> x9, waiting for transfers between devices: 12 us -> 19.1 us  [swap(): lax.ppermute(x, axis, [(i ^ flip, i) for i in range(lax.axis_size(axis))])]
    ppermute x11 -> x9, starting transfers between devices: 17 us -> 12.5 us  [swap(): lax.ppermute(x, axis, [(i ^ flip, i) for i in range(lax.axis_size(axis))])]
    unnamed x8 -> x2, local copies, waits for them, and re-layouts: 1.73 us -> 0.01 us
    ppermute x25, waiting for transfers between devices: 28.4 us -> 27 us  [shift(): return lax.ppermute(x, axis, [((i + k) % n, i) for i in range(n)])]
    pallas_call x15, Pallas kernels: 15.8 us -> 17.1 us  [run(): pl.pallas_call(kernel, out_shape=[jax.ShapeDtypeStruct(o.shape, F32) if i...]
  transfers between devices with their start and end apart: 36 -> 34, of which waited for: 23 -> 23; matrix products, arithmetic and copies ran while one was open for 0% -> 0% of each run, Pallas kernels for 3% -> 4%
where the time goes in v4:
time: 115 us; the launch traced here: 114 us
  starting transfers between devices  49.9 us (43%)
  waiting for transfers between devices  46.1 us (40%)
  Pallas kernels  17.1 us (15%)
    ppermute x25, starting transfers between devices, shift(): return lax.ppermute(x, axis, [((i + k) % n, i) for i in range(n)])  37.5 us
    ppermute x25, waiting for transfers between devices, shift(): return lax.ppermute(x, axis, [((i + k) % n, i) for i in range(n)])  27 us
    ppermute x9, waiting for transfers between devices, swap(): lax.ppermute(x, axis, [(i ^ flip, i) for i in range(lax.axis_size(axis))])  19.1 us
    pallas_call x15, Pallas kernels, run(): pl.pallas_call(kernel, out_shape=[jax.ShapeDtypeStruct(o.shape, F32) if i...  17.1 us
    ppermute x9, starting transfers between devices, swap(): lax.ppermute(x, axis, [(i ^ flip, i) for i in range(lax.axis_size(axis))])  12.5 us
  transfers between devices with their start and end apart: 34, of which 23 were waited for; matrix products, arithmetic and copies ran while one was open for 0% of the time, Pallas kernels for 4%

profile of v4, /device:TPU:32, one launch (start us, length us, event | category | flops | bytes accessed | tf_op | source)
XLA Modules:
  0.0 114.5 jit_solution(14942444770414014468)
XLA Ops:
  0.6 1.7 %prepare.1 = (f32[32,32,128]{2,1,0:T(8,128)S(1)}, f32[8,128]{1,0:T(8,128)S(1)}, f32[296,128]{1,0:T(8,128)S(1)}, f32[296,128]{1,0:T(8,128)S(1)}) custom-call(f32[32,32,128]{2,1,0:T(8,128)} %data.1, f32[8,128]{1,0:T(8,128)} %weights.1), custom_call_target="tpu_custom_call" | custom-call | tf_op jit(solution)/shard_map/prepare/pallas_call | solution.py:663
  2.3 1.9 %collective-permute-start = (f32[296,128]{1,0:T(8,128)S(1)}, f32[296,128]{1,0:T(8,128)S(1)}, u32[]{:S(2)}, u32[]{:S(2)}) collective-permute-start(f32[296,128]{1,0:T(8,128)S(1)} %get-tuple-element.62), channel_id=1, source_target_pairs={{1,0},{2,1},{3,2},{4,3},{5,4},{6,5},{7,6},{0,7},{9,8},{10,9},{11,1... | collective-permute-start | bytes 454664 | tf_op jit(solution)/shard_map/ppermute | solution.py:638
  4.4 3.8 %collective-permute-done.from_right.right = f32[296,128]{1,0:T(8,128)S(1)} collective-permute-done((f32[296,128]{1,0:T(8,128)S(1)}, f32[296,128]{1,0:T(8,128)S(1)}, u32[]{:S(2)}, u32[]{:S(2)}) %collective-permute-start) | collective-permute-done | bytes 151584 | tf_op jit(solution)/shard_map/ppermute | solution.py:638
  8.2 3.8 %collective-permute-done.1.from_left.left = f32[296,128]{1,0:T(8,128)S(1)} collective-permute-done((f32[296,128]{1,0:T(8,128)S(1)}, f32[296,128]{1,0:T(8,128)S(1)}, u32[]{:S(2)}, u32[]{:S(2)}) %collective-permute-start.1) | collective-permute-done | bytes 151584 | tf_op jit(solution)/shard_map/ppermute | solution.py:638
  14.3 1.7 %collective-permute-start.3 = (f32[5,32,128]{2,1,0:T(8,128)S(1)}, f32[5,32,128]{2,1,0:T(8,128)S(1)}, u32[]{:S(2)}, u32[]{:S(2)}) collective-permute-start(f32[5,32,128]{2,1,0:T(8,128)S(1)} %get-tuple-element.66), channel_id=1, source_target_pairs={{64,0},{128,64},{192,128},{0,192},{65,1},{129,65},{193,129},{1,193... | collective-permute-start | bytes 245768 | tf_op jit(solution)/shard_map/ppermute | solution.py:638
  15.9 2.4 %collective-permute-done.2.xlo = f32[5,32,128]{2,1,0:T(8,128)S(1)} collective-permute-done((f32[5,32,128]{2,1,0:T(8,128)S(1)}, f32[5,32,128]{2,1,0:T(8,128)S(1)}, u32[]{:S(2)}, u32[]{:S(2)}) %collective-permute-start.2) | collective-permute-done | bytes 81952 | tf_op jit(solution)/shard_map/ppermute | solution.py:638
  18.9 2.9 %collective-permute-start.5 = (f32[60,4,128]{2,1,0:T(4,128)S(1)}, f32[60,4,128]{2,1,0:T(4,128)S(1)}, u32[]{:S(2)}, u32[]{:S(2)}) collective-permute-start(f32[60,4,128]{2,1,0:T(4,128)S(1)} %get-tuple-element.68), channel_id=1, source_target_pairs={{8,0},{16,8},{24,16},{32,24},{40,32},{48,40},{56,48},{0,56},{9,1},... | collective-permute-start | bytes 368648 | tf_op jit(solution)/shard_map/ppermute | solution.py:638
  24.5 3.3 %down_0.1 = (f32[16,16,128]{2,1,0:T(8,128)S(1)}, f32[6,16,128]{2,1,0:T(8,128)S(1)}, f32[6,16,128]{2,1,0:T(8,128)S(1)}, f32[40,40,256]{2,1,0:T(8,128)S(1)}, f32[4...) custom-call(f32[40,40,256]{2,1,0:T(8,128)S(1)} %gather_0.1.field, f32[60,4,128]{2,1,0:T(4,128)S(1)} %collective-permute-done.4.ylo, ...), custom_call_target="tpu_custom_call" | custom-call | tf_op jit(solution)/shard_map/down_0/pallas_call | solution.py:663
  27.7 3.1 %collective-permute-start.6 = (f32[6,16,128]{2,1,0:T(8,128)S(1)}, f32[6,16,128]{2,1,0:T(8,128)S(1)}, u32[]{:S(2)}, u32[]{:S(2)}) collective-permute-start(f32[6,16,128]{2,1,0:T(8,128)S(1)} %get-tuple-element.77), channel_id=1, source_target_pairs={{1,0},{2,1},{3,2},{4,3},{5,4},{6,5},{7,6},{0,7},{9,8},{10,9},{11,1... | collective-permute-start | bytes 147464 | tf_op jit(solution)/shard_map/ppermute | solution.py:638
  30.8 1.7 %collective-permute-done.6.from_right = f32[6,16,128]{2,1,0:T(8,128)S(1)} collective-permute-done((f32[6,16,128]{2,1,0:T(8,128)S(1)}, f32[6,16,128]{2,1,0:T(8,128)S(1)}, u32[]{:S(2)}, u32[]{:S(2)}) %collective-permute-start.6) | collective-permute-done | bytes 49184 | tf_op jit(solution)/shard_map/ppermute | solution.py:638
  32.5 2.3 %collective-permute-done.7.from_left = f32[6,16,128]{2,1,0:T(8,128)S(1)} collective-permute-done((f32[6,16,128]{2,1,0:T(8,128)S(1)}, f32[6,16,128]{2,1,0:T(8,128)S(1)}, u32[]{:S(2)}, u32[]{:S(2)}) %collective-permute-start.7) | collective-permute-done | bytes 49184 | tf_op jit(solution)/shard_map/ppermute | solution.py:638
  35.0 1.7 %collective-permute-start.8 = (f32[6,16,128]{2,1,0:T(8,128)S(1)}, f32[6,16,128]{2,1,0:T(8,128)S(1)}, u32[]{:S(2)}, u32[]{:S(2)}) collective-permute-start(f32[6,16,128]{2,1,0:T(8,128)S(1)} %get-tuple-element.81), channel_id=1, source_target_pairs={{192,0},{0,64},{64,128},{128,192},{193,1},{1,65},{65,129},{129,193... | collective-permute-start | bytes 147464 | tf_op jit(solution)/shard_map/ppermute | solution.py:638
  36.7 1.7 %collective-permute-start.9 = (f32[6,16,128]{2,1,0:T(8,128)S(1)}, f32[6,16,128]{2,1,0:T(8,128)S(1)}, u32[]{:S(2)}, u32[]{:S(2)}) collective-permute-start(f32[6,16,128]{2,1,0:T(8,128)S(1)} %get-tuple-element.82), channel_id=1, source_target_pairs={{64,0},{128,64},{192,128},{0,192},{65,1},{129,65},{193,129},{1,193... | collective-permute-start | bytes 147464 | tf_op jit(solution)/shard_map/ppermute | solution.py:638
  38.3 2.1 %collective-permute-done.8.xlo = f32[6,16,128]{2,1,0:T(8,128)S(1)} collective-permute-done((f32[6,16,128]{2,1,0:T(8,128)S(1)}, f32[6,16,128]{2,1,0:T(8,128)S(1)}, u32[]{:S(2)}, u32[]{:S(2)}) %collective-permute-start.8) | collective-permute-done | bytes 49184 | tf_op jit(solution)/shard_map/ppermute | solution.py:638
  40.8 2.9 %collective-permute-start.11 = (f32[26,8,128]{2,1,0:T(8,128)S(1)}, f32[26,8,128]{2,1,0:T(8,128)S(1)}, u32[]{:S(2)}, u32[]{:S(2)}) collective-permute-start(f32[26,8,128]{2,1,0:T(8,128)S(1)} %get-tuple-element.84), channel_id=1, source_target_pairs={{8,0},{16,8},{24,16},{32,24},{40,32},{48,40},{56,48},{0,56},{9,1},... | collective-permute-start | bytes 319496 | tf_op jit(solution)/shard_map/ppermute | solution.py:638
  47.1 2.2 %collective-permute-start.16 = (f32[3,8,128]{2,1,0:T(8,128)S(1)}, f32[3,8,128]{2,1,0:T(8,128)S(1)}, u32[]{:S(2)}, u32[]{:S(2)}) collective-permute-start(f32[3,8,128]{2,1,0:T(8,128)S(1)} %get-tuple-element.90.own), channel_id=1, source_target_pairs={{6,0},{7,1},{0,2},{1,3},{2,4},{3,5},{4,6},{5,7},{14,8},{15,9},{8,1... | collective-permute-start | bytes 36872 | tf_op jit(solution)/shard_map/ppermute | solution.py:638
  51.0 3.4 %collective-permute-start.14 = (f32[3,8,128]{2,1,0:T(8,128)S(1)}, f32[3,8,128]{2,1,0:T(8,128)S(1)}, u32[]{:S(2)}, u32[]{:S(2)}) collective-permute-start(f32[3,8,128]{2,1,0:T(8,128)S(1)} %get-tuple-element.90.own), channel_id=1, source_target_pairs={{3,0},{4,1},{5,2},{6,3},{7,4},{0,5},{1,6},{2,7},{11,8},{12,9},{13,... | collective-permute-start | bytes 36872 | tf_op jit(solution)/shard_map/ppermute | solution.py:638
  55.2 3.1 %collective-permute-start.12 = (f32[3,8,128]{2,1,0:T(8,128)S(1)}, f32[3,8,128]{2,1,0:T(8,128)S(1)}, u32[]{:S(2)}, u32[]{:S(2)}) collective-permute-start(f32[3,8,128]{2,1,0:T(8,128)S(1)} %get-tuple-element.90.own), channel_id=1, source_target_pairs={{1,0},{2,1},{3,2},{4,3},{5,4},{6,5},{7,6},{0,7},{9,8},{10,9},{11,1... | collective-permute-start | bytes 36872 | tf_op jit(solution)/shard_map/ppermute | solution.py:638
  61.2 2.0 %collective-permute-start.18 = (f32[16,8,128]{2,1,0:T(8,128)S(1)}, f32[16,8,128]{2,1,0:T(8,128)S(1)}, u32[]{:S(2)}, u32[]{:S(2)}) collective-permute-start(f32[16,8,128]{2,1,0:T(8,128)S(1)} %get-tuple-element.91.own), channel_id=1, source_target_pairs={{64,0},{128,64},{192,128},{0,192},{65,1},{129,65},{193,129},{1,193... | collective-permute-start | bytes 196616 | tf_op jit(solution)/shard_map/ppermute | solution.py:638
  64.7 3.9 %collective-permute-done.19.x2 = f32[8,8,128]{2,1,0:T(8,128)S(1)} collective-permute-done((f32[8,8,128]{2,1,0:T(8,128)S(1)}, f32[8,8,128]{2,1,0:T(8,128)S(1)}, u32[]{:S(2)}, u32[]{:S(2)}) %collective-permute-start.19) | collective-permute-done | bytes 32800 | tf_op jit(solution)/shard_map/ppermute | solution.py:638
  69.1 3.2 %collective-permute-start.24 = (f32[18,3,128]{2,1,0:T(4,128)S(1)}, f32[18,3,128]{2,1,0:T(4,128)S(1)}, u32[]{:S(2)}, u32[]{:S(2)}) collective-permute-start(f32[18,3,128]{2,1,0:T(4,128)S(1)} %get-tuple-element.94), channel_id=1, source_target_pairs={{16,0},{24,8},{32,16},{40,24},{48,32},{56,40},{0,48},{8,56},{17,1}... | collective-permute-start | bytes 82952 | tf_op jit(solution)/shard_map/ppermute | solution.py:638
  75.4 6.0 %up.1 = (f32[32,32,128]{2,1,0:T(8,128)S(1)}, f32[32,32,128]{2,1,0:T(8,128)S(1)}, f32[1,128]{1,0:T(1,128)S(1)}) custom-call(f32[50,8,128]{2,1,0:T(8,128)S(1)} %get-tuple-element.92.r2x, f32[50,8,128]{2,1,0:T(8,128)S(1)} %collective-permute-done.21.ya, f32[50,8,128]{2,1,0:T(8,128)S(1)} %collective-permute-done.22.yb, ...), custom_call_target="tpu_custom_call" | custom-call | tf_op jit(solution)/shard_map/up/pallas_call | solution.py:663
  82.7 3.5 %collective-permute-done.26 = f32[1,128]{1,0:T(1,128)S(1)} collective-permute-done((f32[1,128]{1,0:T(1,128)S(1)}, f32[1,128]{1,0:T(1,128)S(1)}, u32[]{:S(2)}, u32[]{:S(2)}) %collective-permute-start.26) | collective-permute-done | bytes 544 | tf_op jit(solution)/shard_map/ppermute | solution.py:642
  86.2 1.7 %collective-permute-start.27 = (f32[1,128]{1,0:T(1,128)S(1)}, f32[1,128]{1,0:T(1,128)S(1)}, u32[]{:S(2)}, u32[]{:S(2)}) collective-permute-start(f32[1,128]{1,0:T(1,128)S(1)} %add.28), channel_id=1, source_target_pairs={{192,0},{128,64},{64,128},{0,192},{193,1},{129,65},{65,129},{1,193... | collective-permute-start | bytes 1544 | tf_op jit(solution)/shard_map/ppermute | solution.py:642
  87.8 3.1 %collective-permute-done.27 = f32[1,128]{1,0:T(1,128)S(1)} collective-permute-done((f32[1,128]{1,0:T(1,128)S(1)}, f32[1,128]{1,0:T(1,128)S(1)}, u32[]{:S(2)}, u32[]{:S(2)}) %collective-permute-start.27) | collective-permute-done | bytes 544 | tf_op jit(solution)/shard_map/ppermute | solution.py:642
  90.9 3.5 %collective-permute-done.28 = f32[1,128]{1,0:T(1,128)S(1)} collective-permute-done((f32[1,128]{1,0:T(1,128)S(1)}, f32[1,128]{1,0:T(1,128)S(1)}, u32[]{:S(2)}, u32[]{:S(2)}) %collective-permute-start.28) | collective-permute-done | bytes 544 | tf_op jit(solution)/shard_map/ppermute | solution.py:642
  94.5 2.1 %collective-permute-start.29 = (f32[1,128]{1,0:T(1,128)S(1)}, f32[1,128]{1,0:T(1,128)S(1)}, u32[]{:S(2)}, u32[]{:S(2)}) collective-permute-start(f32[1,128]{1,0:T(1,128)S(1)} %add.30), channel_id=1, source_target_pairs={{48,0},{56,8},{32,16},{40,24},{16,32},{24,40},{0,48},{8,56},{49,1}... | collective-permute-start | bytes 1544 | tf_op jit(solution)/shard_map/ppermute | solution.py:642
  96.6 2.6 %collective-permute-done.29 = f32[1,128]{1,0:T(1,128)S(1)} collective-permute-done((f32[1,128]{1,0:T(1,128)S(1)}, f32[1,128]{1,0:T(1,128)S(1)}, u32[]{:S(2)}, u32[]{:S(2)}) %collective-permute-start.29) | collective-permute-done | bytes 544 | tf_op jit(solution)/shard_map/ppermute | solution.py:642
  100.7 3.2 %collective-permute-start.31 = (f32[1,128]{1,0:T(1,128)S(1)}, f32[1,128]{1,0:T(1,128)S(1)}, u32[]{:S(2)}, u32[]{:S(2)}) collective-permute-start(f32[1,128]{1,0:T(1,128)S(1)} %add.31), channel_id=1, source_target_pairs={{2,0},{3,1},{0,2},{1,3},{6,4},{7,5},{4,6},{5,7},{10,8},{11,9},{8,1... | collective-permute-start | bytes 1544 | tf_op jit(solution)/shard_map/ppermute | solution.py:642
  105.4 2.0 %collective-permute-done.30 = f32[1,128]{1,0:T(1,128)S(1)} collective-permute-done((f32[1,128]{1,0:T(1,128)S(1)}, f32[1,128]{1,0:T(1,128)S(1)}, u32[]{:S(2)}, u32[]{:S(2)}) %collective-permute-start.30) | collective-permute-done | bytes 544 | tf_op jit(solution)/shard_map/ppermute | solution.py:642
  107.4 3.6 %collective-permute-start.33 = (f32[1,128]{1,0:T(1,128)S(1)}, f32[1,128]{1,0:T(1,128)S(1)}, u32[]{:S(2)}, u32[]{:S(2)}) collective-permute-start(f32[1,128]{1,0:T(1,128)S(1)} %add_add_fusion), channel_id=1, source_target_pairs={{7,0},{6,1},{5,2},{4,3},{3,4},{2,5},{1,6},{0,7},{15,8},{14,9},{13,... | collective-permute-start | bytes 1544 | tf_op jit(solution)/shard_map/ppermute | solution.py:642
  112.0 2.0 %collective-permute-done.33 = f32[1,128]{1,0:T(1,128)S(1)} collective-permute-done((f32[1,128]{1,0:T(1,128)S(1)}, f32[1,128]{1,0:T(1,128)S(1)}, u32[]{:S(2)}, u32[]{:S(2)}) %collective-permute-start.33) | collective-permute-done | bytes 544 | tf_op jit(solution)/shard_map/ppermute | solution.py:642
  (62 shorter events, 25.7 us)
Async XLA Ops:
  2.3 5.9 %collective-permute-start = (f32[296,128]{1,0:T(8,128)S(1)}, f32[296,128]{1,0:T(8,128)S(1)}, u32[]{:S(2)}, u32[]{:S(2)}) collective-permute-start(f32[296,128]{1,0:T(8,128)S(1)} %get-tuple-element.62), channel_id=1, source_target_pairs={{1,0},{2,1},{3,2},{4,3},{5,4},{6,5},{7,6},{0,7},{9,8},{10,9},{11,1... | collective-permute-start | bytes 454664 | tf_op jit(solution)/shard_map/ppermute | solution.py:638
  4.2 7.8 %collective-permute-start.1 = (f32[296,128]{1,0:T(8,128)S(1)}, f32[296,128]{1,0:T(8,128)S(1)}, u32[]{:S(2)}, u32[]{:S(2)}) collective-permute-start(f32[296,128]{1,0:T(8,128)S(1)} %get-tuple-element.63), channel_id=1, source_target_pairs={{7,0},{0,1},{1,2},{2,3},{3,4},{4,5},{5,6},{6,7},{15,8},{8,9},{9,10... | collective-permute-start | bytes 454664 | tf_op jit(solution)/shard_map/ppermute | solution.py:638
  12.7 5.7 %collective-permute-start.2 = (f32[5,32,128]{2,1,0:T(8,128)S(1)}, f32[5,32,128]{2,1,0:T(8,128)S(1)}, u32[]{:S(2)}, u32[]{:S(2)}) collective-permute-start(f32[5,32,128]{2,1,0:T(8,128)S(1)} %get-tuple-element.65), channel_id=1, source_target_pairs={{192,0},{0,64},{64,128},{128,192},{193,1},{1,65},{65,129},{129,193... | collective-permute-start | bytes 245768 | tf_op jit(solution)/shard_map/ppermute | solution.py:638
  14.3 4.4 %collective-permute-start.3 = (f32[5,32,128]{2,1,0:T(8,128)S(1)}, f32[5,32,128]{2,1,0:T(8,128)S(1)}, u32[]{:S(2)}, u32[]{:S(2)}) collective-permute-start(f32[5,32,128]{2,1,0:T(8,128)S(1)} %get-tuple-element.66), channel_id=1, source_target_pairs={{64,0},{128,64},{192,128},{0,192},{65,1},{129,65},{193,129},{1,193... | collective-permute-start | bytes 245768 | tf_op jit(solution)/shard_map/ppermute | solution.py:638
  18.9 5.5 %collective-permute-start.4 = (f32[60,4,128]{2,1,0:T(4,128)S(1)}, f32[60,4,128]{2,1,0:T(4,128)S(1)}, u32[]{:S(2)}, u32[]{:S(2)}) collective-permute-start(f32[60,4,128]{2,1,0:T(4,128)S(1)} %get-tuple-element.67), channel_id=1, source_target_pairs={{56,0},{0,8},{8,16},{16,24},{24,32},{32,40},{40,48},{48,56},{57,1}... | collective-permute-start | bytes 368648 | tf_op jit(solution)/shard_map/ppermute | solution.py:638
  18.9 5.5 %collective-permute-start.5 = (f32[60,4,128]{2,1,0:T(4,128)S(1)}, f32[60,4,128]{2,1,0:T(4,128)S(1)}, u32[]{:S(2)}, u32[]{:S(2)}) collective-permute-start(f32[60,4,128]{2,1,0:T(4,128)S(1)} %get-tuple-element.68), channel_id=1, source_target_pairs={{8,0},{16,8},{24,16},{32,24},{40,32},{48,40},{56,48},{0,56},{9,1},... | collective-permute-start | bytes 368648 | tf_op jit(solution)/shard_map/ppermute | solution.py:638
  27.7 4.8 %collective-permute-start.6 = (f32[6,16,128]{2,1,0:T(8,128)S(1)}, f32[6,16,128]{2,1,0:T(8,128)S(1)}, u32[]{:S(2)}, u32[]{:S(2)}) collective-permute-start(f32[6,16,128]{2,1,0:T(8,128)S(1)} %get-tuple-element.77), channel_id=1, source_target_pairs={{1,0},{2,1},{3,2},{4,3},{5,4},{6,5},{7,6},{0,7},{9,8},{10,9},{11,1... | collective-permute-start | bytes 147464 | tf_op jit(solution)/shard_map/ppermute | solution.py:638
  30.8 4.1 %collective-permute-start.7 = (f32[6,16,128]{2,1,0:T(8,128)S(1)}, f32[6,16,128]{2,1,0:T(8,128)S(1)}, u32[]{:S(2)}, u32[]{:S(2)}) collective-permute-start(f32[6,16,128]{2,1,0:T(8,128)S(1)} %get-tuple-element.78), channel_id=1, source_target_pairs={{7,0},{0,1},{1,2},{2,3},{3,4},{4,5},{5,6},{6,7},{15,8},{8,9},{9,10... | collective-permute-start | bytes 147464 | tf_op jit(solution)/shard_map/ppermute | solution.py:638
  35.0 5.4 %collective-permute-start.8 = (f32[6,16,128]{2,1,0:T(8,128)S(1)}, f32[6,16,128]{2,1,0:T(8,128)S(1)}, u32[]{:S(2)}, u32[]{:S(2)}) collective-permute-start(f32[6,16,128]{2,1,0:T(8,128)S(1)} %get-tuple-element.81), channel_id=1, source_target_pairs={{192,0},{0,64},{64,128},{128,192},{193,1},{1,65},{65,129},{129,193... | collective-permute-start | bytes 147464 | tf_op jit(solution)/shard_map/ppermute | solution.py:638
  36.7 4.1 %collective-permute-start.9 = (f32[6,16,128]{2,1,0:T(8,128)S(1)}, f32[6,16,128]{2,1,0:T(8,128)S(1)}, u32[]{:S(2)}, u32[]{:S(2)}) collective-permute-start(f32[6,16,128]{2,1,0:T(8,128)S(1)} %get-tuple-element.82), channel_id=1, source_target_pairs={{64,0},{128,64},{192,128},{0,192},{65,1},{129,65},{193,129},{1,193... | collective-permute-start | bytes 147464 | tf_op jit(solution)/shard_map/ppermute | solution.py:638
  40.8 5.4 %collective-permute-start.10 = (f32[26,8,128]{2,1,0:T(8,128)S(1)}, f32[26,8,128]{2,1,0:T(8,128)S(1)}, u32[]{:S(2)}, u32[]{:S(2)}) collective-permute-start(f32[26,8,128]{2,1,0:T(8,128)S(1)} %get-tuple-element.83), channel_id=1, source_target_pairs={{56,0},{0,8},{8,16},{16,24},{24,32},{32,40},{40,48},{48,56},{57,1}... | collective-permute-start | bytes 319496 | tf_op jit(solution)/shard_map/ppermute | solution.py:638
  40.8 5.3 %collective-permute-start.11 = (f32[26,8,128]{2,1,0:T(8,128)S(1)}, f32[26,8,128]{2,1,0:T(8,128)S(1)}, u32[]{:S(2)}, u32[]{:S(2)}) collective-permute-start(f32[26,8,128]{2,1,0:T(8,128)S(1)} %get-tuple-element.84), channel_id=1, source_target_pairs={{8,0},{16,8},{24,16},{32,24},{40,32},{48,40},{56,48},{0,56},{9,1},... | collective-permute-start | bytes 319496 | tf_op jit(solution)/shard_map/ppermute | solution.py:638
  47.1 8.1 %collective-permute-start.17 = (f32[3,8,128]{2,1,0:T(8,128)S(1)}, f32[3,8,128]{2,1,0:T(8,128)S(1)}, u32[]{:S(2)}, u32[]{:S(2)}) collective-permute-start(f32[3,8,128]{2,1,0:T(8,128)S(1)} %get-tuple-element.90.own), channel_id=1, source_target_pairs={{7,0},{0,1},{1,2},{2,3},{3,4},{4,5},{5,6},{6,7},{15,8},{8,9},{9,10... | collective-permute-start | bytes 36872 | tf_op jit(solution)/shard_map/ppermute | solution.py:638
  47.1 11.2 %collective-permute-start.16 = (f32[3,8,128]{2,1,0:T(8,128)S(1)}, f32[3,8,128]{2,1,0:T(8,128)S(1)}, u32[]{:S(2)}, u32[]{:S(2)}) collective-permute-start(f32[3,8,128]{2,1,0:T(8,128)S(1)} %get-tuple-element.90.own), channel_id=1, source_target_pairs={{6,0},{7,1},{0,2},{1,3},{2,4},{3,5},{4,6},{5,7},{14,8},{15,9},{8,1... | collective-permute-start | bytes 36872 | tf_op jit(solution)/shard_map/ppermute | solution.py:638
  49.3 9.0 %collective-permute-start.15 = (f32[3,8,128]{2,1,0:T(8,128)S(1)}, f32[3,8,128]{2,1,0:T(8,128)S(1)}, u32[]{:S(2)}, u32[]{:S(2)}) collective-permute-start(f32[3,8,128]{2,1,0:T(8,128)S(1)} %get-tuple-element.90.own), channel_id=1, source_target_pairs={{5,0},{6,1},{7,2},{0,3},{1,4},{2,5},{3,6},{4,7},{13,8},{14,9},{15,... | collective-permute-start | bytes 36872 | tf_op jit(solution)/shard_map/ppermute | solution.py:638
  51.0 7.4 %collective-permute-start.14 = (f32[3,8,128]{2,1,0:T(8,128)S(1)}, f32[3,8,128]{2,1,0:T(8,128)S(1)}, u32[]{:S(2)}, u32[]{:S(2)}) collective-permute-start(f32[3,8,128]{2,1,0:T(8,128)S(1)} %get-tuple-element.90.own), channel_id=1, source_target_pairs={{3,0},{4,1},{5,2},{6,3},{7,4},{0,5},{1,6},{2,7},{11,8},{12,9},{13,... | collective-permute-start | bytes 36872 | tf_op jit(solution)/shard_map/ppermute | solution.py:638
  54.4 4.6 %collective-permute-start.13 = (f32[3,8,128]{2,1,0:T(8,128)S(1)}, f32[3,8,128]{2,1,0:T(8,128)S(1)}, u32[]{:S(2)}, u32[]{:S(2)}) collective-permute-start(f32[3,8,128]{2,1,0:T(8,128)S(1)} %get-tuple-element.90.own), channel_id=1, source_target_pairs={{2,0},{3,1},{4,2},{5,3},{6,4},{7,5},{0,6},{1,7},{10,8},{11,9},{12,... | collective-permute-start | bytes 36872 | tf_op jit(solution)/shard_map/ppermute | solution.py:638
  55.2 4.6 %collective-permute-start.12 = (f32[3,8,128]{2,1,0:T(8,128)S(1)}, f32[3,8,128]{2,1,0:T(8,128)S(1)}, u32[]{:S(2)}, u32[]{:S(2)}) collective-permute-start(f32[3,8,128]{2,1,0:T(8,128)S(1)} %get-tuple-element.90.own), channel_id=1, source_target_pairs={{1,0},{2,1},{3,2},{4,3},{5,4},{6,5},{7,6},{0,7},{9,8},{10,9},{11,1... | collective-permute-start | bytes 36872 | tf_op jit(solution)/shard_map/ppermute | solution.py:638
  59.8 8.7 %collective-permute-start.20 = (f32[16,8,128]{2,1,0:T(8,128)S(1)}, f32[16,8,128]{2,1,0:T(8,128)S(1)}, u32[]{:S(2)}, u32[]{:S(2)}) collective-permute-start(f32[16,8,128]{2,1,0:T(8,128)S(1)} %get-tuple-element.91.own), channel_id=1, source_target_pairs={{192,0},{0,64},{64,128},{128,192},{193,1},{1,65},{65,129},{129,193... | collective-permute-start | bytes 196616 | tf_op jit(solution)/shard_map/ppermute | solution.py:638
  61.2 7.4 %collective-permute-start.18 = (f32[16,8,128]{2,1,0:T(8,128)S(1)}, f32[16,8,128]{2,1,0:T(8,128)S(1)}, u32[]{:S(2)}, u32[]{:S(2)}) collective-permute-start(f32[16,8,128]{2,1,0:T(8,128)S(1)} %get-tuple-element.91.own), channel_id=1, source_target_pairs={{64,0},{128,64},{192,128},{0,192},{65,1},{129,65},{193,129},{1,193... | collective-permute-start | bytes 196616 | tf_op jit(solution)/shard_map/ppermute | solution.py:638
  63.2 5.4 %collective-permute-start.19 = (f32[8,8,128]{2,1,0:T(8,128)S(1)}, f32[8,8,128]{2,1,0:T(8,128)S(1)}, u32[]{:S(2)}, u32[]{:S(2)}) collective-permute-start(f32[8,8,128]{2,1,0:T(8,128)S(1)} %slice.6), channel_id=1, source_target_pairs={{128,0},{192,64},{0,128},{64,192},{129,1},{193,65},{1,129},{65,193... | collective-permute-start | bytes 98312 | tf_op jit(solution)/shard_map/ppermute | solution.py:638
  68.6 6.1 %collective-permute-start.22 = (f32[50,8,128]{2,1,0:T(8,128)S(1)}, f32[50,8,128]{2,1,0:T(8,128)S(1)}, u32[]{:S(2)}, u32[]{:S(2)}) collective-permute-start(f32[50,8,128]{2,1,0:T(8,128)S(1)} %get-tuple-element.92.r2x), channel_id=1, source_target_pairs={{8,0},{16,8},{24,16},{32,24},{40,32},{48,40},{56,48},{0,56},{9,1},... | collective-permute-start | bytes 614408 | tf_op jit(solution)/shard_map/ppermute | solution.py:638
  68.6 6.8 %collective-permute-start.21 = (f32[50,8,128]{2,1,0:T(8,128)S(1)}, f32[50,8,128]{2,1,0:T(8,128)S(1)}, u32[]{:S(2)}, u32[]{:S(2)}) collective-permute-start(f32[50,8,128]{2,1,0:T(8,128)S(1)} %get-tuple-element.92.r2x), channel_id=1, source_target_pairs={{56,0},{0,8},{8,16},{16,24},{24,32},{32,40},{40,48},{48,56},{57,1}... | collective-permute-start | bytes 614408 | tf_op jit(solution)/shard_map/ppermute | solution.py:638
  69.1 5.6 %collective-permute-start.23 = (f32[18,3,128]{2,1,0:T(4,128)S(1)}, f32[18,3,128]{2,1,0:T(4,128)S(1)}, u32[]{:S(2)}, u32[]{:S(2)}) collective-permute-start(f32[18,3,128]{2,1,0:T(4,128)S(1)} %get-tuple-element.93), channel_id=1, source_target_pairs={{48,0},{56,8},{0,16},{8,24},{16,32},{24,40},{32,48},{40,56},{49,1}... | collective-permute-start | bytes 82952 | tf_op jit(solution)/shard_map/ppermute | solution.py:638
  69.1 5.6 %collective-permute-start.24 = (f32[18,3,128]{2,1,0:T(4,128)S(1)}, f32[18,3,128]{2,1,0:T(4,128)S(1)}, u32[]{:S(2)}, u32[]{:S(2)}) collective-permute-start(f32[18,3,128]{2,1,0:T(4,128)S(1)} %get-tuple-element.94), channel_id=1, source_target_pairs={{16,0},{24,8},{32,16},{40,24},{48,32},{56,40},{0,48},{8,56},{17,1}... | collective-permute-start | bytes 82952 | tf_op jit(solution)/shard_map/ppermute | solution.py:638
  82.6 3.5 %collective-permute-start.26 = (f32[1,128]{1,0:T(1,128)S(1)}, f32[1,128]{1,0:T(1,128)S(1)}, u32[]{:S(2)}, u32[]{:S(2)}) collective-permute-start(f32[1,128]{1,0:T(1,128)S(1)} %add.27), channel_id=1, source_target_pairs={{64,0},{0,64},{192,128},{128,192},{65,1},{1,65},{193,129},{129,193... | collective-permute-start | bytes 1544 | tf_op jit(solution)/shard_map/ppermute | solution.py:642
  86.2 4.8 %collective-permute-start.27 = (f32[1,128]{1,0:T(1,128)S(1)}, f32[1,128]{1,0:T(1,128)S(1)}, u32[]{:S(2)}, u32[]{:S(2)}) collective-permute-start(f32[1,128]{1,0:T(1,128)S(1)} %add.28), channel_id=1, source_target_pairs={{192,0},{128,64},{64,128},{0,192},{193,1},{129,65},{65,129},{1,193... | collective-permute-start | bytes 1544 | tf_op jit(solution)/shard_map/ppermute | solution.py:642
  90.9 3.5 %collective-permute-start.28 = (f32[1,128]{1,0:T(1,128)S(1)}, f32[1,128]{1,0:T(1,128)S(1)}, u32[]{:S(2)}, u32[]{:S(2)}) collective-permute-start(f32[1,128]{1,0:T(1,128)S(1)} %add.29), channel_id=1, source_target_pairs={{16,0},{24,8},{0,16},{8,24},{48,32},{56,40},{32,48},{40,56},{17,1}... | collective-permute-start | bytes 1544 | tf_op jit(solution)/shard_map/ppermute | solution.py:642
  94.5 4.8 %collective-permute-start.29 = (f32[1,128]{1,0:T(1,128)S(1)}, f32[1,128]{1,0:T(1,128)S(1)}, u32[]{:S(2)}, u32[]{:S(2)}) collective-permute-start(f32[1,128]{1,0:T(1,128)S(1)} %add.30), channel_id=1, source_target_pairs={{48,0},{56,8},{32,16},{40,24},{16,32},{24,40},{0,48},{8,56},{49,1}... | collective-permute-start | bytes 1544 | tf_op jit(solution)/shard_map/ppermute | solution.py:642
  99.2 4.7 %collective-permute-start.32 = (f32[1,128]{1,0:T(1,128)S(1)}, f32[1,128]{1,0:T(1,128)S(1)}, u32[]{:S(2)}, u32[]{:S(2)}) collective-permute-start(f32[1,128]{1,0:T(1,128)S(1)} %add.31), channel_id=1, source_target_pairs={{3,0},{2,1},{1,2},{0,3},{7,4},{6,5},{5,6},{4,7},{11,8},{10,9},{9,1... | collective-permute-start | bytes 1544 | tf_op jit(solution)/shard_map/ppermute | solution.py:642
  100.7 4.7 %collective-permute-start.31 = (f32[1,128]{1,0:T(1,128)S(1)}, f32[1,128]{1,0:T(1,128)S(1)}, u32[]{:S(2)}, u32[]{:S(2)}) collective-permute-start(f32[1,128]{1,0:T(1,128)S(1)} %add.31), channel_id=1, source_target_pairs={{2,0},{3,1},{0,2},{1,3},{6,4},{7,5},{4,6},{5,7},{10,8},{11,9},{8,1... | collective-permute-start | bytes 1544 | tf_op jit(solution)/shard_map/ppermute | solution.py:642
  107.4 6.5 %collective-permute-start.33 = (f32[1,128]{1,0:T(1,128)S(1)}, f32[1,128]{1,0:T(1,128)S(1)}, u32[]{:S(2)}, u32[]{:S(2)}) collective-permute-start(f32[1,128]{1,0:T(1,128)S(1)} %add_add_fusion), channel_id=1, source_target_pairs={{7,0},{6,1},{5,2},{4,3},{3,4},{2,5},{1,6},{0,7},{15,8},{14,9},{13,... | collective-permute-start | bytes 1544 | tf_op jit(solution)/shard_map/ppermute | solution.py:642
  (3 other events, 43.3 us)

commit v5 on v4

--- a/solution.py
+++ b/solution.py
@@ -127,10 +127,11 @@
     return [(a, mid), (mid, b)]
 
 
-def relax(src, dst, a, b, matrix, right, side):
+def relax(src, dst, a, b, matrix, right, side, line=None):
     for p, q in chunks(a, b):
         mid, near = around(src, p, q)
-        dst[p:q] = times(mid, matrix) + right(p, q) + side[p:q] * near
+        value = times(mid, matrix) + right(p, q) + side[p:q] * near
+        dst[p:q] = value if line is None else value + mid * line
 
 
 def pack_lanes(planes, height, width, count, to_left, to_right):
@@ -224,6 +225,8 @@
         return out
 
     kept = None
+    for ref in (low, high):
+        ref[60] = jnp.zeros((4, 128), F32)
     for p in range(40):
         if p < H0:
             a, b = ends(xlo, p)
@@ -265,10 +268,13 @@
     lane = rows((8, 128), 1)
     laid = jnp.concatenate([own[...], jnp.where(lane < 64, right[288:296], left[288:296])], axis=1)
     band, op, step, factor = operators(laid, place_0, iz, 0, 36, S0)
-    b0[...] = thrice(jnp.transpose(band))
-    k0[...] = thrice(step)
-    m0[...] = thrice(op)
-    f0[...] = jnp.broadcast_to(factor, (8, 256))
+    eye = jnp.where(rows((256, 256), 0) == rows((256, 256), 1), 1.0, 0.0)
+    lines = [factor]
+    for out, matrix in ((k0, step), (m0, op), (b0, jnp.transpose(band))):
+        own_part = matrix * eye
+        out[...] = thrice(matrix - own_part)
+        lines.append(jnp.sum(own_part, axis=0, keepdims=True))
+    f0[...] = jnp.concatenate(lines + [jnp.zeros((4, 256), F32)], axis=0)
     fold[...] = restrict_matrix(place_0, 256, lambda q: q, 128, iz, 0, 36)
     grow[...] = prolong_matrix(place_1, 128, place_0, 256, iz, 0, 36)
     y = iy * 32 + rows((40, 256), 0) - H0
@@ -346,18 +352,18 @@
             moved = pltpu.roll(edge[40 + p // 2], 100 if p % 2 == 0 else 36, 1)
             d[p, part, :128] = edge[p] * (ok * good)
             d[p, part, 128:] = jnp.where((lane < 28) | (lane >= 100), moved, 0.0) * (ok * good)
-    factor = f0[0:1, :].reshape(1, 1, 256)
+    factor, step_line, op_line, band_line = (f0[i : i + 1, :].reshape(1, 1, 256) for i in range(4))
     for p, q in chunks(0, 40):
-        r = times(d[p:q], b0[...])
+        r = times(d[p:q], b0[...]) + d[p:q] * band_line
         r_out[p:q] = r
         e0[p:q] = r * factor
-    relax(e0, e_out, 1, 39, k0[...], lambda p, q: e0[p:q], side)
+    relax(e0, e_out, 1, 39, k0[...], lambda p, q: e0[p:q], side, step_line)
     e_out[0] = jnp.zeros((40, 256), F32)
     e_out[39] = jnp.zeros((40, 256), F32)
     total = jnp.zeros((40, 128), F32)
     for p, q in chunks(3, 37):
         mid, near = around(e_out, p, q)
-        value = r_out[p:q] - times(mid, m0[...]) + S0 * near
+        value = (r_out[p:q] - mid * op_line) - times(mid, m0[...]) + S0 * near
         x = ix * 32 + rows(value.shape, 0) + (p - H0)
         y = iy * 32 + rows(value.shape, 1) - H0
         value = jnp.where((x >= 0) & (x < NX) & (y >= 0) & (y < NY), value, 0.0)
@@ -460,6 +466,8 @@
     near[30:36] = x3[10:]
     near[36:44] = own[8:]
     near[44:50] = x1[8:14]
+    for ref in (low, high):
+        ref[18] = jnp.zeros((3, 128), F32)
     for i in range(18):
         value = near[i + 6]
         low[i] = value[:3]
@@ -546,7 +554,7 @@
     relax(e3, c3, 1, 11, k3[...], lambda p, q: e3[p:q], side3)
     cz = times_exact(c3[...], grow2[...])
     below, above = pltpu.roll(cz, 1, 1), pltpu.roll(cz, 15, 1)
-    cy2[...] = jnp.zeros((12, 32, 128), F32)
+    cy2[...] = jnp.zeros((12, 40, 128), F32)
     cy2[:, pl.ds(3, 12, stride=2), :] = (0.75 * cz + 0.25 * below)[:, :12]
     cy2[:, pl.ds(4, 12, stride=2), :] = (0.75 * cz + 0.25 * above)[:, :12]
     fr2 = f2[0:1, :128].reshape(1, 1, 128)
@@ -557,7 +565,7 @@
         xr = ix * 8 + f
         y = iy * 8 + yrow - H2
         ok = jnp.where((y >= 0) & (y < NY // 4), jnp.where((xr >= 0) & (xr < NX // 4), 1.0, 0.0), 0.0)
-        ea[xf, :, :128] = eb[xf, :, :128] + ok * (0.75 * cy2[j] + 0.25 * cy2[other])
+        ea[xf, :, :128] = eb[xf, :, :128] + ok * (0.75 * cy2[j, :32] + 0.25 * cy2[other, :32])
 
     def relax_2(src, dst, a, b):
         for p, q in chunks(a, b):
@@ -572,7 +580,7 @@
     for p in range(14):
         r3[p] = ea[8 + p, :, :128]
     r3[...] = times_exact(r3[...], grow1[...])
-    cy1[...] = jnp.zeros((14, 32, 128), F32)
+    cy1[...] = jnp.zeros((14, 40, 128), F32)
     cy1[:, pl.ds(1, 12, stride=2), :] = 0.75 * r3[:, 9:21, :] + 0.25 * r3[:, 8:20, :]
     cy1[:, pl.ds(2, 12, stride=2), :] = 0.75 * r3[:, 9:21, :] + 0.25 * r3[:, 10:22, :]
     fr1 = f1[0:1, :128].reshape(1, 1, 128)
@@ -583,7 +591,7 @@
         ok = jnp.where((y >= 0) & (y < NY // 2), jnp.where((xr >= 0) & (xr < NX // 2), 1.0, 0.0), 0.0)
         j = f // 2 + 3
         other = j - 1 if f % 2 == 0 else j + 1
-        ua[xf] = e1s[xf] + ok * (0.75 * cy1[j] + 0.25 * cy1[other])
+        ua[xf] = e1s[xf] + ok * (0.75 * cy1[j, :32] + 0.25 * cy1[other, :32])
     relax(ua, ub, 2, 24, k1[...], lambda p, q: fr1 * r1s[p:q], side1)
     relax(ub, ua, 3, 23, k1[...], lambda p, q: fr1 * r1s[p:q], side1)
     for p, q in chunks(0, 20):
@@ -592,7 +600,7 @@
             part = cz[:, :, 128 * t : 128 * t + 128]
             cy0[p:q, t, pl.ds(0, 20, stride=2), :] = 0.75 * part[:, 3:23] + 0.25 * part[:, 2:22]
             cy0[p:q, t, pl.ds(1, 20, stride=2), :] = 0.75 * part[:, 3:23] + 0.25 * part[:, 4:24]
-    fr0 = f0[0:1, :].reshape(1, 1, 256)
+    fr0, step_line, op_line = (f0[i : i + 1, :].reshape(1, 1, 256) for i in range(3))
     for xf in range(1, 39):
         f = xf - H0
         xr = ix * 32 + f
@@ -602,9 +610,9 @@
             part = slice(128 * t, 128 * t + 128)
             j = f // 2 + 2
             other = j - 1 if f % 2 == 0 else j + 1
-            va[xf, :, part] = e0s[xf, :, part] + ok * (0.75 * cy0[j, t] + 0.25 * cy0[other, t])
-    relax(va, vb, 2, 38, k0[...], lambda p, q: fr0 * r0s[p:q], side0)
-    relax(vb, va, 3, 37, k0[...], lambda p, q: fr0 * r0s[p:q], side0)
+            va[xf, :, part] = e0s[xf, :, part] + ok * (0.75 * cy0[j, t, :40] + 0.25 * cy0[other, t, :40])
+    relax(va, vb, 2, 38, k0[...], lambda p, q: fr0 * r0s[p:q], side0, step_line)
+    relax(vb, va, 3, 37, k0[...], lambda p, q: fr0 * r0s[p:q], side0, step_line)
     total = jnp.zeros((32, 128), F32)
     last = m0[:, :128]
     for p, q in chunks(4, 36):
@@ -613,15 +621,15 @@
         near = (va[p + 1 : q + 1, :, :128] + va[p - 1 : q - 1, :, :128]) + (
             pltpu.roll(flat, 1, 1) + pltpu.roll(flat, 39, 1)
         )
-        value = (r0s[p:q, :, :128] - times(mid, last) + S0 * near)[:, 4:36]
+        value = ((r0s[p:q, :, :128] - flat * op_line[:, :, :128]) - times(mid, last) + S0 * near)[:, 4:36]
         part = slice(p - 4, q - 4)
         res[part] = value
         sol[part] = va[p:q, 4:36, :128]
         total = total + jnp.sum(value * value, axis=0)
     sum3 = jnp.sum(total)
-    tile = rows((1, 128), 1)
+    tile = rows((8, 128), 1)
     stat[...] = jnp.where(
-        tile == 0, stat0[0:1], jnp.where(tile == 1, stat1[0:1], jnp.where(tile == 2, sum2, jnp.where(tile == 3, sum3, 0.0)))
+        tile == 0, stat0[...], jnp.where(tile == 1, stat1[...], jnp.where(tile == 2, sum2, jnp.where(tile == 3, sum3, 0.0)))
     )
 
 
@@ -684,7 +692,7 @@
         spread_0_kernel, [f32(32, 32, 128), f32(5, 32, 128), f32(5, 32, 128)], [], "spread_0"
     )(own, from_right, from_left)
     xlo, xhi = shift(last, "gx", -1), shift(first, "gx", 1)
-    low, high = call(edges_0_kernel, [f32(60, 4, 128), f32(60, 4, 128)], [], "edges_0")(own, tail, xlo, xhi)
+    low, high = call(edges_0_kernel, [f32(62, 4, 128), f32(62, 4, 128)], [], "edges_0")(own, tail, xlo, xhi)
     ylo, yhi = shift(high, "gy", -1), shift(low, "gy", 1)
     (field,) = call(gather_0_kernel, [f32(40, 40, 256)], [], "gather_0")(own, tail, xlo, xhi)
     b0, k0, m0, f0, r00, p00, side0 = call(
@@ -737,7 +745,7 @@
         [], "weights_coarse",
     )(wide2)
     x1, x2, x3 = shift(r2z, "gx", 1), shift(r2z[:8], "gx", 2), shift(r2z, "gx", 3)
-    r2x, low, high = call(edges_2_kernel, [f32(50, 8, 128), f32(18, 3, 128), f32(18, 3, 128)], [], "edges_2")(
+    r2x, low, high = call(edges_2_kernel, [f32(50, 8, 128), f32(20, 3, 128), f32(20, 3, 128)], [], "edges_2")(
         r2z, x1, x2, x3
     )
     ya, yb = shift(r2x, "gy", -1), shift(r2x, "gy", 1)
@@ -745,12 +753,12 @@
     lev2 = (30, 32, 256)
     sol, res, stat = call(
         up_kernel,
-        [f32(32, 32, 128), f32(32, 32, 128), f32(1, 128)],
+        [f32(32, 32, 128), f32(32, 32, 128), f32(8, 128)],
         [
             scratch(*lev2), scratch(*lev2), scratch(*lev2), scratch(12, 2, 40, 128),
             scratch(14, 32, 128), scratch(12, 16, 128), scratch(12, 16, 128), scratch(12, 16, 128),
-            scratch(12, 32, 128), scratch(*mid), scratch(*mid), scratch(14, 32, 128),
-            scratch(*big), scratch(*big), scratch(20, 2, 40, 128),
+            scratch(12, 40, 128), scratch(*mid), scratch(*mid), scratch(14, 40, 128),
+            scratch(*big), scratch(*big), scratch(20, 2, 48, 128),
         ],
         "up", 24,
     )(
@@ -761,7 +769,7 @@
         store_kernel, [f32(32, 32, 128), f32(32, 32, 128)], [pltpu.SemaphoreType.DMA((2,))], "store", 4, (0, 1)
     )(sol, res)
     t = stat
-    for axis, flips in (("gy", (1,)), ("gx", (1,)), ("gx", (3,)), ("gy", (2,)), ("gy", (6,)), ("gz", (1, 2, 3)), ("gz", (7,))):
+    for axis, flips in (("gy", (1,)), ("gx", (1, 2, 3)), ("gy", (2, 4, 6)), ("gz", (1, 2, 3)), ("gz", (7,))):
         others = [swap(t, axis, f) for f in flips]
         t = t + others[0]
         if len(others) > 1:

time: 115 us -> 113 us (0.983)
  waiting for transfers between devices: 46.1 us -> 39.3 us
  starting transfers between devices: 49.9 us -> 54.5 us
    ppermute x9 -> x11, waiting for transfers between devices: 19.1 us -> 12.3 us  [swap(): lax.ppermute(x, axis, [(i ^ flip, i) for i in range(lax.axis_size(axis))])]
    ppermute x9 -> x11, starting transfers between devices: 12.5 us -> 17 us  [swap(): lax.ppermute(x, axis, [(i ^ flip, i) for i in range(lax.axis_size(axis))])]
  transfers between devices with their start and end apart: 34 -> 36, of which waited for: 23 -> 23; matrix products, arithmetic and copies ran while one was open for 0% -> 0% of each run, Pallas kernels for 4% -> 4%
where the time goes in v5:
time: 113 us
  starting transfers between devices  54.5 us (48%)
  waiting for transfers between devices  39.3 us (35%)
  Pallas kernels  17.6 us (16%)
    ppermute x25, starting transfers between devices, shift(): return lax.ppermute(x, axis, [((i + k) % n, i) for i in range(n)])  37.5 us
    ppermute x25, waiting for transfers between devices, shift(): return lax.ppermute(x, axis, [((i + k) % n, i) for i in range(n)])  27 us
    pallas_call x15, Pallas kernels, run(): pl.pallas_call(kernel, out_shape=[jax.ShapeDtypeStruct(o.shape, F32) if i...  17.6 us
    ppermute x11, starting transfers between devices, swap(): lax.ppermute(x, axis, [(i ^ flip, i) for i in range(lax.axis_size(axis))])  17 us
    ppermute x11, waiting for transfers between devices, swap(): lax.ppermute(x, axis, [(i ^ flip, i) for i in range(lax.axis_size(axis))])  12.3 us
  transfers between devices with their start and end apart: 36, of which 23 were waited for; matrix products, arithmetic and copies ran while one was open for 0% of the time, Pallas kernels for 4%

profile of v5, /device:TPU:32, one launch (start us, length us, event | category | flops | bytes accessed | tf_op | source)
XLA Modules:
  0.0 112.8 jit_solution(321713601568737806)
XLA Ops:
  0.6 1.7 %prepare.1 = (f32[32,32,128]{2,1,0:T(8,128)S(1)}, f32[8,128]{1,0:T(8,128)S(1)}, f32[296,128]{1,0:T(8,128)S(1)}, f32[296,128]{1,0:T(8,128)S(1)}) custom-call(f32[32,32,128]{2,1,0:T(8,128)} %data.1, f32[8,128]{1,0:T(8,128)} %weights.1), custom_call_target="tpu_custom_call" | custom-call | tf_op jit(solution)/shard_map/prepare/pallas_call | solution.py:671
  2.3 1.9 %collective-permute-start = (f32[296,128]{1,0:T(8,128)S(1)}, f32[296,128]{1,0:T(8,128)S(1)}, u32[]{:S(2)}, u32[]{:S(2)}) collective-permute-start(f32[296,128]{1,0:T(8,128)S(1)} %get-tuple-element.62), channel_id=1, source_target_pairs={{1,0},{2,1},{3,2},{4,3},{5,4},{6,5},{7,6},{0,7},{9,8},{10,9},{11,1... | collective-permute-start | bytes 454664 | tf_op jit(solution)/shard_map/ppermute | solution.py:646
  4.4 3.8 %collective-permute-done.from_right.right = f32[296,128]{1,0:T(8,128)S(1)} collective-permute-done((f32[296,128]{1,0:T(8,128)S(1)}, f32[296,128]{1,0:T(8,128)S(1)}, u32[]{:S(2)}, u32[]{:S(2)}) %collective-permute-start) | collective-permute-done | bytes 151584 | tf_op jit(solution)/shard_map/ppermute | solution.py:646
  8.2 3.8 %collective-permute-done.1.from_left.left = f32[296,128]{1,0:T(8,128)S(1)} collective-permute-done((f32[296,128]{1,0:T(8,128)S(1)}, f32[296,128]{1,0:T(8,128)S(1)}, u32[]{:S(2)}, u32[]{:S(2)}) %collective-permute-start.1) | collective-permute-done | bytes 151584 | tf_op jit(solution)/shard_map/ppermute | solution.py:646
  14.3 1.7 %collective-permute-start.3 = (f32[5,32,128]{2,1,0:T(8,128)S(1)}, f32[5,32,128]{2,1,0:T(8,128)S(1)}, u32[]{:S(2)}, u32[]{:S(2)}) collective-permute-start(f32[5,32,128]{2,1,0:T(8,128)S(1)} %get-tuple-element.66), channel_id=1, source_target_pairs={{64,0},{128,64},{192,128},{0,192},{65,1},{129,65},{193,129},{1,193... | collective-permute-start | bytes 245768 | tf_op jit(solution)/shard_map/ppermute | solution.py:646
  15.9 2.4 %collective-permute-done.2.xlo = f32[5,32,128]{2,1,0:T(8,128)S(1)} collective-permute-done((f32[5,32,128]{2,1,0:T(8,128)S(1)}, f32[5,32,128]{2,1,0:T(8,128)S(1)}, u32[]{:S(2)}, u32[]{:S(2)}) %collective-permute-start.2) | collective-permute-done | bytes 81952 | tf_op jit(solution)/shard_map/ppermute | solution.py:646
  18.9 2.9 %collective-permute-start.5 = (f32[62,4,128]{2,1,0:T(4,128)S(1)}, f32[62,4,128]{2,1,0:T(4,128)S(1)}, u32[]{:S(2)}, u32[]{:S(2)}) collective-permute-start(f32[62,4,128]{2,1,0:T(4,128)S(1)} %get-tuple-element.68), channel_id=1, source_target_pairs={{8,0},{16,8},{24,16},{32,24},{40,32},{48,40},{56,48},{0,56},{9,1},... | collective-permute-start | bytes 380936 | tf_op jit(solution)/shard_map/ppermute | solution.py:646
  24.5 3.5 %down_0.1 = (f32[16,16,128]{2,1,0:T(8,128)S(1)}, f32[6,16,128]{2,1,0:T(8,128)S(1)}, f32[6,16,128]{2,1,0:T(8,128)S(1)}, f32[40,40,256]{2,1,0:T(8,128)S(1)}, f32[4...) custom-call(f32[40,40,256]{2,1,0:T(8,128)S(1)} %gather_0.1.field, f32[62,4,128]{2,1,0:T(4,128)S(1)} %collective-permute-done.4.ylo, ...), custom_call_target="tpu_custom_call" | custom-call | tf_op jit(solution)/shard_map/down_0/pallas_call | solution.py:671
  28.0 3.1 %collective-permute-start.6 = (f32[6,16,128]{2,1,0:T(8,128)S(1)}, f32[6,16,128]{2,1,0:T(8,128)S(1)}, u32[]{:S(2)}, u32[]{:S(2)}) collective-permute-start(f32[6,16,128]{2,1,0:T(8,128)S(1)} %get-tuple-element.77), channel_id=1, source_target_pairs={{1,0},{2,1},{3,2},{4,3},{5,4},{6,5},{7,6},{0,7},{9,8},{10,9},{11,1... | collective-permute-start | bytes 147464 | tf_op jit(solution)/shard_map/ppermute | solution.py:646
  31.1 1.7 %collective-permute-done.6.from_right = f32[6,16,128]{2,1,0:T(8,128)S(1)} collective-permute-done((f32[6,16,128]{2,1,0:T(8,128)S(1)}, f32[6,16,128]{2,1,0:T(8,128)S(1)}, u32[]{:S(2)}, u32[]{:S(2)}) %collective-permute-start.6) | collective-permute-done | bytes 49184 | tf_op jit(solution)/shard_map/ppermute | solution.py:646
  32.9 2.3 %collective-permute-done.7.from_left = f32[6,16,128]{2,1,0:T(8,128)S(1)} collective-permute-done((f32[6,16,128]{2,1,0:T(8,128)S(1)}, f32[6,16,128]{2,1,0:T(8,128)S(1)}, u32[]{:S(2)}, u32[]{:S(2)}) %collective-permute-start.7) | collective-permute-done | bytes 49184 | tf_op jit(solution)/shard_map/ppermute | solution.py:646
  35.3 1.7 %collective-permute-start.8 = (f32[6,16,128]{2,1,0:T(8,128)S(1)}, f32[6,16,128]{2,1,0:T(8,128)S(1)}, u32[]{:S(2)}, u32[]{:S(2)}) collective-permute-start(f32[6,16,128]{2,1,0:T(8,128)S(1)} %get-tuple-element.81), channel_id=1, source_target_pairs={{192,0},{0,64},{64,128},{128,192},{193,1},{1,65},{65,129},{129,193... | collective-permute-start | bytes 147464 | tf_op jit(solution)/shard_map/ppermute | solution.py:646
  37.0 1.7 %collective-permute-start.9 = (f32[6,16,128]{2,1,0:T(8,128)S(1)}, f32[6,16,128]{2,1,0:T(8,128)S(1)}, u32[]{:S(2)}, u32[]{:S(2)}) collective-permute-start(f32[6,16,128]{2,1,0:T(8,128)S(1)} %get-tuple-element.82), channel_id=1, source_target_pairs={{64,0},{128,64},{192,128},{0,192},{65,1},{129,65},{193,129},{1,193... | collective-permute-start | bytes 147464 | tf_op jit(solution)/shard_map/ppermute | solution.py:646
  38.6 2.1 %collective-permute-done.8.xlo = f32[6,16,128]{2,1,0:T(8,128)S(1)} collective-permute-done((f32[6,16,128]{2,1,0:T(8,128)S(1)}, f32[6,16,128]{2,1,0:T(8,128)S(1)}, u32[]{:S(2)}, u32[]{:S(2)}) %collective-permute-start.8) | collective-permute-done | bytes 49184 | tf_op jit(solution)/shard_map/ppermute | solution.py:646
  41.1 2.9 %collective-permute-start.11 = (f32[26,8,128]{2,1,0:T(8,128)S(1)}, f32[26,8,128]{2,1,0:T(8,128)S(1)}, u32[]{:S(2)}, u32[]{:S(2)}) collective-permute-start(f32[26,8,128]{2,1,0:T(8,128)S(1)} %get-tuple-element.84), channel_id=1, source_target_pairs={{8,0},{16,8},{24,16},{32,24},{40,32},{48,40},{56,48},{0,56},{9,1},... | collective-permute-start | bytes 319496 | tf_op jit(solution)/shard_map/ppermute | solution.py:646
  47.4 2.2 %collective-permute-start.16 = (f32[3,8,128]{2,1,0:T(8,128)S(1)}, f32[3,8,128]{2,1,0:T(8,128)S(1)}, u32[]{:S(2)}, u32[]{:S(2)}) collective-permute-start(f32[3,8,128]{2,1,0:T(8,128)S(1)} %get-tuple-element.90.own), channel_id=1, source_target_pairs={{6,0},{7,1},{0,2},{1,3},{2,4},{3,5},{4,6},{5,7},{14,8},{15,9},{8,1... | collective-permute-start | bytes 36872 | tf_op jit(solution)/shard_map/ppermute | solution.py:646
  51.3 3.4 %collective-permute-start.14 = (f32[3,8,128]{2,1,0:T(8,128)S(1)}, f32[3,8,128]{2,1,0:T(8,128)S(1)}, u32[]{:S(2)}, u32[]{:S(2)}) collective-permute-start(f32[3,8,128]{2,1,0:T(8,128)S(1)} %get-tuple-element.90.own), channel_id=1, source_target_pairs={{3,0},{4,1},{5,2},{6,3},{7,4},{0,5},{1,6},{2,7},{11,8},{12,9},{13,... | collective-permute-start | bytes 36872 | tf_op jit(solution)/shard_map/ppermute | solution.py:646
  55.5 3.1 %collective-permute-start.12 = (f32[3,8,128]{2,1,0:T(8,128)S(1)}, f32[3,8,128]{2,1,0:T(8,128)S(1)}, u32[]{:S(2)}, u32[]{:S(2)}) collective-permute-start(f32[3,8,128]{2,1,0:T(8,128)S(1)} %get-tuple-element.90.own), channel_id=1, source_target_pairs={{1,0},{2,1},{3,2},{4,3},{5,4},{6,5},{7,6},{0,7},{9,8},{10,9},{11,1... | collective-permute-start | bytes 36872 | tf_op jit(solution)/shard_map/ppermute | solution.py:646
  61.5 2.0 %collective-permute-start.18 = (f32[16,8,128]{2,1,0:T(8,128)S(1)}, f32[16,8,128]{2,1,0:T(8,128)S(1)}, u32[]{:S(2)}, u32[]{:S(2)}) collective-permute-start(f32[16,8,128]{2,1,0:T(8,128)S(1)} %get-tuple-element.91.own), channel_id=1, source_target_pairs={{64,0},{128,64},{192,128},{0,192},{65,1},{129,65},{193,129},{1,193... | collective-permute-start | bytes 196616 | tf_op jit(solution)/shard_map/ppermute | solution.py:646
  65.0 3.9 %collective-permute-done.19.x2 = f32[8,8,128]{2,1,0:T(8,128)S(1)} collective-permute-done((f32[8,8,128]{2,1,0:T(8,128)S(1)}, f32[8,8,128]{2,1,0:T(8,128)S(1)}, u32[]{:S(2)}, u32[]{:S(2)}) %collective-permute-start.19) | collective-permute-done | bytes 32800 | tf_op jit(solution)/shard_map/ppermute | solution.py:646
  69.5 3.2 %collective-permute-start.24 = (f32[20,3,128]{2,1,0:T(4,128)S(1)}, f32[20,3,128]{2,1,0:T(4,128)S(1)}, u32[]{:S(2)}, u32[]{:S(2)}) collective-permute-start(f32[20,3,128]{2,1,0:T(4,128)S(1)} %get-tuple-element.94), channel_id=1, source_target_pairs={{16,0},{24,8},{32,16},{40,24},{48,32},{56,40},{0,48},{8,56},{17,1}... | collective-permute-start | bytes 92168 | tf_op jit(solution)/shard_map/ppermute | solution.py:646
  75.8 6.1 %up.1 = (f32[32,32,128]{2,1,0:T(8,128)S(1)}, f32[32,32,128]{2,1,0:T(8,128)S(1)}, f32[8,128]{1,0:T(8,128)S(1)}) custom-call(f32[50,8,128]{2,1,0:T(8,128)S(1)} %get-tuple-element.92.r2x, f32[50,8,128]{2,1,0:T(8,128)S(1)} %collective-permute-done.21.ya, f32[50,8,128]{2,1,0:T(8,128)S(1)} %collective-permute-done.22.yb, ...), custom_call_target="tpu_custom_call" | custom-call | tf_op jit(solution)/shard_map/up/pallas_call | solution.py:671
  83.1 1.7 %collective-permute-start.28 = (f32[8,128]{1,0:T(8,128)S(1)}, f32[8,128]{1,0:T(8,128)S(1)}, u32[]{:S(2)}, u32[]{:S(2)}) collective-permute-start(f32[8,128]{1,0:T(8,128)S(1)} %add.33), channel_id=1, source_target_pairs={{192,0},{128,64},{64,128},{0,192},{193,1},{129,65},{65,129},{1,193... | collective-permute-start | bytes 12296 | tf_op jit(solution)/shard_map/ppermute | solution.py:650
  85.3 2.0 %collective-permute-start.26 = (f32[8,128]{1,0:T(8,128)S(1)}, f32[8,128]{1,0:T(8,128)S(1)}, u32[]{:S(2)}, u32[]{:S(2)}) collective-permute-start(f32[8,128]{1,0:T(8,128)S(1)} %add.33), channel_id=1, source_target_pairs={{64,0},{0,64},{192,128},{128,192},{65,1},{1,65},{193,129},{129,193... | collective-permute-start | bytes 12296 | tf_op jit(solution)/shard_map/ppermute | solution.py:650
  88.0 2.0 %collective-permute-done.27 = f32[8,128]{1,0:T(8,128)S(1)} collective-permute-done((f32[8,128]{1,0:T(8,128)S(1)}, f32[8,128]{1,0:T(8,128)S(1)}, u32[]{:S(2)}, u32[]{:S(2)}) %collective-permute-start.27) | collective-permute-done | bytes 4128 | tf_op jit(solution)/shard_map/ppermute | solution.py:650
  89.9 2.2 %collective-permute-start.31 = (f32[8,128]{1,0:T(8,128)S(1)}, f32[8,128]{1,0:T(8,128)S(1)}, u32[]{:S(2)}, u32[]{:S(2)}) collective-permute-start(f32[8,128]{1,0:T(8,128)S(1)} %add_add_fusion.2), channel_id=1, source_target_pairs={{48,0},{56,8},{32,16},{40,24},{16,32},{24,40},{0,48},{8,56},{49,1}... | collective-permute-start | bytes 12296 | tf_op jit(solution)/shard_map/ppermute | solution.py:650
  92.2 2.0 %collective-permute-start.29 = (f32[8,128]{1,0:T(8,128)S(1)}, f32[8,128]{1,0:T(8,128)S(1)}, u32[]{:S(2)}, u32[]{:S(2)}) collective-permute-start(f32[8,128]{1,0:T(8,128)S(1)} %add_add_fusion.2), channel_id=1, source_target_pairs={{16,0},{24,8},{0,16},{8,24},{48,32},{56,40},{32,48},{40,56},{17,1}... | collective-permute-start | bytes 12296 | tf_op jit(solution)/shard_map/ppermute | solution.py:650
  94.8 2.4 %collective-permute-done.30 = f32[8,128]{1,0:T(8,128)S(1)} collective-permute-done((f32[8,128]{1,0:T(8,128)S(1)}, f32[8,128]{1,0:T(8,128)S(1)}, u32[]{:S(2)}, u32[]{:S(2)}) %collective-permute-start.30) | collective-permute-done | bytes 4128 | tf_op jit(solution)/shard_map/ppermute | solution.py:650
  98.8 3.2 %collective-permute-start.33 = (f32[8,128]{1,0:T(8,128)S(1)}, f32[8,128]{1,0:T(8,128)S(1)}, u32[]{:S(2)}, u32[]{:S(2)}) collective-permute-start(f32[8,128]{1,0:T(8,128)S(1)} %add_add_fusion.1), channel_id=1, source_target_pairs={{2,0},{3,1},{0,2},{1,3},{6,4},{7,5},{4,6},{5,7},{10,8},{11,9},{8,1... | collective-permute-start | bytes 12296 | tf_op jit(solution)/shard_map/ppermute | solution.py:650
  103.6 2.0 %collective-permute-done.32 = f32[8,128]{1,0:T(8,128)S(1)} collective-permute-done((f32[8,128]{1,0:T(8,128)S(1)}, f32[8,128]{1,0:T(8,128)S(1)}, u32[]{:S(2)}, u32[]{:S(2)}) %collective-permute-start.32) | collective-permute-done | bytes 4128 | tf_op jit(solution)/shard_map/ppermute | solution.py:650
  105.6 3.6 %collective-permute-start.35 = (f32[8,128]{1,0:T(8,128)S(1)}, f32[8,128]{1,0:T(8,128)S(1)}, u32[]{:S(2)}, u32[]{:S(2)}) collective-permute-start(f32[8,128]{1,0:T(8,128)S(1)} %add_add_fusion), channel_id=1, source_target_pairs={{7,0},{6,1},{5,2},{4,3},{3,4},{2,5},{1,6},{0,7},{15,8},{14,9},{13,... | collective-permute-start | bytes 12296 | tf_op jit(solution)/shard_map/ppermute | solution.py:650
  110.2 2.0 %collective-permute-done.35 = f32[8,128]{1,0:T(8,128)S(1)} collective-permute-done((f32[8,128]{1,0:T(8,128)S(1)}, f32[8,128]{1,0:T(8,128)S(1)}, u32[]{:S(2)}, u32[]{:S(2)}) %collective-permute-start.35) | collective-permute-done | bytes 4128 | tf_op jit(solution)/shard_map/ppermute | solution.py:650
  (64 shorter events, 27.9 us)
Async XLA Ops:
  2.3 5.9 %collective-permute-start = (f32[296,128]{1,0:T(8,128)S(1)}, f32[296,128]{1,0:T(8,128)S(1)}, u32[]{:S(2)}, u32[]{:S(2)}) collective-permute-start(f32[296,128]{1,0:T(8,128)S(1)} %get-tuple-element.62), channel_id=1, source_target_pairs={{1,0},{2,1},{3,2},{4,3},{5,4},{6,5},{7,6},{0,7},{9,8},{10,9},{11,1... | collective-permute-start | bytes 454664 | tf_op jit(solution)/shard_map/ppermute | solution.py:646
  4.2 7.8 %collective-permute-start.1 = (f32[296,128]{1,0:T(8,128)S(1)}, f32[296,128]{1,0:T(8,128)S(1)}, u32[]{:S(2)}, u32[]{:S(2)}) collective-permute-start(f32[296,128]{1,0:T(8,128)S(1)} %get-tuple-element.63), channel_id=1, source_target_pairs={{7,0},{0,1},{1,2},{2,3},{3,4},{4,5},{5,6},{6,7},{15,8},{8,9},{9,10... | collective-permute-start | bytes 454664 | tf_op jit(solution)/shard_map/ppermute | solution.py:646
  12.7 5.7 %collective-permute-start.2 = (f32[5,32,128]{2,1,0:T(8,128)S(1)}, f32[5,32,128]{2,1,0:T(8,128)S(1)}, u32[]{:S(2)}, u32[]{:S(2)}) collective-permute-start(f32[5,32,128]{2,1,0:T(8,128)S(1)} %get-tuple-element.65), channel_id=1, source_target_pairs={{192,0},{0,64},{64,128},{128,192},{193,1},{1,65},{65,129},{129,193... | collective-permute-start | bytes 245768 | tf_op jit(solution)/shard_map/ppermute | solution.py:646
  14.3 4.4 %collective-permute-start.3 = (f32[5,32,128]{2,1,0:T(8,128)S(1)}, f32[5,32,128]{2,1,0:T(8,128)S(1)}, u32[]{:S(2)}, u32[]{:S(2)}) collective-permute-start(f32[5,32,128]{2,1,0:T(8,128)S(1)} %get-tuple-element.66), channel_id=1, source_target_pairs={{64,0},{128,64},{192,128},{0,192},{65,1},{129,65},{193,129},{1,193... | collective-permute-start | bytes 245768 | tf_op jit(solution)/shard_map/ppermute | solution.py:646
  18.9 5.6 %collective-permute-start.4 = (f32[62,4,128]{2,1,0:T(4,128)S(1)}, f32[62,4,128]{2,1,0:T(4,128)S(1)}, u32[]{:S(2)}, u32[]{:S(2)}) collective-permute-start(f32[62,4,128]{2,1,0:T(4,128)S(1)} %get-tuple-element.67), channel_id=1, source_target_pairs={{56,0},{0,8},{8,16},{16,24},{24,32},{32,40},{40,48},{48,56},{57,1}... | collective-permute-start | bytes 380936 | tf_op jit(solution)/shard_map/ppermute | solution.py:646
  18.9 5.5 %collective-permute-start.5 = (f32[62,4,128]{2,1,0:T(4,128)S(1)}, f32[62,4,128]{2,1,0:T(4,128)S(1)}, u32[]{:S(2)}, u32[]{:S(2)}) collective-permute-start(f32[62,4,128]{2,1,0:T(4,128)S(1)} %get-tuple-element.68), channel_id=1, source_target_pairs={{8,0},{16,8},{24,16},{32,24},{40,32},{48,40},{56,48},{0,56},{9,1},... | collective-permute-start | bytes 380936 | tf_op jit(solution)/shard_map/ppermute | solution.py:646
  28.0 4.8 %collective-permute-start.6 = (f32[6,16,128]{2,1,0:T(8,128)S(1)}, f32[6,16,128]{2,1,0:T(8,128)S(1)}, u32[]{:S(2)}, u32[]{:S(2)}) collective-permute-start(f32[6,16,128]{2,1,0:T(8,128)S(1)} %get-tuple-element.77), channel_id=1, source_target_pairs={{1,0},{2,1},{3,2},{4,3},{5,4},{6,5},{7,6},{0,7},{9,8},{10,9},{11,1... | collective-permute-start | bytes 147464 | tf_op jit(solution)/shard_map/ppermute | solution.py:646
  35.3 5.4 %collective-permute-start.8 = (f32[6,16,128]{2,1,0:T(8,128)S(1)}, f32[6,16,128]{2,1,0:T(8,128)S(1)}, u32[]{:S(2)}, u32[]{:S(2)}) collective-permute-start(f32[6,16,128]{2,1,0:T(8,128)S(1)} %get-tuple-element.81), channel_id=1, source_target_pairs={{192,0},{0,64},{64,128},{128,192},{193,1},{1,65},{65,129},{129,193... | collective-permute-start | bytes 147464 | tf_op jit(solution)/shard_map/ppermute | solution.py:646
  41.1 5.4 %collective-permute-start.10 = (f32[26,8,128]{2,1,0:T(8,128)S(1)}, f32[26,8,128]{2,1,0:T(8,128)S(1)}, u32[]{:S(2)}, u32[]{:S(2)}) collective-permute-start(f32[26,8,128]{2,1,0:T(8,128)S(1)} %get-tuple-element.83), channel_id=1, source_target_pairs={{56,0},{0,8},{8,16},{16,24},{24,32},{32,40},{40,48},{48,56},{57,1}... | collective-permute-start | bytes 319496 | tf_op jit(solution)/shard_map/ppermute | solution.py:646
  41.1 5.3 %collective-permute-start.11 = (f32[26,8,128]{2,1,0:T(8,128)S(1)}, f32[26,8,128]{2,1,0:T(8,128)S(1)}, u32[]{:S(2)}, u32[]{:S(2)}) collective-permute-start(f32[26,8,128]{2,1,0:T(8,128)S(1)} %get-tuple-element.84), channel_id=1, source_target_pairs={{8,0},{16,8},{24,16},{32,24},{40,32},{48,40},{56,48},{0,56},{9,1},... | collective-permute-start | bytes 319496 | tf_op jit(solution)/shard_map/ppermute | solution.py:646
  47.4 8.1 %collective-permute-start.17 = (f32[3,8,128]{2,1,0:T(8,128)S(1)}, f32[3,8,128]{2,1,0:T(8,128)S(1)}, u32[]{:S(2)}, u32[]{:S(2)}) collective-permute-start(f32[3,8,128]{2,1,0:T(8,128)S(1)} %get-tuple-element.90.own), channel_id=1, source_target_pairs={{7,0},{0,1},{1,2},{2,3},{3,4},{4,5},{5,6},{6,7},{15,8},{8,9},{9,10... | collective-permute-start | bytes 36872 | tf_op jit(solution)/shard_map/ppermute | solution.py:646
  47.4 11.2 %collective-permute-start.16 = (f32[3,8,128]{2,1,0:T(8,128)S(1)}, f32[3,8,128]{2,1,0:T(8,128)S(1)}, u32[]{:S(2)}, u32[]{:S(2)}) collective-permute-start(f32[3,8,128]{2,1,0:T(8,128)S(1)} %get-tuple-element.90.own), channel_id=1, source_target_pairs={{6,0},{7,1},{0,2},{1,3},{2,4},{3,5},{4,6},{5,7},{14,8},{15,9},{8,1... | collective-permute-start | bytes 36872 | tf_op jit(solution)/shard_map/ppermute | solution.py:646
  49.6 9.0 %collective-permute-start.15 = (f32[3,8,128]{2,1,0:T(8,128)S(1)}, f32[3,8,128]{2,1,0:T(8,128)S(1)}, u32[]{:S(2)}, u32[]{:S(2)}) collective-permute-start(f32[3,8,128]{2,1,0:T(8,128)S(1)} %get-tuple-element.90.own), channel_id=1, source_target_pairs={{5,0},{6,1},{7,2},{0,3},{1,4},{2,5},{3,6},{4,7},{13,8},{14,9},{15,... | collective-permute-start | bytes 36872 | tf_op jit(solution)/shard_map/ppermute | solution.py:646
  51.3 7.4 %collective-permute-start.14 = (f32[3,8,128]{2,1,0:T(8,128)S(1)}, f32[3,8,128]{2,1,0:T(8,128)S(1)}, u32[]{:S(2)}, u32[]{:S(2)}) collective-permute-start(f32[3,8,128]{2,1,0:T(8,128)S(1)} %get-tuple-element.90.own), channel_id=1, source_target_pairs={{3,0},{4,1},{5,2},{6,3},{7,4},{0,5},{1,6},{2,7},{11,8},{12,9},{13,... | collective-permute-start | bytes 36872 | tf_op jit(solution)/shard_map/ppermute | solution.py:646
  54.7 4.6 %collective-permute-start.13 = (f32[3,8,128]{2,1,0:T(8,128)S(1)}, f32[3,8,128]{2,1,0:T(8,128)S(1)}, u32[]{:S(2)}, u32[]{:S(2)}) collective-permute-start(f32[3,8,128]{2,1,0:T(8,128)S(1)} %get-tuple-element.90.own), channel_id=1, source_target_pairs={{2,0},{3,1},{4,2},{5,3},{6,4},{7,5},{0,6},{1,7},{10,8},{11,9},{12,... | collective-permute-start | bytes 36872 | tf_op jit(solution)/shard_map/ppermute | solution.py:646
  55.5 4.6 %collective-permute-start.12 = (f32[3,8,128]{2,1,0:T(8,128)S(1)}, f32[3,8,128]{2,1,0:T(8,128)S(1)}, u32[]{:S(2)}, u32[]{:S(2)}) collective-permute-start(f32[3,8,128]{2,1,0:T(8,128)S(1)} %get-tuple-element.90.own), channel_id=1, source_target_pairs={{1,0},{2,1},{3,2},{4,3},{5,4},{6,5},{7,6},{0,7},{9,8},{10,9},{11,1... | collective-permute-start | bytes 36872 | tf_op jit(solution)/shard_map/ppermute | solution.py:646
  60.2 8.7 %collective-permute-start.20 = (f32[16,8,128]{2,1,0:T(8,128)S(1)}, f32[16,8,128]{2,1,0:T(8,128)S(1)}, u32[]{:S(2)}, u32[]{:S(2)}) collective-permute-start(f32[16,8,128]{2,1,0:T(8,128)S(1)} %get-tuple-element.91.own), channel_id=1, source_target_pairs={{192,0},{0,64},{64,128},{128,192},{193,1},{1,65},{65,129},{129,193... | collective-permute-start | bytes 196616 | tf_op jit(solution)/shard_map/ppermute | solution.py:646
  61.5 7.4 %collective-permute-start.18 = (f32[16,8,128]{2,1,0:T(8,128)S(1)}, f32[16,8,128]{2,1,0:T(8,128)S(1)}, u32[]{:S(2)}, u32[]{:S(2)}) collective-permute-start(f32[16,8,128]{2,1,0:T(8,128)S(1)} %get-tuple-element.91.own), channel_id=1, source_target_pairs={{64,0},{128,64},{192,128},{0,192},{65,1},{129,65},{193,129},{1,193... | collective-permute-start | bytes 196616 | tf_op jit(solution)/shard_map/ppermute | solution.py:646
  63.5 5.4 %collective-permute-start.19 = (f32[8,8,128]{2,1,0:T(8,128)S(1)}, f32[8,8,128]{2,1,0:T(8,128)S(1)}, u32[]{:S(2)}, u32[]{:S(2)}) collective-permute-start(f32[8,8,128]{2,1,0:T(8,128)S(1)} %slice.6), channel_id=1, source_target_pairs={{128,0},{192,64},{0,128},{64,192},{129,1},{193,65},{1,129},{65,193... | collective-permute-start | bytes 98312 | tf_op jit(solution)/shard_map/ppermute | solution.py:646
  68.9 6.2 %collective-permute-start.22 = (f32[50,8,128]{2,1,0:T(8,128)S(1)}, f32[50,8,128]{2,1,0:T(8,128)S(1)}, u32[]{:S(2)}, u32[]{:S(2)}) collective-permute-start(f32[50,8,128]{2,1,0:T(8,128)S(1)} %get-tuple-element.92.r2x), channel_id=1, source_target_pairs={{8,0},{16,8},{24,16},{32,24},{40,32},{48,40},{56,48},{0,56},{9,1},... | collective-permute-start | bytes 614408 | tf_op jit(solution)/shard_map/ppermute | solution.py:646
  69.0 6.8 %collective-permute-start.21 = (f32[50,8,128]{2,1,0:T(8,128)S(1)}, f32[50,8,128]{2,1,0:T(8,128)S(1)}, u32[]{:S(2)}, u32[]{:S(2)}) collective-permute-start(f32[50,8,128]{2,1,0:T(8,128)S(1)} %get-tuple-element.92.r2x), channel_id=1, source_target_pairs={{56,0},{0,8},{8,16},{16,24},{24,32},{32,40},{40,48},{48,56},{57,1}... | collective-permute-start | bytes 614408 | tf_op jit(solution)/shard_map/ppermute | solution.py:646
  69.5 5.7 %collective-permute-start.23 = (f32[20,3,128]{2,1,0:T(4,128)S(1)}, f32[20,3,128]{2,1,0:T(4,128)S(1)}, u32[]{:S(2)}, u32[]{:S(2)}) collective-permute-start(f32[20,3,128]{2,1,0:T(4,128)S(1)} %get-tuple-element.93), channel_id=1, source_target_pairs={{48,0},{56,8},{0,16},{8,24},{16,32},{24,40},{32,48},{40,56},{49,1}... | collective-permute-start | bytes 92168 | tf_op jit(solution)/shard_map/ppermute | solution.py:646
  69.5 5.7 %collective-permute-start.24 = (f32[20,3,128]{2,1,0:T(4,128)S(1)}, f32[20,3,128]{2,1,0:T(4,128)S(1)}, u32[]{:S(2)}, u32[]{:S(2)}) collective-permute-start(f32[20,3,128]{2,1,0:T(4,128)S(1)} %get-tuple-element.94), channel_id=1, source_target_pairs={{16,0},{24,8},{32,16},{40,24},{48,32},{56,40},{0,48},{8,56},{17,1}... | collective-permute-start | bytes 92168 | tf_op jit(solution)/shard_map/ppermute | solution.py:646
  83.1 4.8 %collective-permute-start.28 = (f32[8,128]{1,0:T(8,128)S(1)}, f32[8,128]{1,0:T(8,128)S(1)}, u32[]{:S(2)}, u32[]{:S(2)}) collective-permute-start(f32[8,128]{1,0:T(8,128)S(1)} %add.33), channel_id=1, source_target_pairs={{192,0},{128,64},{64,128},{0,192},{193,1},{129,65},{65,129},{1,193... | collective-permute-start | bytes 12296 | tf_op jit(solution)/shard_map/ppermute | solution.py:650
  84.8 5.1 %collective-permute-start.27 = (f32[8,128]{1,0:T(8,128)S(1)}, f32[8,128]{1,0:T(8,128)S(1)}, u32[]{:S(2)}, u32[]{:S(2)}) collective-permute-start(f32[8,128]{1,0:T(8,128)S(1)} %add.33), channel_id=1, source_target_pairs={{128,0},{192,64},{0,128},{64,192},{129,1},{193,65},{1,129},{65,193... | collective-permute-start | bytes 12296 | tf_op jit(solution)/shard_map/ppermute | solution.py:650
  85.3 4.6 %collective-permute-start.26 = (f32[8,128]{1,0:T(8,128)S(1)}, f32[8,128]{1,0:T(8,128)S(1)}, u32[]{:S(2)}, u32[]{:S(2)}) collective-permute-start(f32[8,128]{1,0:T(8,128)S(1)} %add.33), channel_id=1, source_target_pairs={{64,0},{0,64},{192,128},{128,192},{65,1},{1,65},{193,129},{129,193... | collective-permute-start | bytes 12296 | tf_op jit(solution)/shard_map/ppermute | solution.py:650
  89.9 4.9 %collective-permute-start.31 = (f32[8,128]{1,0:T(8,128)S(1)}, f32[8,128]{1,0:T(8,128)S(1)}, u32[]{:S(2)}, u32[]{:S(2)}) collective-permute-start(f32[8,128]{1,0:T(8,128)S(1)} %add_add_fusion.2), channel_id=1, source_target_pairs={{48,0},{56,8},{32,16},{40,24},{16,32},{24,40},{0,48},{8,56},{49,1}... | collective-permute-start | bytes 12296 | tf_op jit(solution)/shard_map/ppermute | solution.py:650
  92.1 5.1 %collective-permute-start.30 = (f32[8,128]{1,0:T(8,128)S(1)}, f32[8,128]{1,0:T(8,128)S(1)}, u32[]{:S(2)}, u32[]{:S(2)}) collective-permute-start(f32[8,128]{1,0:T(8,128)S(1)} %add_add_fusion.2), channel_id=1, source_target_pairs={{32,0},{40,8},{48,16},{56,24},{0,32},{8,40},{16,48},{24,56},{33,1}... | collective-permute-start | bytes 12296 | tf_op jit(solution)/shard_map/ppermute | solution.py:650
  92.2 5.1 %collective-permute-start.29 = (f32[8,128]{1,0:T(8,128)S(1)}, f32[8,128]{1,0:T(8,128)S(1)}, u32[]{:S(2)}, u32[]{:S(2)}) collective-permute-start(f32[8,128]{1,0:T(8,128)S(1)} %add_add_fusion.2), channel_id=1, source_target_pairs={{16,0},{24,8},{0,16},{8,24},{48,32},{56,40},{32,48},{40,56},{17,1}... | collective-permute-start | bytes 12296 | tf_op jit(solution)/shard_map/ppermute | solution.py:650
  97.3 4.7 %collective-permute-start.34 = (f32[8,128]{1,0:T(8,128)S(1)}, f32[8,128]{1,0:T(8,128)S(1)}, u32[]{:S(2)}, u32[]{:S(2)}) collective-permute-start(f32[8,128]{1,0:T(8,128)S(1)} %add_add_fusion.1), channel_id=1, source_target_pairs={{3,0},{2,1},{1,2},{0,3},{7,4},{6,5},{5,6},{4,7},{11,8},{10,9},{9,1... | collective-permute-start | bytes 12296 | tf_op jit(solution)/shard_map/ppermute | solution.py:650
  98.8 4.8 %collective-permute-start.33 = (f32[8,128]{1,0:T(8,128)S(1)}, f32[8,128]{1,0:T(8,128)S(1)}, u32[]{:S(2)}, u32[]{:S(2)}) collective-permute-start(f32[8,128]{1,0:T(8,128)S(1)} %add_add_fusion.1), channel_id=1, source_target_pairs={{2,0},{3,1},{0,2},{1,3},{6,4},{7,5},{4,6},{5,7},{10,8},{11,9},{8,1... | collective-permute-start | bytes 12296 | tf_op jit(solution)/shard_map/ppermute | solution.py:650
  105.6 6.6 %collective-permute-start.35 = (f32[8,128]{1,0:T(8,128)S(1)}, f32[8,128]{1,0:T(8,128)S(1)}, u32[]{:S(2)}, u32[]{:S(2)}) collective-permute-start(f32[8,128]{1,0:T(8,128)S(1)} %add_add_fusion), channel_id=1, source_target_pairs={{7,0},{6,1},{5,2},{4,3},{3,4},{2,5},{1,6},{0,7},{15,8},{14,9},{13,... | collective-permute-start | bytes 12296 | tf_op jit(solution)/shard_map/ppermute | solution.py:650
  (5 other events, 49.5 us)
